TPU v7x, 512 devices: a whole 4x8x8 slice. The times are simulated.
512 devices in a mesh: grp: 16 (over x, y_hi), ctx: 32 (over y_lo, z, core).
Axes of the slice: x: 4, y: 8 (y_hi: 4, y_lo: 2; y = y_hi * 2 + y_lo), z: 8, core: 2. Of those that a mesh axis runs over, the one named last changes fastest.
Arguments:
- query_raw: bfloat16 [131072, 256], P(('grp', 'ctx')), may hold values from -6 to 6
- key_raw: bfloat16 [131072, 256], P(('grp', 'ctx')), may hold values from -6 to 6
- values: bfloat16 [131072, 256], P(('grp', 'ctx')), may hold values from -6 to 6
- band_reach: int32 [1024], P(('grp', 'ctx')), may hold values from 1 to 2, as said below
- partners: int32 [1024, 4], P(('grp', 'ctx')), may hold values from 0 to 1023, as said below
- gain_query: float32 [2, 128], replicated, may hold values from 0.5 to 2
- gain_key: float32 [2, 128], replicated, may hold values from 0.5 to 2
- cotangent: bfloat16 [131072, 256], P(('grp', 'ctx')), may hold values from -6 to 6
Outputs:
- output: bfloat16 [131072, 256], P(('grp', 'ctx'))
- grad_query: bfloat16 [131072, 256], P(('grp', 'ctx'))
- grad_key: bfloat16 [131072, 256], P(('grp', 'ctx'))
- grad_value: bfloat16 [131072, 256], P(('grp', 'ctx'))
Inputs may be any that keep to these rules, and one draw needn't show every extreme that they name: `band_reach`: some query block has reach 2. partners[b, l] is a block of the device whose index is (b // 2) xor (512 // 2**(l+1)).
All inputs are finite; a program needn't handle non-finite values.
Results may differ from a plain program's by a relative error of at most 0.0099.
Values may be sent and summed in bfloat16 or wider, within the bound.
No kernel may reach another device: no remote copies, remote signals or barrier semaphores. Data moves between devices by JAX's collectives and lax.ppermute only.
A program may use at most 64 MiB of HBM per device.

v0:
```python
import jax
import jax.numpy as jnp
from jax import lax
from jax.sharding import PartitionSpec as P

HEADS = 2
BLOCK = 128
BAND = 2
LEVELS = 4


epsilon = 1e-05


def with_halo(x, sides, width):
    edges = {}
    for axis, dim in sides:
        devices, length = (lax.axis_size(axis), x.shape[dim])
        up = [(i, (i + 1) % devices) for i in range(devices - 1)]
        last = lax.slice_in_dim(x, length - width, length, axis=dim)
        leading = lax.slice_in_dim(x, 0, width, axis=dim)
        edges[dim] = (
            lax.ppermute(last, axis, up),
            lax.ppermute(leading, axis, [(b, a) for a, b in up]),
        )
    done = []
    for _, dim in sides:
        low, high = edges[dim]
        around = [(width, width) if d in done else (0, 0) for d in range(x.ndim)]
        x = jnp.concatenate([jnp.pad(low, around), x, jnp.pad(high, around)], axis=dim)
        done.append(dim)
    return x


def partner(value, axis, apart):
    mask = 2**apart
    pairs = [(source, source ^ mask) for source in range(lax.axis_size(axis))]
    return lax.ppermute(value, axis, pairs)


def from_behind(x, axis, by):
    devices = lax.axis_size(axis)
    pairs = [(i, i + by) for i in range(devices) if 0 <= i + by < devices]
    return lax.ppermute(x, axis, pairs)


def layer_norm(inputs, gain_row):
    average = jnp.mean(inputs, axis=-1, keepdims=True)
    centred = inputs - average
    inverse = lax.rsqrt(jnp.mean(centred * centred, axis=-1, keepdims=True) + epsilon)
    normed = centred * inverse
    return (normed, inverse, normed * gain_row)


def norm_back(upstream, normed, inverse, gain_row):
    scaled = upstream * gain_row
    first = jnp.mean(scaled, axis=-1, keepdims=True)
    second = jnp.mean(scaled * normed, axis=-1, keepdims=True)
    return (scaled - first - normed * second) * inverse


def body(query_raw, key_raw, values, band_reach, partners, gain_query, gain_key, cotangent):
    row_count, row_width = query_raw.shape
    head_dim = row_width // HEADS
    blocks = row_count // BLOCK
    block_extent = 2 * BAND + 1
    score_scale = head_dim ** (-0.5)
    shard_count = lax.axis_size(("grp", "ctx"))
    device = lax.axis_index(("grp", "ctx"))
    top_bit = shard_count.bit_length() - 1
    q_normed, q_inverse, q_scaled = layer_norm(
        query_raw.astype(jnp.float32).reshape(row_count, HEADS, head_dim), gain_query
    )
    k_normed, k_inverse, k_scaled = layer_norm(
        key_raw.astype(jnp.float32).reshape(row_count, HEADS, head_dim), gain_key
    )
    query_low = q_scaled.astype(jnp.bfloat16).reshape(row_count, row_width)
    key_low = k_scaled.astype(jnp.bfloat16).reshape(row_count, row_width)
    paired = jnp.stack((key_low, values))
    padded = with_halo(paired, ((("grp", "ctx"), 1),), BAND * BLOCK)
    padded = padded.reshape(2, blocks + 2 * BAND, BLOCK, row_width)
    band_sets = jnp.stack(
        [padded[:, offset : offset + blocks] for offset in range(block_extent)], axis=2
    )
    level_order = list(range(LEVELS))
    fetched = {}
    local_picks = {}
    for level_index in level_order:
        bit_number = top_bit - 1 - level_index
        partner_device = jnp.bitwise_xor(device, 1 << bit_number)
        received = partner(paired, ("grp", "ctx"), bit_number).reshape(2, blocks, BLOCK, row_width)
        local_picks[level_index] = partners[:, level_index] - partner_device * blocks
        fetched[level_index] = jnp.take(received, local_picks[level_index], axis=1)
    partner_sets = jnp.stack([fetched[level_index] for level_index in range(LEVELS)], axis=2)
    key_sets = jnp.concatenate((band_sets, partner_sets), axis=2)
    pick_table = jnp.stack([local_picks[level_index] for level_index in range(LEVELS)], axis=1)
    offsets = jnp.arange(block_extent, dtype=jnp.int32) - BAND
    block_ids = device * blocks + jnp.arange(blocks, dtype=jnp.int32)
    target = block_ids[:, None] + offsets[None, :]
    band_ok = (
        (jnp.abs(offsets)[None, :] <= band_reach[:, None])
        & (target >= 0)
        & (target < shard_count * blocks)
    )
    usable = jnp.concatenate((band_ok, jnp.ones((blocks, LEVELS), dtype=jnp.bool_)), axis=1)
    allowed = usable[:, None, :, None]
    slots = jnp.arange(blocks, dtype=jnp.int32)
    pick_match = (pick_table[:, :, None] == slots[None, None, :]).astype(jnp.float32)
    outputs = []
    grad_qnorms = []
    log_totals = []
    row_deltas = []
    band_parts = []
    partner_terms = []
    for head_index in range(HEADS):
        head_cols = slice(head_index * head_dim, (head_index + 1) * head_dim)
        head_queries = query_low[:, head_cols].reshape(blocks, BLOCK, head_dim)
        head_gradient = cotangent[:, head_cols].reshape(blocks, BLOCK, head_dim)
        head_keys = key_sets[0, ..., head_cols]
        head_values = key_sets[1, ..., head_cols]
        scores = (
            jnp.einsum(
                "gor,gxar->goxa", head_queries, head_keys, preferred_element_type=jnp.float32
            )
            * score_scale
        )
        row_total = jnp.sum(jnp.where(allowed, jnp.exp(scores), 0.0), axis=(2, 3))
        log_total = jnp.log(row_total)
        probability = jnp.where(allowed, jnp.exp(scores - log_total[:, :, None, None]), 0.0)
        attention_weight = probability.astype(jnp.bfloat16)
        output = jnp.einsum(
            "ieuz,iuzg->ieg", attention_weight, head_values, preferred_element_type=jnp.float32
        ).astype(jnp.bfloat16)
        row_delta = jnp.sum(head_gradient.astype(jnp.float32) * output.astype(jnp.float32), axis=-1)
        grad_prob = jnp.einsum(
            "gor,gxar->goxa", head_gradient, head_values, preferred_element_type=jnp.float32
        )
        score_gradient = (probability * (grad_prob - row_delta[:, :, None, None])).astype(
            jnp.bfloat16
        )
        grad_qnorm = (
            jnp.einsum(
                "ieuz,iuzg->ieg", score_gradient, head_keys, preferred_element_type=jnp.float32
            )
            * score_scale
        )
        key_terms = (
            jnp.einsum(
                "snwh,snc->swhc",
                score_gradient[:, :, :block_extent],
                head_queries,
                preferred_element_type=jnp.float32,
            )
            * score_scale
        )
        value_terms = jnp.einsum(
            "snwh,snc->swhc",
            attention_weight[:, :, :block_extent],
            head_gradient,
            preferred_element_type=jnp.float32,
        )
        band_buffer = jnp.zeros((2, blocks + 2 * BAND, BLOCK, head_dim), jnp.float32)
        for offset in range(block_extent):
            band_buffer = band_buffer.at[:, offset : offset + blocks].add(
                jnp.stack((key_terms[:, offset], value_terms[:, offset]))
            )
        far_keys = (
            jnp.einsum(
                "snwh,snc->swhc",
                score_gradient[:, :, block_extent:],
                head_queries,
                preferred_element_type=jnp.float32,
            )
            * score_scale
        )
        far_values = jnp.einsum(
            "snwh,snc->swhc",
            attention_weight[:, :, block_extent:],
            head_gradient,
            preferred_element_type=jnp.float32,
        )
        far_terms = jnp.stack((far_keys, far_values))
        partner_terms.append(jnp.einsum("ilb,gilkd->lgbkd", pick_match, far_terms))
        outputs.append(output)
        grad_qnorms.append(grad_qnorm)
        log_totals.append(log_total)
        row_deltas.append(row_delta)
        band_parts.append(band_buffer)
    band_all = jnp.concatenate(band_parts, axis=-1)
    local_grads = band_all[:, BAND : BAND + blocks]
    for shift_by in (1, -1):
        rim_part = band_all[:, BAND + blocks :] if shift_by == 1 else band_all[:, :BAND]
        arrived = from_behind(rim_part.astype(jnp.bfloat16), ("grp", "ctx"), shift_by).astype(
            rim_part.dtype
        )
        if shift_by == 1:
            local_grads = local_grads.at[:, :BAND].add(arrived)
        else:
            local_grads = local_grads.at[:, blocks - BAND :].add(arrived)
    partner_grads = jnp.concatenate(partner_terms, axis=-1)
    for level_index in level_order:
        bit_number = top_bit - 1 - level_index
        local_grads = local_grads + partner(
            partner_grads[level_index].astype(jnp.bfloat16), ("grp", "ctx"), bit_number
        ).astype(jnp.float32)
    output_all = jnp.concatenate(outputs, axis=-1).reshape(row_count, row_width)
    grad_qnorm_all = jnp.stack(grad_qnorms, axis=2).reshape(row_count, HEADS, head_dim)
    grad_query = (
        norm_back(grad_qnorm_all, q_normed, q_inverse, gain_query)
        .astype(jnp.bfloat16)
        .reshape(row_count, row_width)
    )
    grad_knorm = local_grads[0].reshape(row_count, HEADS, head_dim)
    grad_key = (
        norm_back(grad_knorm, k_normed, k_inverse, gain_key)
        .astype(jnp.bfloat16)
        .reshape(row_count, row_width)
    )
    grad_value = local_grads[1].astype(jnp.bfloat16).reshape(row_count, row_width)
    return (output_all, grad_query, grad_key, grad_value)


def solution(mesh):
    return jax.shard_map(
        body,
        mesh=mesh,
        in_specs=(
            P(("grp", "ctx"), None),
            P(("grp", "ctx"), None),
            P(("grp", "ctx"), None),
            P(("grp", "ctx")),
            P(("grp", "ctx"), None),
            P(),
            P(),
            P(("grp", "ctx"), None),
        ),
        out_specs=(
            P(("grp", "ctx"), None),
            P(("grp", "ctx"), None),
            P(("grp", "ctx"), None),
            P(("grp", "ctx"), None),
        ),
        check_vma=False,
    )
```

profile of v0, /device:TPU:2, one launch (start us, length us, event | category | flops | bytes accessed | tf_op | source)
XLA Modules:
  0.0 133.9 jit_solution(17286163957218596036)
XLA Ops:
  4.3 13.3 %collective-permute-start.1 = (bf16[2,256,256]{2,1,0:T(8,128)(2,1)}, bf16[2,256,256]{2,1,0:T(8,128)(2,1)}, u32[]{:S(2)}, u32[]{:S(2)}) collective-permute-start(bf16[2,256,256]{2,1,0:T(8,128)(2,1)} %pad_maximum_fusion.4), channel_id=1, source_target_pairs={{1,0},{2,1},{3,2},{4,3},{5,4},{6,5},{7,6},{8,7},{9,8},{10,9},{11,1... | collective-permute-start | bytes 786440 | tf_op jit(solution)/shard_map/ppermute | solution.py:24
  17.6 1.9 %collective-permute-start = (bf16[2,256,256]{2,1,0:T(8,128)(2,1)}, bf16[2,256,256]{2,1,0:T(8,128)(2,1)}, u32[]{:S(2)}, u32[]{:S(2)}) collective-permute-start(bf16[2,256,256]{2,1,0:T(8,128)(2,1)} %pad_maximum_fusion.4), channel_id=1, source_target_pairs={{0,1},{1,2},{2,3},{3,4},{4,5},{5,6},{6,7},{7,8},{8,9},{9,10},{10,1... | collective-permute-start | bytes 786440 | tf_op jit(solution)/shard_map/ppermute | solution.py:23
  19.5 4.3 %collective-permute-start.2 = (bf16[2,256,256]{2,1,0:T(8,128)(2,1)}, bf16[2,256,256]{2,1,0:T(8,128)(2,1)S(1)}, u32[]{:S(2)}, u32[]{:S(2)}) collective-permute-start(bf16[2,256,256]{2,1,0:T(8,128)(2,1)} %pad_maximum_fusion.4), channel_id=1, source_target_pairs={{0,256},{1,257},{2,258},{3,259},{4,260},{5,261},{6,262},{7,263},{8... | collective-permute-start | bytes 786440 | tf_op jit(solution)/shard_map/ppermute | solution.py:38
  23.9 3.0 %collective-permute-start.3 = (bf16[2,256,256]{2,1,0:T(8,128)(2,1)}, bf16[2,256,256]{2,1,0:T(8,128)(2,1)S(1)}, u32[]{:S(2)}, u32[]{:S(2)}) collective-permute-start(bf16[2,256,256]{2,1,0:T(8,128)(2,1)} %pad_maximum_fusion.4), channel_id=1, source_target_pairs={{0,128},{1,129},{2,130},{3,131},{4,132},{5,133},{6,134},{7,135},{8... | collective-permute-start | bytes 786440 | tf_op jit(solution)/shard_map/ppermute | solution.py:38
  26.9 4.7 %collective-permute-start.4 = (bf16[2,256,256]{2,1,0:T(8,128)(2,1)}, bf16[2,256,256]{2,1,0:T(8,128)(2,1)S(1)}, u32[]{:S(2)}, u32[]{:S(2)}) collective-permute-start(bf16[2,256,256]{2,1,0:T(8,128)(2,1)} %pad_maximum_fusion.4), channel_id=1, source_target_pairs={{0,64},{1,65},{2,66},{3,67},{4,68},{5,69},{6,70},{7,71},{8,72},{9,... | collective-permute-start | bytes 786440 | tf_op jit(solution)/shard_map/ppermute | solution.py:38
  39.6 3.8 %collective-permute-start.5 = (bf16[2,256,256]{2,1,0:T(8,128)(2,1)}, bf16[2,256,256]{2,1,0:T(8,128)(2,1)}, u32[]{:S(2)}, u32[]{:S(2)}) collective-permute-start(bf16[2,256,256]{2,1,0:T(8,128)(2,1)} %pad_maximum_fusion.4), channel_id=1, source_target_pairs={{0,32},{1,33},{2,34},{3,35},{4,36},{5,37},{6,38},{7,39},{8,40},{9,... | collective-permute-start | bytes 786440 | tf_op jit(solution)/shard_map/ppermute | solution.py:38
  50.0 1.9 %collective-permute-done.5 = bf16[2,256,256]{2,1,0:T(8,128)(2,1)} collective-permute-done((bf16[2,256,256]{2,1,0:T(8,128)(2,1)}, bf16[2,256,256]{2,1,0:T(8,128)(2,1)}, u32[]{:S(2)}, u32[]{:S(2)}) %collective-permute-start.5) | collective-permute-done | bytes 262176 | tf_op jit(solution)/shard_map/ppermute | solution.py:38
  51.9 1.5 %gather_fusion.3 = bf16[2,2,128,256]{3,2,1,0:T(8,128)(2,1)S(1)} fusion(bf16[2,2,128,256]{3,2,1,0:T(8,128)(2,1)} %bitcast.26, s32[1024]{0:T(1024)S(1)} %pad_clamp_fusion), kind=kCustom, calls=%fused_computation.3.clone | custom fusion | bytes 524296 | tf_op jit(solution)/shard_map/jit(_take)/gather | solution.py:93
  58.1 1.6 %select_reduce_fusion.1 = (f32[2,128]{1,0:T(2,128)S(1)}, f32[2,128]{1,0:T(2,128)S(1)}, f32[2,128,9,128]{1,3,2,0:T(8,128)S(1)}) fusion(pred[2,9]{1,0:T(4,128)(4,1)S(1)} %copy-done.56, f32[2,128,9,128]{1,3,2,0:T(8,128)S(1)} %convolution_multiply_fusion, bf16[2,128,128,1]{2,1,3,0:T(8,128)(2,1)S(1)} %bitcast.350, ...), kind=kOutput, calls=%fused_computation.30 | convolution fusion | flops 76971520 | bytes 3016722 | tf_op jit(solution)/shard_map/gor,gxar->goxa/dot_general | solution.py:122
  60.6 1.5 %multiply_reduce_fusion.7 = (f32[2,128]{1,0:T(2,128)S(1)}, bf16[2,128,128]{1,2,0:T(8,128)(2,1)S(1)}) fusion(bf16[2,128,128]{1,2,0:T(8,128)(2,1)S(1)} %copy-done.47, bf16[2,128,9,128]{1,3,2,0:T(8,128)(2,1)S(1)} %get-tuple-element.216, bf16[2,2,9,128,256]{4,3,2,1,0:T(8,128)(2,1)} %bitcast_dynamic-update-slice_fusion), kind=kOutput, calls=%fused_computation.158 | convolution fusion | flops 75661056 | bytes 1311744 | tf_op jit(solution)/shard_map/ieuz,iuzg->ieg/dot_general | solution.py:131
  63.5 2.1 %fusion.10 = f32[2,128,128]{2,1,0:T(8,128)} fusion(bf16[2,128,9,128]{1,3,2,0:T(8,128)(2,1)S(1)} %fusion.5, bf16[2,2,9,128,256]{4,3,2,1,0:T(8,128)(2,1)} %bitcast_dynamic-update-slice_fusion), kind=kOutput, calls=%fused_computation.34 | convolution fusion | flops 75530240 | bytes 1310720 | tf_op jit(solution)/shard_map/ieuz,iuzg->ieg/dot_general | solution.py:142
  65.9 1.5 %multiply_reduce_fusion.6 = (f32[2,128]{1,0:T(2,128)S(1)}, bf16[2,128,128]{1,2,0:T(8,128)(2,1)S(1)}) fusion(bf16[2,128,128]{1,2,0:T(8,128)(2,1)S(1)} %copy-done.46, bf16[2,128,9,128]{1,3,2,0:T(8,128)(2,1)S(1)} %get-tuple-element.217, bf16[2,2,9,128,256]{4,3,2,1,0:T(8,128)(2,1)} %bitcast_dynamic-update-slice_fusion), kind=kOutput, calls=%fused_computation.157 | convolution fusion | flops 75661056 | bytes 1311744 | tf_op jit(solution)/shard_map/ieuz,iuzg->ieg/dot_general | solution.py:131
  68.3 1.5 %fusion.6 = bf16[2,128,9,128]{1,3,2,0:T(8,128)(2,1)S(1)} fusion(bf16[2,128,128,1]{2,1,3,0:T(8,128)(2,1)S(1)} %bitcast.340, f32[2,128,9,128]{1,3,2,0:T(8,128)S(1)} %convolution_multiply_fusion, f32[2,128]{1,0:T(2,128)S(1)} %get-tuple-element.219, f32[2,128]{1,0:T(2,128)S(1)} %log.15, pred[2,9]{1,0:T(4,128)(4,1)S(1)} %copy-done.56, ...), kind=kOutput, calls=%fused_computation.18 | convolution fusion | flops 76972032 | bytes 2426898 | tf_op jit(solution)/shard_map/gor,gxar->goxa/dot_general | solution.py:135
  69.8 2.1 %fusion.9 = f32[2,128,128]{2,1,0:T(8,128)} fusion(bf16[2,128,9,128]{1,3,2,0:T(8,128)(2,1)S(1)} %fusion.6, bf16[2,2,9,128,256]{4,3,2,1,0:T(8,128)(2,1)} %bitcast_dynamic-update-slice_fusion), kind=kOutput, calls=%fused_computation.32 | convolution fusion | flops 75530240 | bytes 1310720 | tf_op jit(solution)/shard_map/ieuz,iuzg->ieg/dot_general | solution.py:142
  75.3 1.7 %copy.257 = bf16[2,128,256]{2,1,0:T(8,128)(2,1)} copy(bf16[2,128,256]{1,2,0:T(8,128)(2,1)} %pad_maximum_fusion.6) | data formatting | bytes 262144 | tf_op jit(solution)/shard_map/concatenate | solution.py:206
  77.0 2.5 %multiply_reduce_fusion.4 = (f32[256,2]{0,1:T(2,128)}, f32[256,2]{0,1:T(2,128)S(1)}, f32[2,32,8,128]{3,2,1,0:T(8,128)}) fusion(f32[256,1,128]{2,0,1:T(8,128)} %bitcast.356, f32[256,1,128]{2,0,1:T(8,128)} %bitcast.355, f32[2,128]{1,0:T(2,128)S(1)} %copy-done.49, f32[256,2]{0,1:T(2,128)S(1)} %add_rsqrt_fusion.1, f32[256,2]{0,1:T(2,128)S(1)} %broadcast_multiply_fusion.5, ...), kind=kLoop, calls=%fused_computation.131 | loop fusion | flops 523264 | bytes 664576 | tf_op jit(solution)/shard_map/reduce_sum | solution.py:57
  88.8 2.1 %collective-permute-start.11 = (bf16[2,2,128,256]{2,3,1,0:T(8,128)(2,1)S(1)}, bf16[2,2,128,256]{2,3,1,0:T(8,128)(2,1)S(1)}, u32[]{:S(2)}, u32[]{:S(2)}) collective-permute-start(bf16[2,2,128,256]{2,3,1,0:T(8,128)(2,1)S(1)} %get-tuple-element.180), channel_id=1, source_target_pairs={{0,32},{1,33},{2,34},{3,35},{4,36},{5,37},{6,38},{7,39},{8,40},{9,... | collective-permute-start | bytes 786440 | tf_op jit(solution)/shard_map/ppermute | solution.py:38
  90.9 4.4 %collective-permute-start.10 = (bf16[2,2,128,256]{2,3,1,0:T(8,128)(2,1)S(1)}, bf16[2,2,128,256]{2,3,1,0:T(8,128)(2,1)S(1)}, u32[]{:S(2)}, u32[]{:S(2)}) collective-permute-start(bf16[2,2,128,256]{2,3,1,0:T(8,128)(2,1)S(1)} %get-tuple-element.181), channel_id=1, source_target_pairs={{0,64},{1,65},{2,66},{3,67},{4,68},{5,69},{6,70},{7,71},{8,72},{9,... | collective-permute-start | bytes 786440 | tf_op jit(solution)/shard_map/ppermute | solution.py:38
  95.3 2.7 %collective-permute-start.9 = (bf16[2,2,128,256]{2,3,1,0:T(8,128)(2,1)S(1)}, bf16[2,2,128,256]{2,3,1,0:T(8,128)(2,1)S(1)}, u32[]{:S(2)}, u32[]{:S(2)}) collective-permute-start(bf16[2,2,128,256]{2,3,1,0:T(8,128)(2,1)S(1)} %get-tuple-element.182), channel_id=1, source_target_pairs={{0,128},{1,129},{2,130},{3,131},{4,132},{5,133},{6,134},{7,135},{8... | collective-permute-start | bytes 786440 | tf_op jit(solution)/shard_map/ppermute | solution.py:38
  98.0 3.1 %collective-permute-start.8 = (bf16[2,2,128,256]{2,3,1,0:T(8,128)(2,1)S(1)}, bf16[2,2,128,256]{2,3,1,0:T(8,128)(2,1)S(1)}, u32[]{:S(2)}, u32[]{:S(2)}) collective-permute-start(bf16[2,2,128,256]{2,3,1,0:T(8,128)(2,1)S(1)} %get-tuple-element.179), channel_id=1, source_target_pairs={{0,256},{1,257},{2,258},{3,259},{4,260},{5,261},{6,262},{7,263},{8... | collective-permute-start | bytes 786440 | tf_op jit(solution)/shard_map/ppermute | solution.py:38
  103.6 9.8 %collective-permute-start.7 = (bf16[2,2,128,256]{2,3,1,0:T(8,128)(2,1)S(1)}, bf16[2,2,128,256]{2,3,1,0:T(8,128)(2,1)S(1)}, u32[]{:S(2)}, u32[]{:S(2)}) collective-permute-start(bf16[2,2,128,256]{2,3,1,0:T(8,128)(2,1)S(1)} %get-tuple-element.184), channel_id=1, source_target_pairs={{1,0},{2,1},{3,2},{4,3},{5,4},{6,5},{7,6},{8,7},{9,8},{10,9},{11,1... | collective-permute-start | bytes 786440 | tf_op jit(solution)/shard_map/ppermute | solution.py:44
  113.4 2.1 %collective-permute-start.6 = (bf16[2,2,128,256]{2,3,1,0:T(8,128)(2,1)S(1)}, bf16[2,2,128,256]{2,3,1,0:T(8,128)(2,1)S(1)}, u32[]{:S(2)}, u32[]{:S(2)}) collective-permute-start(bf16[2,2,128,256]{2,3,1,0:T(8,128)(2,1)S(1)} %get-tuple-element.183), channel_id=1, source_target_pairs={{0,1},{1,2},{2,3},{3,4},{4,5},{5,6},{6,7},{7,8},{8,9},{9,10},{10,1... | collective-permute-start | bytes 786440 | tf_op jit(solution)/shard_map/ppermute | solution.py:44
  117.3 11.6 %collective-permute-done.6 = bf16[2,2,128,256]{2,3,1,0:T(8,128)(2,1)S(1)} collective-permute-done((bf16[2,2,128,256]{2,3,1,0:T(8,128)(2,1)S(1)}, bf16[2,2,128,256]{2,3,1,0:T(8,128)(2,1)S(1)}, u32[]{:S(2)}, u32[]{:S(2)}) %collective-permute-start.6) | collective-permute-done | bytes 262176 | tf_op jit(solution)/shard_map/ppermute | solution.py:44
  130.0 1.6 %multiply_reduce_fusion.5 = (f32[256,2]{1,0:T(8,128)S(1)}, f32[256,2]{1,0:T(8,128)S(1)}) fusion(f32[256,2,128]{2,1,0:T(2,128)S(1)} %reshape_squeeze.6, f32[2,128]{1,0:T(2,128)S(1)} %copy-done.50, f32[256,2]{1,0:T(8,128)S(1)} %copy-done.8, f32[256,2,128]{2,1,0:T(2,128)S(1)} %reshape.599, f32[256,2]{1,0:T(8,128)S(1)} %copy-done.6), kind=kLoop, calls=%fused_computation.132 | loop fusion | flops 392192 | bytes 533504 | tf_op jit(solution)/shard_map/reduce_sum | solution.py:57
  (238 shorter events, 45.8 us)
Async XLA Ops:
  2.1 29.6 %copy-start = (bf16[256,256]{1,0:T(8,128)(2,1)S(1)}, bf16[256,256]{1,0:T(8,128)(2,1)}, u32[]{:S(2)}) copy-start(bf16[256,256]{1,0:T(8,128)(2,1)} %param.38) | copy-start | bytes 393220
  2.1 29.7 %copy-start.5 = (f32[256,2]{1,0:T(8,128)}, f32[256,2]{1,0:T(8,128)S(1)}, u32[]{:S(2)}) copy-start(f32[256,2]{1,0:T(8,128)S(1)} %broadcast_multiply_fusion.2) | copy-start | bytes 6148
  2.8 29.7 %copy-start.7 = (f32[256,2]{1,0:T(8,128)}, f32[256,2]{1,0:T(8,128)S(1)}, u32[]{:S(2)}) copy-start(f32[256,2]{1,0:T(8,128)S(1)} %add_rsqrt_fusion) | copy-start | bytes 6148
  2.8 29.9 %copy-start.48 = (s32[2,4]{1,0:T(2,128)S(1)}, s32[2,4]{1,0:T(2,128)}, u32[]{:S(2)}) copy-start(s32[2,4]{1,0:T(2,128)} %param.42) | copy-start | bytes 100
  3.2 32.0 %copy-start.45 = (bf16[256,256]{1,0:T(8,128)(2,1)S(1)}, bf16[256,256]{1,0:T(8,128)(2,1)}, u32[]{:S(2)}) copy-start(bf16[256,256]{1,0:T(8,128)(2,1)} %param.45) | copy-start | bytes 393220
  3.6 32.5 %copy-start.49 = (f32[2,128]{1,0:T(2,128)S(1)}, f32[2,128]{1,0:T(2,128)}, u32[]{:S(2)}) copy-start(f32[2,128]{1,0:T(2,128)} %param.43) | copy-start | bytes 3076
  4.3 35.3 %collective-permute-start.1 = (bf16[2,256,256]{2,1,0:T(8,128)(2,1)}, bf16[2,256,256]{2,1,0:T(8,128)(2,1)}, u32[]{:S(2)}, u32[]{:S(2)}) collective-permute-start(bf16[2,256,256]{2,1,0:T(8,128)(2,1)} %pad_maximum_fusion.4), channel_id=1, source_target_pairs={{1,0},{2,1},{3,2},{4,3},{5,4},{6,5},{7,6},{8,7},{9,8},{10,9},{11,1... | collective-permute-start | bytes 786440 | tf_op jit(solution)/shard_map/ppermute | solution.py:24
  17.6 25.8 %collective-permute-start = (bf16[2,256,256]{2,1,0:T(8,128)(2,1)}, bf16[2,256,256]{2,1,0:T(8,128)(2,1)}, u32[]{:S(2)}, u32[]{:S(2)}) collective-permute-start(bf16[2,256,256]{2,1,0:T(8,128)(2,1)} %pad_maximum_fusion.4), channel_id=1, source_target_pairs={{0,1},{1,2},{2,3},{3,4},{4,5},{5,6},{6,7},{7,8},{8,9},{9,10},{10,1... | collective-permute-start | bytes 786440 | tf_op jit(solution)/shard_map/ppermute | solution.py:23
  19.5 28.0 %collective-permute-start.2 = (bf16[2,256,256]{2,1,0:T(8,128)(2,1)}, bf16[2,256,256]{2,1,0:T(8,128)(2,1)S(1)}, u32[]{:S(2)}, u32[]{:S(2)}) collective-permute-start(bf16[2,256,256]{2,1,0:T(8,128)(2,1)} %pad_maximum_fusion.4), channel_id=1, source_target_pairs={{0,256},{1,257},{2,258},{3,259},{4,260},{5,261},{6,262},{7,263},{8... | collective-permute-start | bytes 786440 | tf_op jit(solution)/shard_map/ppermute | solution.py:38
  23.9 24.2 %collective-permute-start.3 = (bf16[2,256,256]{2,1,0:T(8,128)(2,1)}, bf16[2,256,256]{2,1,0:T(8,128)(2,1)S(1)}, u32[]{:S(2)}, u32[]{:S(2)}) collective-permute-start(bf16[2,256,256]{2,1,0:T(8,128)(2,1)} %pad_maximum_fusion.4), channel_id=1, source_target_pairs={{0,128},{1,129},{2,130},{3,131},{4,132},{5,133},{6,134},{7,135},{8... | collective-permute-start | bytes 786440 | tf_op jit(solution)/shard_map/ppermute | solution.py:38
  26.9 21.8 %collective-permute-start.4 = (bf16[2,256,256]{2,1,0:T(8,128)(2,1)}, bf16[2,256,256]{2,1,0:T(8,128)(2,1)S(1)}, u32[]{:S(2)}, u32[]{:S(2)}) collective-permute-start(bf16[2,256,256]{2,1,0:T(8,128)(2,1)} %pad_maximum_fusion.4), channel_id=1, source_target_pairs={{0,64},{1,65},{2,66},{3,67},{4,68},{5,69},{6,70},{7,71},{8,72},{9,... | collective-permute-start | bytes 786440 | tf_op jit(solution)/shard_map/ppermute | solution.py:38
  35.2 26.9 %copy-start.15 = (bf16[256,128]{1,0:T(8,128)(2,1)}, bf16[256,128]{1,0:T(8,128)(2,1)S(1)}, u32[]{:S(2)}) copy-start(bf16[256,128]{1,0:T(8,128)(2,1)S(1)} %get-tuple-element.206) | copy-start | bytes 196612
  39.6 17.1 %copy-start.11 = (bf16[256,128]{1,0:T(8,128)(2,1)}, bf16[256,128]{1,0:T(8,128)(2,1)S(1)}, u32[]{:S(2)}) copy-start(bf16[256,128]{1,0:T(8,128)(2,1)S(1)} %get-tuple-element.209) | copy-start | bytes 196612
  39.6 12.3 %collective-permute-start.5 = (bf16[2,256,256]{2,1,0:T(8,128)(2,1)}, bf16[2,256,256]{2,1,0:T(8,128)(2,1)}, u32[]{:S(2)}, u32[]{:S(2)}) collective-permute-start(bf16[2,256,256]{2,1,0:T(8,128)(2,1)} %pad_maximum_fusion.4), channel_id=1, source_target_pairs={{0,32},{1,33},{2,34},{3,35},{4,36},{5,37},{6,38},{7,39},{8,40},{9,... | collective-permute-start | bytes 786440 | tf_op jit(solution)/shard_map/ppermute | solution.py:38
  88.8 12.7 %copy-start.31 = (f32[1,2,128,128]{2,3,1,0:T(8,128)S(1)}, f32[1,2,128,128]{2,3,1,0:T(8,128)}, u32[]{:S(2)}) copy-start(f32[1,2,128,128]{2,3,1,0:T(8,128)} %get-tuple-element.202) | copy-start | bytes 393220
  88.8 24.6 %collective-permute-start.11 = (bf16[2,2,128,256]{2,3,1,0:T(8,128)(2,1)S(1)}, bf16[2,2,128,256]{2,3,1,0:T(8,128)(2,1)S(1)}, u32[]{:S(2)}, u32[]{:S(2)}) collective-permute-start(bf16[2,2,128,256]{2,3,1,0:T(8,128)(2,1)S(1)} %get-tuple-element.180), channel_id=1, source_target_pairs={{0,32},{1,33},{2,34},{3,35},{4,36},{5,37},{6,38},{7,39},{8,40},{9,... | collective-permute-start | bytes 786440 | tf_op jit(solution)/shard_map/ppermute | solution.py:38
  90.9 26.2 %collective-permute-start.10 = (bf16[2,2,128,256]{2,3,1,0:T(8,128)(2,1)S(1)}, bf16[2,2,128,256]{2,3,1,0:T(8,128)(2,1)S(1)}, u32[]{:S(2)}, u32[]{:S(2)}) collective-permute-start(bf16[2,2,128,256]{2,3,1,0:T(8,128)(2,1)S(1)} %get-tuple-element.181), channel_id=1, source_target_pairs={{0,64},{1,65},{2,66},{3,67},{4,68},{5,69},{6,70},{7,71},{8,72},{9,... | collective-permute-start | bytes 786440 | tf_op jit(solution)/shard_map/ppermute | solution.py:38
  95.3 21.7 %collective-permute-start.9 = (bf16[2,2,128,256]{2,3,1,0:T(8,128)(2,1)S(1)}, bf16[2,2,128,256]{2,3,1,0:T(8,128)(2,1)S(1)}, u32[]{:S(2)}, u32[]{:S(2)}) collective-permute-start(bf16[2,2,128,256]{2,3,1,0:T(8,128)(2,1)S(1)} %get-tuple-element.182), channel_id=1, source_target_pairs={{0,128},{1,129},{2,130},{3,131},{4,132},{5,133},{6,134},{7,135},{8... | collective-permute-start | bytes 786440 | tf_op jit(solution)/shard_map/ppermute | solution.py:38
  98.0 19.0 %collective-permute-start.8 = (bf16[2,2,128,256]{2,3,1,0:T(8,128)(2,1)S(1)}, bf16[2,2,128,256]{2,3,1,0:T(8,128)(2,1)S(1)}, u32[]{:S(2)}, u32[]{:S(2)}) collective-permute-start(bf16[2,2,128,256]{2,3,1,0:T(8,128)(2,1)S(1)} %get-tuple-element.179), channel_id=1, source_target_pairs={{0,256},{1,257},{2,258},{3,259},{4,260},{5,261},{6,262},{7,263},{8... | collective-permute-start | bytes 786440 | tf_op jit(solution)/shard_map/ppermute | solution.py:38
  103.4 12.9 %copy-start.2 = (f32[256,2,128]{2,1,0:T(2,128)S(1)}, f32[256,2,128]{2,1,0:T(2,128)}, u32[]{:S(2)}) copy-start(f32[256,2,128]{2,1,0:T(2,128)} %copy-done.1) | copy-start | bytes 786436
  103.4 12.9 %copy-start.4 = (f32[256,2,128]{2,1,0:T(2,128)S(1)}, f32[256,2,128]{2,1,0:T(2,128)}, u32[]{:S(2)}) copy-start(f32[256,2,128]{2,1,0:T(2,128)} %copy-done.3) | copy-start | bytes 786436
  103.4 12.9 %copy-start.17 = (f32[2,32,8,128]{3,2,1,0:T(8,128)S(1)}, f32[2,32,8,128]{3,2,1,0:T(8,128)}, u32[]{:S(2)}) copy-start(f32[2,32,8,128]{3,2,1,0:T(8,128)} %get-tuple-element.205) | copy-start | bytes 786436
  103.6 13.7 %collective-permute-start.7 = (bf16[2,2,128,256]{2,3,1,0:T(8,128)(2,1)S(1)}, bf16[2,2,128,256]{2,3,1,0:T(8,128)(2,1)S(1)}, u32[]{:S(2)}, u32[]{:S(2)}) collective-permute-start(bf16[2,2,128,256]{2,3,1,0:T(8,128)(2,1)S(1)} %get-tuple-element.184), channel_id=1, source_target_pairs={{1,0},{2,1},{3,2},{4,3},{5,4},{6,5},{7,6},{8,7},{9,8},{10,9},{11,1... | collective-permute-start | bytes 786440 | tf_op jit(solution)/shard_map/ppermute | solution.py:44
  113.4 15.4 %collective-permute-start.6 = (bf16[2,2,128,256]{2,3,1,0:T(8,128)(2,1)S(1)}, bf16[2,2,128,256]{2,3,1,0:T(8,128)(2,1)S(1)}, u32[]{:S(2)}, u32[]{:S(2)}) collective-permute-start(bf16[2,2,128,256]{2,3,1,0:T(8,128)(2,1)S(1)} %get-tuple-element.183), channel_id=1, source_target_pairs={{0,1},{1,2},{2,3},{3,4},{4,5},{5,6},{6,7},{7,8},{8,9},{9,10},{10,1... | collective-permute-start | bytes 786440 | tf_op jit(solution)/shard_map/ppermute | solution.py:44
  (46 other events, 221.1 us)
where the time goes:
time: 135 us; the launch traced here: 134 us
  starting transfers between devices  55.3 us (41%)
  local copies, waits for them, and re-layouts  25.8 us (19%)
  matrix products  19.2 us (14%)
  other arithmetic  17.8 us (13%)
  waiting for transfers between devices  13.7 us (10%)
  between operations  1.9 us (1%)
    ppermute x8, starting transfers between devices, partner(): return lax.ppermute(value, axis, pairs)  28.2 us
    ppermute x1, starting transfers between devices, with_halo(): lax.ppermute(leading, axis, [(b, a) for a, b in up])  13.3 us
    ppermute x2, starting transfers between devices, from_behind(): return lax.ppermute(x, axis, pairs)  12 us
    ppermute x2, waiting for transfers between devices, from_behind(): return lax.ppermute(x, axis, pairs)  11.8 us
    unnamed x123, local copies, waits for them, and re-layouts  6.63 us
    dot_general x2, matrix products, body(): jnp.einsum('ieuz,iuzg->ieg', score_gradient, head_keys, preferred_element...  4.27 us
    reduce_sum x2, other arithmetic, norm_back(): first = jnp.mean(scaled, axis=-1, keepdims=True)  4.05 us
    another operation x4, local copies, waits for them, and re-layouts, body(): jnp.stack((key_terms[:, offset], value_terms[:, offset]))  3.38 us
  transfers between devices with their start and end apart: 12, of which 3 were waited for; matrix products, arithmetic and copies ran while one was open for 12% of the time, Pallas kernels for 0%

commit v1 on v0

v1 whole, which is shorter than its diff:
```python
import functools

import jax
import jax.numpy as jnp
from jax import lax
from jax.experimental import pallas as pl
from jax.experimental.pallas import tpu as pltpu
from jax.sharding import PartitionSpec as P


HEADS = 2
BLOCK = 128
BAND = 2
LEVELS = 4
SLOTS = 7
AXES = ("grp", "ctx")
EPS = 1e-05
F32 = jnp.float32
BF16 = jnp.bfloat16

NT = (((1,), (1,)), ((), ()))
NN = (((1,), (0,)), ((), ()))
TN = (((0,), (0,)), ((), ()))


def dot(a, b, dims):
    return lax.dot_general(a, b, dims, preferred_element_type=F32)


def norm(raw, gain):
    x = raw.astype(F32)
    centred = x - jnp.mean(x, axis=-1, keepdims=True)
    inverse = lax.rsqrt(jnp.mean(centred * centred, axis=-1, keepdims=True) + EPS)
    normed = centred * inverse
    return normed, inverse, normed * gain


def norm_back(upstream, normed, inverse, gain):
    scaled = upstream * gain
    first = jnp.mean(scaled, axis=-1, keepdims=True)
    second = jnp.mean(scaled * normed, axis=-1, keepdims=True)
    return (scaled - first - normed * second) * inverse


def cols(h):
    return slice(h * 128, (h + 1) * 128)


def rows(i):
    return slice(i * BLOCK, (i + 1) * BLOCK)


def picked(ref, kind, pick, h):
    return ref[kind, pl.ds(pl.multiple_of(pick * BLOCK, BLOCK), BLOCK), cols(h)]


def prep_kernel(k_ref, v_ref, gain_ref, pack_ref):
    for h in range(HEADS):
        _, _, scaled = norm(k_ref[:, cols(h)], gain_ref[h : h + 1, :])
        pack_ref[0, :, cols(h)] = scaled.astype(BF16)
    pack_ref[1] = v_ref[...]


def local_kernel(
    dev_ref, reach_ref, part_ref, q_ref, gain_ref, cot_ref, own, left, right, x2, x1,
    qn_ref, e_ref, d_ref, o_ref, l_ref, *, last_block,
):
    scale = 128 ** (-0.5)
    for h in range(HEADS):
        _, _, scaled = norm(q_ref[:, cols(h)], gain_ref[h : h + 1, :])
        qn = scaled.astype(BF16)
        qn_ref[:, cols(h)] = qn
        ct = cot_ref[:, cols(h)]
        near = (left, own, right)
        s_near = [dot(qn, r[0, :, cols(h)], NT) for r in near]
        d_near = [dot(ct, r[1, :, cols(h)], NT) for r in near]
        for i in range(2):
            block = dev_ref[0] * 2 + i
            total = None
            e_list = []
            for slot in range(SLOTS):
                if slot < 5:
                    c = i + slot
                    s = s_near[c // 2][rows(i), rows(c % 2)]
                    d = d_near[c // 2][rows(i), rows(c % 2)]
                else:
                    ref = (x2, x1)[slot - 5]
                    pick = part_ref[i, slot - 5] & 1
                    s = dot(qn[rows(i)], picked(ref, 0, pick, h), NT)
                    d = dot(ct[rows(i)], picked(ref, 1, pick, h), NT)
                e = jnp.exp(s * scale)
                if slot < 5 and slot != 2:
                    off = slot - BAND
                    goal = block + off
                    ok = (abs(off) <= reach_ref[i]) & (goal >= 0) & (goal <= last_block)
                    e = e * jnp.where(ok, 1.0, 0.0).astype(F32)
                total = e if total is None else total + e
                low = e.astype(BF16)
                e_list.append(low)
                e_ref[h, slot, rows(i), :] = low
                d_ref[h, slot, rows(i), :] = d.astype(BF16)
            l_ref[h, rows(i), :] = jnp.broadcast_to(
                jnp.sum(total, axis=-1, keepdims=True), (BLOCK, 128)
            )
            v_list = [near[(i + s) // 2][1, rows((i + s) % 2), cols(h)] for s in range(5)]
            v_list += [picked(r, 1, part_ref[i, n] & 1, h) for n, r in enumerate((x2, x1))]
            o_ref[rows(i), cols(h)] = dot(
                jnp.concatenate(e_list, axis=1), jnp.concatenate(v_list, axis=0), NN
            )


def spread(terms, picks, g):
    parts = [t * jnp.where(p == g, 1.0, 0.0).astype(F32) for t, p in zip(terms, picks)]
    return (parts[0] + parts[1]).astype(BF16)


def far_kernel(
    part_ref, qn_ref, cot_ref, y2, y1, o_ref, l_ref,
    g2_ref, g1_ref, out_ref, rl_ref, delta_ref, dq_ref,
):
    scale = 128 ** (-0.5)
    for h in range(HEADS):
        k_terms = [[], []]
        v_terms = [[], []]
        for i in range(2):
            q = qn_ref[rows(i), cols(h)]
            ct = cot_ref[rows(i), cols(h)]
            picks = [part_ref[i, 2] & 1, part_ref[i, 3] & 1]
            ks = jnp.concatenate([picked(r, 0, p, h) for r, p in zip((y2, y1), picks)], axis=0)
            vs = jnp.concatenate([picked(r, 1, p, h) for r, p in zip((y2, y1), picks)], axis=0)
            e = jnp.exp(dot(q, ks, NT) * scale)
            dp = dot(ct, vs, NT)
            total = l_ref[h, rows(i), :1] + jnp.sum(e, axis=-1, keepdims=True)
            rl = 1.0 / total
            o = ((o_ref[rows(i), cols(h)] + dot(e.astype(BF16), vs, NN)) * rl).astype(BF16)
            out_ref[rows(i), cols(h)] = o
            delta = jnp.sum(ct.astype(F32) * o.astype(F32), axis=-1, keepdims=True)
            rl_ref[h, rows(i), :] = jnp.broadcast_to(rl, (BLOCK, 128))
            delta_ref[h, rows(i), :] = jnp.broadcast_to(delta, (BLOCK, 128))
            p = e * rl
            w = p.astype(BF16)
            ds = (p * (dp - delta)).astype(BF16)
            dq_ref[rows(i), cols(h)] = dot(ds, ks, NN)
            dk = dot(ds, q, TN) * scale
            dv = dot(w, ct, TN)
            for n in range(2):
                k_terms[n].append(dk[rows(n)])
                v_terms[n].append(dv[rows(n)])
        for n, ref in enumerate((g2_ref, g1_ref)):
            picks = [part_ref[i, 2 + n] & 1 for i in range(2)]
            for g in range(2):
                ref[0, rows(g), cols(h)] = spread(k_terms[n], picks, g)
                ref[1, rows(g), cols(h)] = spread(v_terms[n], picks, g)


def near_kernel(
    part_ref, q_ref, gain_ref, qn_ref, cot_ref, own, left, right, x2, x1, e_ref, d_ref,
    rl_ref, delta_ref, dqy_ref,
    gx2_ref, gx1_ref, gl_ref, gr_ref, gown_ref, gq_ref,
):
    scale = 128 ** (-0.5)
    near = (left, own, right)
    for h in range(HEADS):
        qn = qn_ref[:, cols(h)]
        ct = cot_ref[:, cols(h)]
        weights, grads = [], []
        for slot in range(SLOTS):
            p = e_ref[h, slot].astype(F32) * rl_ref[h]
            weights.append(p.astype(BF16))
            grads.append((p * (d_ref[h, slot].astype(F32) - delta_ref[h])).astype(BF16))
        for n, (src, ref) in enumerate(((x2, gx2_ref), (x1, gx1_ref))):
            slot = 5 + n
            picks = [part_ref[i, n] & 1 for i in range(2)]
            k_terms = [dot(grads[slot][rows(i)], qn[rows(i)], TN) * scale for i in range(2)]
            v_terms = [dot(weights[slot][rows(i)], ct[rows(i)], TN) for i in range(2)]
            for g in range(2):
                ref[0, rows(g), cols(h)] = spread(k_terms, picks, g)
                ref[1, rows(g), cols(h)] = spread(v_terms, picks, g)
        for c in range(6):
            picked_rows = [i for i in range(2) if 0 <= c - i < 5]
            span = slice(picked_rows[0] * BLOCK, (picked_rows[-1] + 1) * BLOCK)
            ds = jnp.concatenate([grads[c - i][rows(i)] for i in picked_rows], axis=0)
            w = jnp.concatenate([weights[c - i][rows(i)] for i in picked_rows], axis=0)
            dk = dot(ds, qn[span], TN) * scale
            dv = dot(w, ct[span], TN)
            ref = (gl_ref, gown_ref, gr_ref)[c // 2]
            ref[0, rows(c % 2), cols(h)] = dk.astype(ref.dtype)
            ref[1, rows(c % 2), cols(h)] = dv.astype(ref.dtype)
        normed, inverse, _ = norm(q_ref[:, cols(h)], gain_ref[h : h + 1, :])
        for i in range(2):
            k_list = [near[(i + s) // 2][0, rows((i + s) % 2), cols(h)] for s in range(5)]
            k_list += [picked(r, 0, part_ref[i, n] & 1, h) for n, r in enumerate((x2, x1))]
            dq = dot(
                jnp.concatenate([g[rows(i)] for g in grads], axis=1),
                jnp.concatenate(k_list, axis=0),
                NN,
            )
            dq = (dq + dqy_ref[rows(i), cols(h)]) * scale
            gq_ref[rows(i), cols(h)] = norm_back(
                dq, normed[rows(i)], inverse[rows(i)], gain_ref[h : h + 1, :]
            ).astype(BF16)


def final_kernel(k_ref, gain_ref, own, a, b, c, d, e, f, gk_ref, gv_ref):
    terms = (a, b, c, d, e, f)
    for h in range(HEADS):
        dk = own[0, :, cols(h)]
        dv = own[1, :, cols(h)]
        for t in terms:
            dk = dk + t[0, :, cols(h)].astype(F32)
            dv = dv + t[1, :, cols(h)].astype(F32)
        normed, inverse, _ = norm(k_ref[:, cols(h)], gain_ref[h : h + 1, :])
        gk_ref[:, cols(h)] = norm_back(dk, normed, inverse, gain_ref[h : h + 1, :]).astype(BF16)
        gv_ref[:, cols(h)] = dv.astype(BF16)


V = pl.BlockSpec(memory_space=pltpu.VMEM)
S = pl.BlockSpec(memory_space=pltpu.SMEM)


def call(kernel, specs, outs, flops, *args):
    shapes = [jax.ShapeDtypeStruct(s, t) for s, t in outs]
    moved = sum(a.size * a.dtype.itemsize for a in args)
    moved += sum(s.size * s.dtype.itemsize for s in shapes)
    return pl.pallas_call(
        kernel,
        out_shape=shapes,
        in_specs=specs,
        out_specs=[V] * len(shapes),
        compiler_params=pltpu.CompilerParams(vmem_limit_bytes=24 * 2**20),
        cost_estimate=pl.CostEstimate(flops=flops, transcendentals=0, bytes_accessed=moved),
    )(*args)


def body(query_raw, key_raw, values, band_reach, partners, gain_query, gain_key, cotangent):
    count = lax.axis_size(AXES)
    device = lax.axis_index(AXES).astype(jnp.int32).reshape(1)
    ups = [(i, i + 1) for i in range(count - 1)]
    downs = [(b, a) for a, b in ups]
    masks = [count >> (level + 1) for level in range(LEVELS)]
    across = [[(i, i ^ m) for i in range(count)] for m in masks]

    def send(value, perm):
        return lax.ppermute(value, AXES, perm)

    pack_t = ((2, 256, 256), BF16)

    (pack,) = call(prep_kernel, [V, V, V], [pack_t], 10**6, key_raw, values, gain_key)
    y2 = send(pack, across[2])
    y1 = send(pack, across[3])
    x2 = send(pack, across[0])
    x1 = send(pack, across[1])
    left = send(pack, ups)
    right = send(pack, downs)

    tiles = ((HEADS, SLOTS, 256, 128), BF16)
    rowstat = ((HEADS, 256, 128), F32)
    full = ((256, 256), F32)
    qn, e, d, o_part, l_part = call(
        functools.partial(local_kernel, last_block=2 * count - 1),
        [S, S, S] + [V] * 8,
        [((256, 256), BF16), tiles, tiles, full, rowstat],
        28 * 3 * 2 * 128**3,
        device, band_reach, partners, query_raw, gain_query, cotangent, pack, left, right, x2, x1,
    )
    gy2, gy1, out, rl, delta, dqy = call(
        far_kernel,
        [S] + [V] * 6,
        [pack_t, pack_t, ((256, 256), BF16), rowstat, rowstat, full],
        8 * 6 * 2 * 128**3,
        partners, qn, cotangent, y2, y1, o_part, l_part,
    )
    ry2 = send(gy2, across[2])
    ry1 = send(gy1, across[3])
    gx2, gx1, gl, gr, gown, grad_query = call(
        near_kernel,
        [S] + [V] * 14,
        [pack_t, pack_t, pack_t, pack_t, ((2, 256, 256), F32), ((256, 256), BF16)],
        28 * 3 * 2 * 128**3,
        partners, query_raw, gain_query, qn, cotangent, pack, left, right, x2, x1, e, d,
        rl, delta, dqy,
    )
    rx2 = send(gx2, across[0])
    rx1 = send(gx1, across[1])
    rl_ = send(gr, ups)
    rr_ = send(gl, downs)
    grad_key, grad_value = call(
        final_kernel,
        [V] * 9,
        [((256, 256), BF16), ((256, 256), BF16)],
        10**6,
        key_raw, gain_key, gown, ry2, ry1, rx2, rx1, rl_, rr_,
    )
    return (out, grad_query, grad_key, grad_value)


def solution(mesh):
    wide = P(AXES, None)
    return jax.shard_map(
        body,
        mesh=mesh,
        in_specs=(wide, wide, wide, P(AXES), wide, P(), P(), wide),
        out_specs=(wide, wide, wide, wide),
        check_vma=False,
    )
```

time: 135 us -> 97.4 us (0.72)
  the two profiles are of different devices: /device:TPU:2 before, /device:TPU:1 now
where the time goes in v1:
time: 97.4 us; the launch traced here: 96.9 us
  starting transfers between devices  58.5 us (60%)
  waiting for transfers between devices  25.3 us (26%)
  Pallas kernels  9.02 us (9%)
  local copies, waits for them, and re-layouts  3.16 us (3%)
    ppermute x12, starting transfers between devices, send(): return lax.ppermute(value, AXES, perm)  58.5 us
    ppermute x12, waiting for transfers between devices, send(): return lax.ppermute(value, AXES, perm)  25.3 us
    pallas_call x5, Pallas kernels, call(): pl.pallas_call(kernel, out_shape=shapes, in_specs=specs, out_specs=[V] *...  9.02 us
    unnamed x20, local copies, waits for them, and re-layouts  3.16 us
  transfers between devices with their start and end apart: 12, of which 2 were waited for; matrix products, arithmetic and copies ran while one was open for 0% of the time, Pallas kernels for 2%

profile of v1, /device:TPU:1, one launch (start us, length us, event | category | flops | bytes accessed | tf_op | source)
XLA Modules:
  0.0 96.9 jit_solution(18150482458106916001)
XLA Ops:
  0.7 0.9 copy-done.1
  1.6 0.9 copy-done.4
  2.5 0.7 copy-done.6
  3.2 0.2 shard_map.111.own
  3.4 3.9 %collective-permute-start.3 = (bf16[2,256,256]{2,1,0:T(8,128)(2,1)S(1)}, bf16[2,256,256]{2,1,0:T(8,128)(2,1)S(1)}, u32[]{:S(2)}, u32[]{:S(2)}) collective-permute-start(bf16[2,256,256]{2,1,0:T(8,128)(2,1)S(1)} %shard_map.111.own), channel_id=1, source_target_pairs={{0,128},{1,129},{2,130},{3,131},{4,132},{5,133},{6,134},{7,135},{8... | collective-permute-start | bytes 786440 | tf_op jit(solution)/shard_map/ppermute | solution.py:244
  7.4 4.4 %collective-permute-start.2 = (bf16[2,256,256]{2,1,0:T(8,128)(2,1)S(1)}, bf16[2,256,256]{2,1,0:T(8,128)(2,1)S(1)}, u32[]{:S(2)}, u32[]{:S(2)}) collective-permute-start(bf16[2,256,256]{2,1,0:T(8,128)(2,1)S(1)} %shard_map.111.own), channel_id=1, source_target_pairs={{0,256},{1,257},{2,258},{3,259},{4,260},{5,261},{6,262},{7,263},{8... | collective-permute-start | bytes 786440 | tf_op jit(solution)/shard_map/ppermute | solution.py:244
  11.7 4.3 %collective-permute-start.1 = (bf16[2,256,256]{2,1,0:T(8,128)(2,1)S(1)}, bf16[2,256,256]{2,1,0:T(8,128)(2,1)S(1)}, u32[]{:S(2)}, u32[]{:S(2)}) collective-permute-start(bf16[2,256,256]{2,1,0:T(8,128)(2,1)S(1)} %shard_map.111.own), channel_id=1, source_target_pairs={{1,0},{2,1},{3,2},{4,3},{5,4},{6,5},{7,6},{8,7},{9,8},{10,9},{11,1... | collective-permute-start | bytes 786440 | tf_op jit(solution)/shard_map/ppermute | solution.py:244
  16.0 2.7 %collective-permute-start = (bf16[2,256,256]{2,1,0:T(8,128)(2,1)S(1)}, bf16[2,256,256]{2,1,0:T(8,128)(2,1)S(1)}, u32[]{:S(2)}, u32[]{:S(2)}) collective-permute-start(bf16[2,256,256]{2,1,0:T(8,128)(2,1)S(1)} %shard_map.111.own), channel_id=1, source_target_pairs={{0,1},{1,2},{2,3},{3,4},{4,5},{5,6},{6,7},{7,8},{8,9},{9,10},{10,1... | collective-permute-start | bytes 786440 | tf_op jit(solution)/shard_map/ppermute | solution.py:244
  18.8 4.2 %collective-permute-start.5 = (bf16[2,256,256]{2,1,0:T(8,128)(2,1)S(1)}, bf16[2,256,256]{2,1,0:T(8,128)(2,1)S(1)}, u32[]{:S(2)}, u32[]{:S(2)}) collective-permute-start(bf16[2,256,256]{2,1,0:T(8,128)(2,1)S(1)} %shard_map.111.own), channel_id=1, source_target_pairs={{0,32},{1,33},{2,34},{3,35},{4,36},{5,37},{6,38},{7,39},{8,40},{9,... | collective-permute-start | bytes 786440 | tf_op jit(solution)/shard_map/ppermute | solution.py:244
  23.0 5.7 %collective-permute-start.4 = (bf16[2,256,256]{2,1,0:T(8,128)(2,1)S(1)}, bf16[2,256,256]{2,1,0:T(8,128)(2,1)S(1)}, u32[]{:S(2)}, u32[]{:S(2)}) collective-permute-start(bf16[2,256,256]{2,1,0:T(8,128)(2,1)S(1)} %shard_map.111.own), channel_id=1, source_target_pairs={{0,64},{1,65},{2,66},{3,67},{4,68},{5,69},{6,70},{7,71},{8,72},{9,... | collective-permute-start | bytes 786440 | tf_op jit(solution)/shard_map/ppermute | solution.py:244
  28.8 0.6 copy-done.8
  29.4 0.0 copy-done.5
  29.4 2.1 %shard_map.112 = (bf16[256,256]{1,0:T(8,128)(2,1)S(1)}, bf16[2,7,256,128]{3,2,1,0:T(8,128)(2,1)S(1)}, bf16[2,7,256,128]{3,2,1,0:T(8,128)(2,1)S(1)}, f32[256,256]{1,0:T(8,128)S(1)}, f32[2,256,128]{2,1,0:T(8,128)S(1)}) custom-call(s32[1]{0:T(128)} %bitcast.dev_ref, s32[2]{0:T(128)S(1)} %copy-done.9, s32[2,4]{1,0:T(2,128)S(1)} %copy-done.5, ...), custom_call_target="tpu_custom_call" | custom-call | flops 352321536 | bytes 4064300 | tf_op jit(solution)/shard_map/pallas_call | solution.py:225
  31.5 8.4 %collective-permute-done.4.y2 = bf16[2,256,256]{2,1,0:T(8,128)(2,1)S(1)} collective-permute-done((bf16[2,256,256]{2,1,0:T(8,128)(2,1)S(1)}, bf16[2,256,256]{2,1,0:T(8,128)(2,1)S(1)}, u32[]{:S(2)}, u32[]{:S(2)}) %collective-permute-start.4) | collective-permute-done | bytes 262176 | tf_op jit(solution)/shard_map/ppermute | solution.py:244
  39.9 3.0 %shard_map.113 = (bf16[2,256,256]{2,1,0:T(8,128)(2,1)S(1)}, bf16[2,256,256]{2,1,0:T(8,128)(2,1)S(1)}, bf16[256,256]{1,0:T(8,128)(2,1)}, f32[2,256,128]{2,1,0:T(8...) custom-call(s32[2,4]{1,0:T(2,128)S(1)} %copy-done.5, bf16[256,256]{1,0:T(8,128)(2,1)S(1)} %get-tuple-element.23.qn_ref, ...), custom_call_target="tpu_custom_call" | custom-call | flops 201326592 | bytes 2752544 | tf_op jit(solution)/shard_map/pallas_call | solution.py:225
  42.9 2.5 %shard_map.114 = (bf16[2,256,256]{2,1,0:T(8,128)(2,1)S(1)}, bf16[2,256,256]{2,1,0:T(8,128)(2,1)S(1)}, bf16[2,256,256]{2,1,0:T(8,128)(2,1)S(1)}, bf16[2,256,256]{...) custom-call(s32[2,4]{1,0:T(2,128)S(1)} %copy-done.5, bf16[256,256]{1,0:T(8,128)(2,1)S(1)} %copy-done.3, ...), custom_call_target="tpu_custom_call" | custom-call | flops 352321536 | bytes 6030368 | tf_op jit(solution)/shard_map/pallas_call | solution.py:225
  45.4 10.0 %collective-permute-start.8 = (bf16[2,256,256]{2,1,0:T(8,128)(2,1)S(1)}, bf16[2,256,256]{2,1,0:T(8,128)(2,1)S(1)}, u32[]{:S(2)}, u32[]{:S(2)}) collective-permute-start(bf16[2,256,256]{2,1,0:T(8,128)(2,1)S(1)} %get-tuple-element.36), channel_id=1, source_target_pairs={{0,256},{1,257},{2,258},{3,259},{4,260},{5,261},{6,262},{7,263},{8... | collective-permute-start | bytes 786440 | tf_op jit(solution)/shard_map/ppermute | solution.py:244
  55.4 2.6 %collective-permute-start.9 = (bf16[2,256,256]{2,1,0:T(8,128)(2,1)S(1)}, bf16[2,256,256]{2,1,0:T(8,128)(2,1)S(1)}, u32[]{:S(2)}, u32[]{:S(2)}) collective-permute-start(bf16[2,256,256]{2,1,0:T(8,128)(2,1)S(1)} %get-tuple-element.37), channel_id=1, source_target_pairs={{0,128},{1,129},{2,130},{3,131},{4,132},{5,133},{6,134},{7,135},{8... | collective-permute-start | bytes 786440 | tf_op jit(solution)/shard_map/ppermute | solution.py:244
  58.0 1.9 %collective-permute-start.10 = (bf16[2,256,256]{2,1,0:T(8,128)(2,1)S(1)}, bf16[2,256,256]{2,1,0:T(8,128)(2,1)S(1)}, u32[]{:S(2)}, u32[]{:S(2)}) collective-permute-start(bf16[2,256,256]{2,1,0:T(8,128)(2,1)S(1)} %get-tuple-element.38), channel_id=1, source_target_pairs={{0,1},{1,2},{2,3},{3,4},{4,5},{5,6},{6,7},{7,8},{8,9},{9,10},{10,1... | collective-permute-start | bytes 786440 | tf_op jit(solution)/shard_map/ppermute | solution.py:244
  59.9 4.9 %collective-permute-start.11 = (bf16[2,256,256]{2,1,0:T(8,128)(2,1)S(1)}, bf16[2,256,256]{2,1,0:T(8,128)(2,1)S(1)}, u32[]{:S(2)}, u32[]{:S(2)}) collective-permute-start(bf16[2,256,256]{2,1,0:T(8,128)(2,1)S(1)} %get-tuple-element.39), channel_id=1, source_target_pairs={{1,0},{2,1},{3,2},{4,3},{5,4},{6,5},{7,6},{8,7},{9,8},{10,9},{11,1... | collective-permute-start | bytes 786440 | tf_op jit(solution)/shard_map/ppermute | solution.py:244
  64.8 7.1 %collective-permute-start.6 = (bf16[2,256,256]{2,1,0:T(8,128)(2,1)S(1)}, bf16[2,256,256]{2,1,0:T(8,128)(2,1)S(1)}, u32[]{:S(2)}, u32[]{:S(2)}) collective-permute-start(bf16[2,256,256]{2,1,0:T(8,128)(2,1)S(1)} %get-tuple-element.34), channel_id=1, source_target_pairs={{0,64},{1,65},{2,66},{3,67},{4,68},{5,69},{6,70},{7,71},{8,72},{9,... | collective-permute-start | bytes 786440 | tf_op jit(solution)/shard_map/ppermute | solution.py:244
  71.9 6.8 %collective-permute-start.7 = (bf16[2,256,256]{2,1,0:T(8,128)(2,1)S(1)}, bf16[2,256,256]{2,1,0:T(8,128)(2,1)S(1)}, u32[]{:S(2)}, u32[]{:S(2)}) collective-permute-start(bf16[2,256,256]{2,1,0:T(8,128)(2,1)S(1)} %get-tuple-element.35), channel_id=1, source_target_pairs={{0,32},{1,33},{2,34},{3,35},{4,36},{5,37},{6,38},{7,39},{8,40},{9,... | collective-permute-start | bytes 786440 | tf_op jit(solution)/shard_map/ppermute | solution.py:244
  78.8 16.9 %collective-permute-done.7.b = bf16[2,256,256]{2,1,0:T(8,128)(2,1)S(1)} collective-permute-done((bf16[2,256,256]{2,1,0:T(8,128)(2,1)S(1)}, bf16[2,256,256]{2,1,0:T(8,128)(2,1)S(1)}, u32[]{:S(2)}, u32[]{:S(2)}) %collective-permute-start.7) | collective-permute-done | bytes 262176 | tf_op jit(solution)/shard_map/ppermute | solution.py:244
  95.7 1.2 %shard_map.115 = (bf16[256,256]{1,0:T(8,128)(2,1)}, bf16[256,256]{1,0:T(8,128)(2,1)}) custom-call(bf16[256,256]{1,0:T(8,128)(2,1)S(1)} %copy-done.2, f32[2,128]{1,0:T(2,128)S(1)} %copy-done.7, f32[2,256,256]{2,1,0:T(8,128)S(1)} %get-tuple-element.33.own, bf16[2,256,256]{2,1,0:T(8,128)(2,1)S(1)} %collective-permute-done.6.a, ...), custom_call_target="tpu_custom_call" | custom-call | flops 1000000 | bytes 2491392 | tf_op jit(solution)/shard_map/pallas_call | solution.py:225
  (25 shorter events, 0.1 us)
Async XLA Ops:
  0.6 28.1 %copy-start = (bf16[256,256]{1,0:T(8,128)(2,1)S(1)}, bf16[256,256]{1,0:T(8,128)(2,1)}, u32[]{:S(2)}) copy-start(bf16[256,256]{1,0:T(8,128)(2,1)} %cot_ref.5) | copy-start | bytes 393220
  0.6 0.9 copy-start.1
  1.6 0.9 copy-start.4
  2.5 0.7 copy-start.6
  3.2 25.6 %copy-start.3 = (bf16[256,256]{1,0:T(8,128)(2,1)S(1)}, bf16[256,256]{1,0:T(8,128)(2,1)}, u32[]{:S(2)}) copy-start(bf16[256,256]{1,0:T(8,128)(2,1)} %q_ref.3) | copy-start | bytes 393220
  3.4 19.6 %collective-permute-start.3 = (bf16[2,256,256]{2,1,0:T(8,128)(2,1)S(1)}, bf16[2,256,256]{2,1,0:T(8,128)(2,1)S(1)}, u32[]{:S(2)}, u32[]{:S(2)}) collective-permute-start(bf16[2,256,256]{2,1,0:T(8,128)(2,1)S(1)} %shard_map.111.own), channel_id=1, source_target_pairs={{0,128},{1,129},{2,130},{3,131},{4,132},{5,133},{6,134},{7,135},{8... | collective-permute-start | bytes 786440 | tf_op jit(solution)/shard_map/ppermute | solution.py:244
  7.4 21.4 %collective-permute-start.2 = (bf16[2,256,256]{2,1,0:T(8,128)(2,1)S(1)}, bf16[2,256,256]{2,1,0:T(8,128)(2,1)S(1)}, u32[]{:S(2)}, u32[]{:S(2)}) collective-permute-start(bf16[2,256,256]{2,1,0:T(8,128)(2,1)S(1)} %shard_map.111.own), channel_id=1, source_target_pairs={{0,256},{1,257},{2,258},{3,259},{4,260},{5,261},{6,262},{7,263},{8... | collective-permute-start | bytes 786440 | tf_op jit(solution)/shard_map/ppermute | solution.py:244
  11.7 17.0 %collective-permute-start.1 = (bf16[2,256,256]{2,1,0:T(8,128)(2,1)S(1)}, bf16[2,256,256]{2,1,0:T(8,128)(2,1)S(1)}, u32[]{:S(2)}, u32[]{:S(2)}) collective-permute-start(bf16[2,256,256]{2,1,0:T(8,128)(2,1)S(1)} %shard_map.111.own), channel_id=1, source_target_pairs={{1,0},{2,1},{3,2},{4,3},{5,4},{6,5},{7,6},{8,7},{9,8},{10,9},{11,1... | collective-permute-start | bytes 786440 | tf_op jit(solution)/shard_map/ppermute | solution.py:244
  16.0 12.7 %collective-permute-start = (bf16[2,256,256]{2,1,0:T(8,128)(2,1)S(1)}, bf16[2,256,256]{2,1,0:T(8,128)(2,1)S(1)}, u32[]{:S(2)}, u32[]{:S(2)}) collective-permute-start(bf16[2,256,256]{2,1,0:T(8,128)(2,1)S(1)} %shard_map.111.own), channel_id=1, source_target_pairs={{0,1},{1,2},{2,3},{3,4},{4,5},{5,6},{6,7},{7,8},{8,9},{9,10},{10,1... | collective-permute-start | bytes 786440 | tf_op jit(solution)/shard_map/ppermute | solution.py:244
  18.8 12.7 %collective-permute-start.5 = (bf16[2,256,256]{2,1,0:T(8,128)(2,1)S(1)}, bf16[2,256,256]{2,1,0:T(8,128)(2,1)S(1)}, u32[]{:S(2)}, u32[]{:S(2)}) collective-permute-start(bf16[2,256,256]{2,1,0:T(8,128)(2,1)S(1)} %shard_map.111.own), channel_id=1, source_target_pairs={{0,32},{1,33},{2,34},{3,35},{4,36},{5,37},{6,38},{7,39},{8,40},{9,... | collective-permute-start | bytes 786440 | tf_op jit(solution)/shard_map/ppermute | solution.py:244
  23.0 16.9 %collective-permute-start.4 = (bf16[2,256,256]{2,1,0:T(8,128)(2,1)S(1)}, bf16[2,256,256]{2,1,0:T(8,128)(2,1)S(1)}, u32[]{:S(2)}, u32[]{:S(2)}) collective-permute-start(bf16[2,256,256]{2,1,0:T(8,128)(2,1)S(1)} %shard_map.111.own), channel_id=1, source_target_pairs={{0,64},{1,65},{2,66},{3,67},{4,68},{5,69},{6,70},{7,71},{8,72},{9,... | collective-permute-start | bytes 786440 | tf_op jit(solution)/shard_map/ppermute | solution.py:244
  28.7 0.7 copy-start.8
  28.7 0.7 copy-start.5
  28.7 0.7 copy-start.9
  42.9 52.8 %copy-start.2 = (bf16[256,256]{1,0:T(8,128)(2,1)S(1)}, bf16[256,256]{1,0:T(8,128)(2,1)}, u32[]{:S(2)}) copy-start(bf16[256,256]{1,0:T(8,128)(2,1)} %k_ref.3) | copy-start | bytes 393220
  45.4 26.5 %collective-permute-start.8 = (bf16[2,256,256]{2,1,0:T(8,128)(2,1)S(1)}, bf16[2,256,256]{2,1,0:T(8,128)(2,1)S(1)}, u32[]{:S(2)}, u32[]{:S(2)}) collective-permute-start(bf16[2,256,256]{2,1,0:T(8,128)(2,1)S(1)} %get-tuple-element.36), channel_id=1, source_target_pairs={{0,256},{1,257},{2,258},{3,259},{4,260},{5,261},{6,262},{7,263},{8... | collective-permute-start | bytes 786440 | tf_op jit(solution)/shard_map/ppermute | solution.py:244
  55.4 23.4 %collective-permute-start.9 = (bf16[2,256,256]{2,1,0:T(8,128)(2,1)S(1)}, bf16[2,256,256]{2,1,0:T(8,128)(2,1)S(1)}, u32[]{:S(2)}, u32[]{:S(2)}) collective-permute-start(bf16[2,256,256]{2,1,0:T(8,128)(2,1)S(1)} %get-tuple-element.37), channel_id=1, source_target_pairs={{0,128},{1,129},{2,130},{3,131},{4,132},{5,133},{6,134},{7,135},{8... | collective-permute-start | bytes 786440 | tf_op jit(solution)/shard_map/ppermute | solution.py:244
  58.0 20.8 %collective-permute-start.10 = (bf16[2,256,256]{2,1,0:T(8,128)(2,1)S(1)}, bf16[2,256,256]{2,1,0:T(8,128)(2,1)S(1)}, u32[]{:S(2)}, u32[]{:S(2)}) collective-permute-start(bf16[2,256,256]{2,1,0:T(8,128)(2,1)S(1)} %get-tuple-element.38), channel_id=1, source_target_pairs={{0,1},{1,2},{2,3},{3,4},{4,5},{5,6},{6,7},{7,8},{8,9},{9,10},{10,1... | collective-permute-start | bytes 786440 | tf_op jit(solution)/shard_map/ppermute | solution.py:244
  59.9 18.9 %collective-permute-start.11 = (bf16[2,256,256]{2,1,0:T(8,128)(2,1)S(1)}, bf16[2,256,256]{2,1,0:T(8,128)(2,1)S(1)}, u32[]{:S(2)}, u32[]{:S(2)}) collective-permute-start(bf16[2,256,256]{2,1,0:T(8,128)(2,1)S(1)} %get-tuple-element.39), channel_id=1, source_target_pairs={{1,0},{2,1},{3,2},{4,3},{5,4},{6,5},{7,6},{8,7},{9,8},{10,9},{11,1... | collective-permute-start | bytes 786440 | tf_op jit(solution)/shard_map/ppermute | solution.py:244
  64.8 14.0 %collective-permute-start.6 = (bf16[2,256,256]{2,1,0:T(8,128)(2,1)S(1)}, bf16[2,256,256]{2,1,0:T(8,128)(2,1)S(1)}, u32[]{:S(2)}, u32[]{:S(2)}) collective-permute-start(bf16[2,256,256]{2,1,0:T(8,128)(2,1)S(1)} %get-tuple-element.34), channel_id=1, source_target_pairs={{0,64},{1,65},{2,66},{3,67},{4,68},{5,69},{6,70},{7,71},{8,72},{9,... | collective-permute-start | bytes 786440 | tf_op jit(solution)/shard_map/ppermute | solution.py:244
  71.9 23.8 %copy-start.7 = (f32[2,128]{1,0:T(2,128)S(1)}, f32[2,128]{1,0:T(2,128)}, u32[]{:S(2)}) copy-start(f32[2,128]{1,0:T(2,128)} %gain_ref.7) | copy-start | bytes 3076
  71.9 23.8 %collective-permute-start.7 = (bf16[2,256,256]{2,1,0:T(8,128)(2,1)S(1)}, bf16[2,256,256]{2,1,0:T(8,128)(2,1)S(1)}, u32[]{:S(2)}, u32[]{:S(2)}) collective-permute-start(bf16[2,256,256]{2,1,0:T(8,128)(2,1)S(1)} %get-tuple-element.35), channel_id=1, source_target_pairs={{0,32},{1,33},{2,34},{3,35},{4,36},{5,37},{6,38},{7,39},{8,40},{9,... | collective-permute-start | bytes 786440 | tf_op jit(solution)/shard_map/ppermute | solution.py:244

commit v2 on v1

--- a/solution.py
+++ b/solution.py
@@ -12,7 +12,7 @@
 BLOCK = 128
 BAND = 2
 LEVELS = 4
-SLOTS = 7
+BANDS = 2 * BAND + 1
 AXES = ("grp", "ctx")
 EPS = 1e-05
 F32 = jnp.float32
@@ -54,42 +54,49 @@
     return ref[kind, pl.ds(pl.multiple_of(pick * BLOCK, BLOCK), BLOCK), cols(h)]
 
 
-def prep_kernel(k_ref, v_ref, gain_ref, pack_ref):
+def prep_kernel(k_hbm, v_hbm, gain_hbm, pack_ref, k_ref, gain_ref, sems):
+    copies = [
+        pltpu.make_async_copy(k_hbm, k_ref, sems.at[0]),
+        pltpu.make_async_copy(gain_hbm, gain_ref, sems.at[1]),
+        pltpu.make_async_copy(v_hbm, pack_ref.at[1], sems.at[2]),
+    ]
+    for copy in copies:
+        copy.start()
+    copies[0].wait()
+    copies[1].wait()
     for h in range(HEADS):
         _, _, scaled = norm(k_ref[:, cols(h)], gain_ref[h : h + 1, :])
         pack_ref[0, :, cols(h)] = scaled.astype(BF16)
-    pack_ref[1] = v_ref[...]
+    copies[2].wait()
 
 
 def local_kernel(
-    dev_ref, reach_ref, part_ref, q_ref, gain_ref, cot_ref, own, left, right, x2, x1,
+    dev_ref, reach_ref, part_ref, q_ref, gain_ref, cot_ref, own, left, right,
     qn_ref, e_ref, d_ref, o_ref, l_ref, *, last_block,
 ):
     scale = 128 ** (-0.5)
-    for h in range(HEADS):
-        _, _, scaled = norm(q_ref[:, cols(h)], gain_ref[h : h + 1, :])
-        qn = scaled.astype(BF16)
-        qn_ref[:, cols(h)] = qn
-        ct = cot_ref[:, cols(h)]
-        near = (left, own, right)
-        s_near = [dot(qn, r[0, :, cols(h)], NT) for r in near]
-        d_near = [dot(ct, r[1, :, cols(h)], NT) for r in near]
+    near = (left, own, right)
+    both = range(HEADS)
+    qn = [norm(q_ref[:, cols(h)], gain_ref[h : h + 1, :])[2].astype(BF16) for h in both]
+    ct = [cot_ref[:, cols(h)] for h in both]
+    for h in both:
+        qn_ref[:, cols(h)] = qn[h]
+    s_near = [[dot(qn[h], r[0, :, cols(h)], NT) for r in near] for h in both]
+    for h in both:
+        d_near = [dot(ct[h], r[1, :, cols(h)], NT) for r in near]
+        for i in range(2):
+            for slot in range(BANDS):
+                c = i + slot
+                d_ref[h, slot, rows(i), :] = d_near[c // 2][rows(i), rows(c % 2)].astype(BF16)
+    for h in both:
         for i in range(2):
             block = dev_ref[0] * 2 + i
             total = None
             e_list = []
-            for slot in range(SLOTS):
-                if slot < 5:
-                    c = i + slot
-                    s = s_near[c // 2][rows(i), rows(c % 2)]
-                    d = d_near[c // 2][rows(i), rows(c % 2)]
-                else:
-                    ref = (x2, x1)[slot - 5]
-                    pick = part_ref[i, slot - 5] & 1
-                    s = dot(qn[rows(i)], picked(ref, 0, pick, h), NT)
-                    d = dot(ct[rows(i)], picked(ref, 1, pick, h), NT)
-                e = jnp.exp(s * scale)
-                if slot < 5 and slot != 2:
+            for slot in range(BANDS):
+                c = i + slot
+                e = jnp.exp(s_near[h][c // 2][rows(i), rows(c % 2)] * scale)
+                if slot != BAND:
                     off = slot - BAND
                     goal = block + off
                     ok = (abs(off) <= reach_ref[i]) & (goal >= 0) & (goal <= last_block)
@@ -98,12 +105,10 @@
                 low = e.astype(BF16)
                 e_list.append(low)
                 e_ref[h, slot, rows(i), :] = low
-                d_ref[h, slot, rows(i), :] = d.astype(BF16)
             l_ref[h, rows(i), :] = jnp.broadcast_to(
                 jnp.sum(total, axis=-1, keepdims=True), (BLOCK, 128)
             )
-            v_list = [near[(i + s) // 2][1, rows((i + s) % 2), cols(h)] for s in range(5)]
-            v_list += [picked(r, 1, part_ref[i, n] & 1, h) for n, r in enumerate((x2, x1))]
+            v_list = [near[(i + s) // 2][1, rows((i + s) % 2), cols(h)] for s in range(BANDS)]
             o_ref[rows(i), cols(h)] = dot(
                 jnp.concatenate(e_list, axis=1), jnp.concatenate(v_list, axis=0), NN
             )
@@ -115,47 +120,60 @@
 
 
 def far_kernel(
-    part_ref, qn_ref, cot_ref, y2, y1, o_ref, l_ref,
-    g2_ref, g1_ref, out_ref, rl_ref, delta_ref, dq_ref,
+    part_ref, qn_ref, cot_ref, x2, x1, y2, y1, o_ref, l_ref,
+    g2_ref, g1_ref, out_ref, rl_ref, delta_ref, dq_ref, e_ref, d_ref,
 ):
     scale = 128 ** (-0.5)
+    levels = (x2, x1, y2, y1)
+    each = [(h, i) for h in range(HEADS) for i in range(2)]
+    pick = [[part_ref[i, n] & 1 for n in range(LEVELS)] for i in range(2)]
+    q = {(h, i): qn_ref[rows(i), cols(h)] for h, i in each}
+    ct = {(h, i): cot_ref[rows(i), cols(h)] for h, i in each}
+    ks = {
+        (h, i): jnp.concatenate([picked(r, 0, p, h) for r, p in zip(levels, pick[i])], axis=0)
+        for h, i in each
+    }
+    vs = {
+        (h, i): jnp.concatenate([picked(r, 1, p, h) for r, p in zip(levels, pick[i])], axis=0)
+        for h, i in each
+    }
+    e = {t: jnp.exp(dot(q[t], ks[t], NT) * scale) for t in each}
+    dp = {t: dot(ct[t], vs[t], NT) for t in each}
+    low = {t: e[t].astype(BF16) for t in each}
+    far_o = {t: dot(low[t], vs[t], NN) for t in each}
+    p, ds, rl = {}, {}, {}
+    for t in each:
+        h, i = t
+        total = e[t][:, :128] + e[t][:, 128:256] + e[t][:, 256:384] + e[t][:, 384:]
+        total = l_ref[h, rows(i), :1] + jnp.sum(total, axis=-1, keepdims=True)
+        rl[t] = 1.0 / total
+        o = ((o_ref[rows(i), cols(h)] + far_o[t]) * rl[t]).astype(BF16)
+        out_ref[rows(i), cols(h)] = o
+        delta = jnp.sum(ct[t].astype(F32) * o.astype(F32), axis=-1, keepdims=True)
+        rl_ref[h, rows(i), :] = jnp.broadcast_to(rl[t], (BLOCK, 128))
+        delta_ref[h, rows(i), :] = jnp.broadcast_to(delta, (BLOCK, 128))
+        y = slice(256, 512)
+        p[t] = e[t][:, y] * rl[t]
+        ds[t] = (p[t] * (dp[t][:, y] - delta)).astype(BF16)
+    dk = {t: dot(ds[t], q[t], TN) * scale for t in each}
+    dv = {t: dot(p[t].astype(BF16), ct[t], TN) for t in each}
     for h in range(HEADS):
-        k_terms = [[], []]
-        v_terms = [[], []]
-        for i in range(2):
-            q = qn_ref[rows(i), cols(h)]
-            ct = cot_ref[rows(i), cols(h)]
-            picks = [part_ref[i, 2] & 1, part_ref[i, 3] & 1]
-            ks = jnp.concatenate([picked(r, 0, p, h) for r, p in zip((y2, y1), picks)], axis=0)
-            vs = jnp.concatenate([picked(r, 1, p, h) for r, p in zip((y2, y1), picks)], axis=0)
-            e = jnp.exp(dot(q, ks, NT) * scale)
-            dp = dot(ct, vs, NT)
-            total = l_ref[h, rows(i), :1] + jnp.sum(e, axis=-1, keepdims=True)
-            rl = 1.0 / total
-            o = ((o_ref[rows(i), cols(h)] + dot(e.astype(BF16), vs, NN)) * rl).astype(BF16)
-            out_ref[rows(i), cols(h)] = o
-            delta = jnp.sum(ct.astype(F32) * o.astype(F32), axis=-1, keepdims=True)
-            rl_ref[h, rows(i), :] = jnp.broadcast_to(rl, (BLOCK, 128))
-            delta_ref[h, rows(i), :] = jnp.broadcast_to(delta, (BLOCK, 128))
-            p = e * rl
-            w = p.astype(BF16)
-            ds = (p * (dp - delta)).astype(BF16)
-            dq_ref[rows(i), cols(h)] = dot(ds, ks, NN)
-            dk = dot(ds, q, TN) * scale
-            dv = dot(w, ct, TN)
-            for n in range(2):
-                k_terms[n].append(dk[rows(n)])
-                v_terms[n].append(dv[rows(n)])
         for n, ref in enumerate((g2_ref, g1_ref)):
-            picks = [part_ref[i, 2 + n] & 1 for i in range(2)]
+            picks = [pick[i][2 + n] for i in range(2)]
             for g in range(2):
-                ref[0, rows(g), cols(h)] = spread(k_terms[n], picks, g)
-                ref[1, rows(g), cols(h)] = spread(v_terms[n], picks, g)
+                ref[0, rows(g), cols(h)] = spread([dk[h, i][rows(n)] for i in range(2)], picks, g)
+                ref[1, rows(g), cols(h)] = spread([dv[h, i][rows(n)] for i in range(2)], picks, g)
+    for t in each:
+        h, i = t
+        dq_ref[rows(i), cols(h)] = dot(ds[t], ks[t][256:], NN)
+        for n in range(2):
+            e_ref[h, n, rows(i), :] = low[t][:, rows(n)]
+            d_ref[h, n, rows(i), :] = dp[t][:, rows(n)].astype(BF16)
 
 
 def near_kernel(
     part_ref, q_ref, gain_ref, qn_ref, cot_ref, own, left, right, x2, x1, e_ref, d_ref,
-    rl_ref, delta_ref, dqy_ref,
+    ex_ref, dx_ref, rl_ref, delta_ref, dqy_ref,
     gx2_ref, gx1_ref, gl_ref, gr_ref, gown_ref, gq_ref,
 ):
     scale = 128 ** (-0.5)
@@ -164,12 +182,14 @@
         qn = qn_ref[:, cols(h)]
         ct = cot_ref[:, cols(h)]
         weights, grads = [], []
-        for slot in range(SLOTS):
-            p = e_ref[h, slot].astype(F32) * rl_ref[h]
+        tiles = [(e_ref[h, s], d_ref[h, s]) for s in range(BANDS)]
+        tiles += [(ex_ref[h, s], dx_ref[h, s]) for s in range(2)]
+        for e, d in tiles:
+            p = e.astype(F32) * rl_ref[h]
             weights.append(p.astype(BF16))
-            grads.append((p * (d_ref[h, slot].astype(F32) - delta_ref[h])).astype(BF16))
+            grads.append((p * (d.astype(F32) - delta_ref[h])).astype(BF16))
         for n, (src, ref) in enumerate(((x2, gx2_ref), (x1, gx1_ref))):
-            slot = 5 + n
+            slot = BANDS + n
             picks = [part_ref[i, n] & 1 for i in range(2)]
             k_terms = [dot(grads[slot][rows(i)], qn[rows(i)], TN) * scale for i in range(2)]
             v_terms = [dot(weights[slot][rows(i)], ct[rows(i)], TN) for i in range(2)]
@@ -216,9 +236,10 @@
 
 V = pl.BlockSpec(memory_space=pltpu.VMEM)
 S = pl.BlockSpec(memory_space=pltpu.SMEM)
-
-
-def call(kernel, specs, outs, flops, *args):
+H = pl.BlockSpec(memory_space=pltpu.HBM)
+
+
+def call(kernel, specs, outs, flops, *args, scratch=()):
     shapes = [jax.ShapeDtypeStruct(s, t) for s, t in outs]
     moved = sum(a.size * a.dtype.itemsize for a in args)
     moved += sum(s.size * s.dtype.itemsize for s in shapes)
@@ -227,6 +248,7 @@
         out_shape=shapes,
         in_specs=specs,
         out_specs=[V] * len(shapes),
+        scratch_shapes=scratch,
         compiler_params=pltpu.CompilerParams(vmem_limit_bytes=24 * 2**20),
         cost_estimate=pl.CostEstimate(flops=flops, transcendentals=0, bytes_accessed=moved),
     )(*args)
@@ -245,7 +267,14 @@
 
     pack_t = ((2, 256, 256), BF16)
 
-    (pack,) = call(prep_kernel, [V, V, V], [pack_t], 10**6, key_raw, values, gain_key)
+    (pack,) = call(
+        prep_kernel, [H, H, H], [pack_t], 10**6,
+        *[pltpu.with_memory_space_constraint(a, pltpu.HBM) for a in (key_raw, values, gain_key)],
+        scratch=[
+            pltpu.VMEM((256, 256), BF16), pltpu.VMEM((HEADS, 128), F32),
+            pltpu.SemaphoreType.DMA((3,)),
+        ],
+    )
     y2 = send(pack, across[2])
     y1 = send(pack, across[3])
     x2 = send(pack, across[0])
@@ -253,32 +282,33 @@
     left = send(pack, ups)
     right = send(pack, downs)
 
-    tiles = ((HEADS, SLOTS, 256, 128), BF16)
+    tiles = ((HEADS, BANDS, 256, 128), BF16)
+    x_tiles = ((HEADS, 2, 256, 128), BF16)
     rowstat = ((HEADS, 256, 128), F32)
     full = ((256, 256), F32)
     qn, e, d, o_part, l_part = call(
         functools.partial(local_kernel, last_block=2 * count - 1),
-        [S, S, S] + [V] * 8,
+        [S, S, S] + [V] * 6,
         [((256, 256), BF16), tiles, tiles, full, rowstat],
-        28 * 3 * 2 * 128**3,
-        device, band_reach, partners, query_raw, gain_query, cotangent, pack, left, right, x2, x1,
-    )
-    gy2, gy1, out, rl, delta, dqy = call(
+        20 * 3 * 2 * 128**3,
+        device, band_reach, partners, query_raw, gain_query, cotangent, pack, left, right,
+    )
+    gy2, gy1, out, rl, delta, dqy, ex, dx = call(
         far_kernel,
-        [S] + [V] * 6,
-        [pack_t, pack_t, ((256, 256), BF16), rowstat, rowstat, full],
-        8 * 6 * 2 * 128**3,
-        partners, qn, cotangent, y2, y1, o_part, l_part,
+        [S] + [V] * 8,
+        [pack_t, pack_t, ((256, 256), BF16), rowstat, rowstat, full, x_tiles, x_tiles],
+        8 * 9 * 2 * 128**3,
+        partners, qn, cotangent, x2, x1, y2, y1, o_part, l_part,
     )
     ry2 = send(gy2, across[2])
     ry1 = send(gy1, across[3])
     gx2, gx1, gl, gr, gown, grad_query = call(
         near_kernel,
-        [S] + [V] * 14,
+        [S] + [V] * 16,
         [pack_t, pack_t, pack_t, pack_t, ((2, 256, 256), F32), ((256, 256), BF16)],
         28 * 3 * 2 * 128**3,
         partners, query_raw, gain_query, qn, cotangent, pack, left, right, x2, x1, e, d,
-        rl, delta, dqy,
+        ex, dx, rl, delta, dqy,
     )
     rx2 = send(gx2, across[0])
     rx1 = send(gx1, across[1])

time: 97.4 us -> 90.5 us (0.929)
  the two profiles are of different devices: /device:TPU:1 before, /device:TPU:2 now
where the time goes in v2:
time: 90.5 us; the launch traced here: 90.1 us
  starting transfers between devices  61.4 us (68%)
  waiting for transfers between devices  18.3 us (20%)
  Pallas kernels  8.84 us (10%)
    ppermute x12, starting transfers between devices, send(): return lax.ppermute(value, AXES, perm)  61.4 us
    ppermute x12, waiting for transfers between devices, send(): return lax.ppermute(value, AXES, perm)  18.3 us
    pallas_call x5, Pallas kernels, call(): pl.pallas_call(kernel, out_shape=shapes, in_specs=specs, out_specs=[V] *...  8.84 us
  transfers between devices with their start and end apart: 12, of which 4 were waited for; matrix products, arithmetic and copies ran while one was open for 0% of the time, Pallas kernels for 2%

profile of v2, /device:TPU:2, one launch (start us, length us, event | category | flops | bytes accessed | tf_op | source)
XLA Modules:
  0.0 90.1 jit_solution(7699310999441032688)
XLA Ops:
  0.7 1.2 %shard_map.111.own = bf16[2,256,256]{2,1,0:T(8,128)(2,1)S(1)} custom-call(bf16[256,256]{1,0:T(8,128)(2,1)} %k_ref.1, bf16[256,256]{1,0:T(8,128)(2,1)} %v_hbm.1, f32[2,128]{1,0:T(2,128)} %gain_ref.5), custom_call_target="tpu_custom_call" | custom-call | flops 1000000 | bytes 525312 | tf_op jit(solution)/shard_map/pallas_call | solution.py:246
  1.9 13.3 %collective-permute-start.1 = (bf16[2,256,256]{2,1,0:T(8,128)(2,1)S(1)}, bf16[2,256,256]{2,1,0:T(8,128)(2,1)S(1)}, u32[]{:S(2)}, u32[]{:S(2)}) collective-permute-start(bf16[2,256,256]{2,1,0:T(8,128)(2,1)S(1)} %shard_map.111.own), channel_id=1, source_target_pairs={{1,0},{2,1},{3,2},{4,3},{5,4},{6,5},{7,6},{8,7},{9,8},{10,9},{11,1... | collective-permute-start | bytes 786440 | tf_op jit(solution)/shard_map/ppermute | solution.py:266
  15.1 1.9 %collective-permute-start = (bf16[2,256,256]{2,1,0:T(8,128)(2,1)S(1)}, bf16[2,256,256]{2,1,0:T(8,128)(2,1)S(1)}, u32[]{:S(2)}, u32[]{:S(2)}) collective-permute-start(bf16[2,256,256]{2,1,0:T(8,128)(2,1)S(1)} %shard_map.111.own), channel_id=1, source_target_pairs={{0,1},{1,2},{2,3},{3,4},{4,5},{5,6},{6,7},{7,8},{8,9},{9,10},{10,1... | collective-permute-start | bytes 786440 | tf_op jit(solution)/shard_map/ppermute | solution.py:266
  17.1 1.9 %collective-permute-start.5 = (bf16[2,256,256]{2,1,0:T(8,128)(2,1)S(1)}, bf16[2,256,256]{2,1,0:T(8,128)(2,1)S(1)}, u32[]{:S(2)}, u32[]{:S(2)}) collective-permute-start(bf16[2,256,256]{2,1,0:T(8,128)(2,1)S(1)} %shard_map.111.own), channel_id=1, source_target_pairs={{0,32},{1,33},{2,34},{3,35},{4,36},{5,37},{6,38},{7,39},{8,40},{9,... | collective-permute-start | bytes 786440 | tf_op jit(solution)/shard_map/ppermute | solution.py:266
  19.0 6.4 %collective-permute-start.4 = (bf16[2,256,256]{2,1,0:T(8,128)(2,1)S(1)}, bf16[2,256,256]{2,1,0:T(8,128)(2,1)S(1)}, u32[]{:S(2)}, u32[]{:S(2)}) collective-permute-start(bf16[2,256,256]{2,1,0:T(8,128)(2,1)S(1)} %shard_map.111.own), channel_id=1, source_target_pairs={{0,64},{1,65},{2,66},{3,67},{4,68},{5,69},{6,70},{7,71},{8,72},{9,... | collective-permute-start | bytes 786440 | tf_op jit(solution)/shard_map/ppermute | solution.py:266
  25.4 2.4 %collective-permute-start.3 = (bf16[2,256,256]{2,1,0:T(8,128)(2,1)S(1)}, bf16[2,256,256]{2,1,0:T(8,128)(2,1)S(1)}, u32[]{:S(2)}, u32[]{:S(2)}) collective-permute-start(bf16[2,256,256]{2,1,0:T(8,128)(2,1)S(1)} %shard_map.111.own), channel_id=1, source_target_pairs={{0,128},{1,129},{2,130},{3,131},{4,132},{5,133},{6,134},{7,135},{8... | collective-permute-start | bytes 786440 | tf_op jit(solution)/shard_map/ppermute | solution.py:266
  27.9 4.3 %collective-permute-start.2 = (bf16[2,256,256]{2,1,0:T(8,128)(2,1)S(1)}, bf16[2,256,256]{2,1,0:T(8,128)(2,1)S(1)}, u32[]{:S(2)}, u32[]{:S(2)}) collective-permute-start(bf16[2,256,256]{2,1,0:T(8,128)(2,1)S(1)} %shard_map.111.own), channel_id=1, source_target_pairs={{0,256},{1,257},{2,258},{3,259},{4,260},{5,261},{6,262},{7,263},{8... | collective-permute-start | bytes 786440 | tf_op jit(solution)/shard_map/ppermute | solution.py:266
  32.2 0.0 copy-start.5
  32.3 0.6 copy-done.5
  32.9 0.0 copy-done.3
  32.9 1.6 %shard_map.112 = (bf16[256,256]{1,0:T(8,128)(2,1)S(1)}, bf16[2,5,256,128]{3,2,1,0:T(8,128)(2,1)S(1)}, bf16[2,5,256,128]{3,2,1,0:T(8,128)(2,1)S(1)}, f32[256,256]{1,0:T(8,128)S(1)}, f32[2,256,128]{2,1,0:T(8,128)S(1)}) custom-call(s32[1]{0:T(128)} %bitcast.dev_ref, s32[2]{0:T(128)S(1)} %copy-done.6, s32[2,4]{1,0:T(2,128)S(1)} %copy-done.3, ...), custom_call_target="tpu_custom_call" | custom-call | flops 251658240 | bytes 3015724 | tf_op jit(solution)/shard_map/pallas_call | solution.py:246
  34.5 4.3 %collective-permute-done.5.y1 = bf16[2,256,256]{2,1,0:T(8,128)(2,1)S(1)} collective-permute-done((bf16[2,256,256]{2,1,0:T(8,128)(2,1)S(1)}, bf16[2,256,256]{2,1,0:T(8,128)(2,1)S(1)}, u32[]{:S(2)}, u32[]{:S(2)}) %collective-permute-start.5) | collective-permute-done | bytes 262176 | tf_op jit(solution)/shard_map/ppermute | solution.py:266
  38.9 2.3 %shard_map.113 = (bf16[2,256,256]{2,1,0:T(8,128)(2,1)S(1)}, bf16[2,256,256]{2,1,0:T(8,128)(2,1)S(1)}, bf16[256,256]{1,0:T(8,128)(2,1)}, f32[2,256,128]{2,1,0:T(8...) custom-call(s32[2,4]{1,0:T(2,128)S(1)} %copy-done.3, ...), custom_call_target="tpu_custom_call" | custom-call | flops 301989888 | bytes 3801120 | tf_op jit(solution)/shard_map/pallas_call | solution.py:246
  41.2 2.5 %shard_map.114 = (bf16[2,256,256]{2,1,0:T(8,128)(2,1)S(1)}, bf16[2,256,256]{2,1,0:T(8,128)(2,1)S(1)}, bf16[2,256,256]{2,1,0:T(8,128)(2,1)S(1)}, bf16[2,256,256]{...) custom-call(s32[2,4]{1,0:T(2,128)S(1)} %copy-done.3, bf16[256,256]{1,0:T(8,128)(2,1)S(1)} %copy-done.1, ...), custom_call_target="tpu_custom_call" | custom-call | flops 352321536 | bytes 6030368 | tf_op jit(solution)/shard_map/pallas_call | solution.py:246
  43.7 4.0 %collective-permute-start.8 = (bf16[2,256,256]{2,1,0:T(8,128)(2,1)S(1)}, bf16[2,256,256]{2,1,0:T(8,128)(2,1)S(1)}, u32[]{:S(2)}, u32[]{:S(2)}) collective-permute-start(bf16[2,256,256]{2,1,0:T(8,128)(2,1)S(1)} %get-tuple-element.40), channel_id=1, source_target_pairs={{0,256},{1,257},{2,258},{3,259},{4,260},{5,261},{6,262},{7,263},{8... | collective-permute-start | bytes 786440 | tf_op jit(solution)/shard_map/ppermute | solution.py:266
  47.7 3.3 %collective-permute-start.9 = (bf16[2,256,256]{2,1,0:T(8,128)(2,1)S(1)}, bf16[2,256,256]{2,1,0:T(8,128)(2,1)S(1)}, u32[]{:S(2)}, u32[]{:S(2)}) collective-permute-start(bf16[2,256,256]{2,1,0:T(8,128)(2,1)S(1)} %get-tuple-element.41), channel_id=1, source_target_pairs={{0,128},{1,129},{2,130},{3,131},{4,132},{5,133},{6,134},{7,135},{8... | collective-permute-start | bytes 786440 | tf_op jit(solution)/shard_map/ppermute | solution.py:266
  51.1 1.9 %collective-permute-start.10 = (bf16[2,256,256]{2,1,0:T(8,128)(2,1)S(1)}, bf16[2,256,256]{2,1,0:T(8,128)(2,1)S(1)}, u32[]{:S(2)}, u32[]{:S(2)}) collective-permute-start(bf16[2,256,256]{2,1,0:T(8,128)(2,1)S(1)} %get-tuple-element.42), channel_id=1, source_target_pairs={{0,1},{1,2},{2,3},{3,4},{4,5},{5,6},{6,7},{7,8},{8,9},{9,10},{10,1... | collective-permute-start | bytes 786440 | tf_op jit(solution)/shard_map/ppermute | solution.py:266
  53.0 11.5 %collective-permute-start.11 = (bf16[2,256,256]{2,1,0:T(8,128)(2,1)S(1)}, bf16[2,256,256]{2,1,0:T(8,128)(2,1)S(1)}, u32[]{:S(2)}, u32[]{:S(2)}) collective-permute-start(bf16[2,256,256]{2,1,0:T(8,128)(2,1)S(1)} %get-tuple-element.43), channel_id=1, source_target_pairs={{1,0},{2,1},{3,2},{4,3},{5,4},{6,5},{7,6},{8,7},{9,8},{10,9},{11,1... | collective-permute-start | bytes 786440 | tf_op jit(solution)/shard_map/ppermute | solution.py:266
  64.5 3.2 %collective-permute-start.6 = (bf16[2,256,256]{2,1,0:T(8,128)(2,1)S(1)}, bf16[2,256,256]{2,1,0:T(8,128)(2,1)S(1)}, u32[]{:S(2)}, u32[]{:S(2)}) collective-permute-start(bf16[2,256,256]{2,1,0:T(8,128)(2,1)S(1)} %get-tuple-element.38), channel_id=1, source_target_pairs={{0,64},{1,65},{2,66},{3,67},{4,68},{5,69},{6,70},{7,71},{8,72},{9,... | collective-permute-start | bytes 786440 | tf_op jit(solution)/shard_map/ppermute | solution.py:266
  67.7 7.2 %collective-permute-start.7 = (bf16[2,256,256]{2,1,0:T(8,128)(2,1)S(1)}, bf16[2,256,256]{2,1,0:T(8,128)(2,1)S(1)}, u32[]{:S(2)}, u32[]{:S(2)}) collective-permute-start(bf16[2,256,256]{2,1,0:T(8,128)(2,1)S(1)} %get-tuple-element.39), channel_id=1, source_target_pairs={{0,32},{1,33},{2,34},{3,35},{4,36},{5,37},{6,38},{7,39},{8,40},{9,... | collective-permute-start | bytes 786440 | tf_op jit(solution)/shard_map/ppermute | solution.py:266
  74.9 1.5 %collective-permute-done.10.e = bf16[2,256,256]{2,1,0:T(8,128)(2,1)S(1)} collective-permute-done((bf16[2,256,256]{2,1,0:T(8,128)(2,1)S(1)}, bf16[2,256,256]{2,1,0:T(8,128)(2,1)S(1)}, u32[]{:S(2)}, u32[]{:S(2)}) %collective-permute-start.10) | collective-permute-done | bytes 262176 | tf_op jit(solution)/shard_map/ppermute | solution.py:266
  76.4 8.2 %collective-permute-done.6.a = bf16[2,256,256]{2,1,0:T(8,128)(2,1)S(1)} collective-permute-done((bf16[2,256,256]{2,1,0:T(8,128)(2,1)S(1)}, bf16[2,256,256]{2,1,0:T(8,128)(2,1)S(1)}, u32[]{:S(2)}, u32[]{:S(2)}) %collective-permute-start.6) | collective-permute-done | bytes 262176 | tf_op jit(solution)/shard_map/ppermute | solution.py:266
  84.6 4.3 %collective-permute-done.7.b = bf16[2,256,256]{2,1,0:T(8,128)(2,1)S(1)} collective-permute-done((bf16[2,256,256]{2,1,0:T(8,128)(2,1)S(1)}, bf16[2,256,256]{2,1,0:T(8,128)(2,1)S(1)}, u32[]{:S(2)}, u32[]{:S(2)}) %collective-permute-start.7) | collective-permute-done | bytes 262176 | tf_op jit(solution)/shard_map/ppermute | solution.py:266
  88.9 1.2 %shard_map.115 = (bf16[256,256]{1,0:T(8,128)(2,1)}, bf16[256,256]{1,0:T(8,128)(2,1)}) custom-call(bf16[256,256]{1,0:T(8,128)(2,1)S(1)} %copy-done.2, f32[2,128]{1,0:T(2,128)S(1)} %copy-done.4, f32[2,256,256]{2,1,0:T(8,128)S(1)} %get-tuple-element.37.own, bf16[2,256,256]{2,1,0:T(8,128)(2,1)S(1)} %collective-permute-done.6.a, ...), custom_call_target="tpu_custom_call" | custom-call | flops 1000000 | bytes 2491392 | tf_op jit(solution)/shard_map/pallas_call | solution.py:246
  (19 shorter events, 0.1 us)
Async XLA Ops:
  0.6 31.6 %copy-start = (bf16[256,256]{1,0:T(8,128)(2,1)S(1)}, bf16[256,256]{1,0:T(8,128)(2,1)}, u32[]{:S(2)}) copy-start(bf16[256,256]{1,0:T(8,128)(2,1)} %cot_ref.5) | copy-start | bytes 393220
  0.6 31.6 %copy-start.1 = (bf16[256,256]{1,0:T(8,128)(2,1)S(1)}, bf16[256,256]{1,0:T(8,128)(2,1)}, u32[]{:S(2)}) copy-start(bf16[256,256]{1,0:T(8,128)(2,1)} %q_ref.3) | copy-start | bytes 393220
  1.9 26.0 %collective-permute-start.1 = (bf16[2,256,256]{2,1,0:T(8,128)(2,1)S(1)}, bf16[2,256,256]{2,1,0:T(8,128)(2,1)S(1)}, u32[]{:S(2)}, u32[]{:S(2)}) collective-permute-start(bf16[2,256,256]{2,1,0:T(8,128)(2,1)S(1)} %shard_map.111.own), channel_id=1, source_target_pairs={{1,0},{2,1},{3,2},{4,3},{5,4},{6,5},{7,6},{8,7},{9,8},{10,9},{11,1... | collective-permute-start | bytes 786440 | tf_op jit(solution)/shard_map/ppermute | solution.py:266
  15.1 17.1 %collective-permute-start = (bf16[2,256,256]{2,1,0:T(8,128)(2,1)S(1)}, bf16[2,256,256]{2,1,0:T(8,128)(2,1)S(1)}, u32[]{:S(2)}, u32[]{:S(2)}) collective-permute-start(bf16[2,256,256]{2,1,0:T(8,128)(2,1)S(1)} %shard_map.111.own), channel_id=1, source_target_pairs={{0,1},{1,2},{2,3},{3,4},{4,5},{5,6},{6,7},{7,8},{8,9},{9,10},{10,1... | collective-permute-start | bytes 786440 | tf_op jit(solution)/shard_map/ppermute | solution.py:266
  17.1 21.8 %collective-permute-start.5 = (bf16[2,256,256]{2,1,0:T(8,128)(2,1)S(1)}, bf16[2,256,256]{2,1,0:T(8,128)(2,1)S(1)}, u32[]{:S(2)}, u32[]{:S(2)}) collective-permute-start(bf16[2,256,256]{2,1,0:T(8,128)(2,1)S(1)} %shard_map.111.own), channel_id=1, source_target_pairs={{0,32},{1,33},{2,34},{3,35},{4,36},{5,37},{6,38},{7,39},{8,40},{9,... | collective-permute-start | bytes 786440 | tf_op jit(solution)/shard_map/ppermute | solution.py:266
  19.0 19.9 %collective-permute-start.4 = (bf16[2,256,256]{2,1,0:T(8,128)(2,1)S(1)}, bf16[2,256,256]{2,1,0:T(8,128)(2,1)S(1)}, u32[]{:S(2)}, u32[]{:S(2)}) collective-permute-start(bf16[2,256,256]{2,1,0:T(8,128)(2,1)S(1)} %shard_map.111.own), channel_id=1, source_target_pairs={{0,64},{1,65},{2,66},{3,67},{4,68},{5,69},{6,70},{7,71},{8,72},{9,... | collective-permute-start | bytes 786440 | tf_op jit(solution)/shard_map/ppermute | solution.py:266
  25.4 13.4 %collective-permute-start.3 = (bf16[2,256,256]{2,1,0:T(8,128)(2,1)S(1)}, bf16[2,256,256]{2,1,0:T(8,128)(2,1)S(1)}, u32[]{:S(2)}, u32[]{:S(2)}) collective-permute-start(bf16[2,256,256]{2,1,0:T(8,128)(2,1)S(1)} %shard_map.111.own), channel_id=1, source_target_pairs={{0,128},{1,129},{2,130},{3,131},{4,132},{5,133},{6,134},{7,135},{8... | collective-permute-start | bytes 786440 | tf_op jit(solution)/shard_map/ppermute | solution.py:266
  27.9 11.0 %collective-permute-start.2 = (bf16[2,256,256]{2,1,0:T(8,128)(2,1)S(1)}, bf16[2,256,256]{2,1,0:T(8,128)(2,1)S(1)}, u32[]{:S(2)}, u32[]{:S(2)}) collective-permute-start(bf16[2,256,256]{2,1,0:T(8,128)(2,1)S(1)} %shard_map.111.own), channel_id=1, source_target_pairs={{0,256},{1,257},{2,258},{3,259},{4,260},{5,261},{6,262},{7,263},{8... | collective-permute-start | bytes 786440 | tf_op jit(solution)/shard_map/ppermute | solution.py:266
  32.2 0.7 copy-start.5
  32.2 0.7 copy-start.3
  32.3 0.7 copy-start.6
  41.2 47.7 %copy-start.2 = (bf16[256,256]{1,0:T(8,128)(2,1)S(1)}, bf16[256,256]{1,0:T(8,128)(2,1)}, u32[]{:S(2)}) copy-start(bf16[256,256]{1,0:T(8,128)(2,1)} %k_ref.1) | copy-start | bytes 393220
  43.7 24.0 %collective-permute-start.8 = (bf16[2,256,256]{2,1,0:T(8,128)(2,1)S(1)}, bf16[2,256,256]{2,1,0:T(8,128)(2,1)S(1)}, u32[]{:S(2)}, u32[]{:S(2)}) collective-permute-start(bf16[2,256,256]{2,1,0:T(8,128)(2,1)S(1)} %get-tuple-element.40), channel_id=1, source_target_pairs={{0,256},{1,257},{2,258},{3,259},{4,260},{5,261},{6,262},{7,263},{8... | collective-permute-start | bytes 786440 | tf_op jit(solution)/shard_map/ppermute | solution.py:266
  47.7 27.2 %collective-permute-start.9 = (bf16[2,256,256]{2,1,0:T(8,128)(2,1)S(1)}, bf16[2,256,256]{2,1,0:T(8,128)(2,1)S(1)}, u32[]{:S(2)}, u32[]{:S(2)}) collective-permute-start(bf16[2,256,256]{2,1,0:T(8,128)(2,1)S(1)} %get-tuple-element.41), channel_id=1, source_target_pairs={{0,128},{1,129},{2,130},{3,131},{4,132},{5,133},{6,134},{7,135},{8... | collective-permute-start | bytes 786440 | tf_op jit(solution)/shard_map/ppermute | solution.py:266
  51.1 25.3 %collective-permute-start.10 = (bf16[2,256,256]{2,1,0:T(8,128)(2,1)S(1)}, bf16[2,256,256]{2,1,0:T(8,128)(2,1)S(1)}, u32[]{:S(2)}, u32[]{:S(2)}) collective-permute-start(bf16[2,256,256]{2,1,0:T(8,128)(2,1)S(1)} %get-tuple-element.42), channel_id=1, source_target_pairs={{0,1},{1,2},{2,3},{3,4},{4,5},{5,6},{6,7},{7,8},{8,9},{9,10},{10,1... | collective-permute-start | bytes 786440 | tf_op jit(solution)/shard_map/ppermute | solution.py:266
  53.0 23.4 %collective-permute-start.11 = (bf16[2,256,256]{2,1,0:T(8,128)(2,1)S(1)}, bf16[2,256,256]{2,1,0:T(8,128)(2,1)S(1)}, u32[]{:S(2)}, u32[]{:S(2)}) collective-permute-start(bf16[2,256,256]{2,1,0:T(8,128)(2,1)S(1)} %get-tuple-element.43), channel_id=1, source_target_pairs={{1,0},{2,1},{3,2},{4,3},{5,4},{6,5},{7,6},{8,7},{9,8},{10,9},{11,1... | collective-permute-start | bytes 786440 | tf_op jit(solution)/shard_map/ppermute | solution.py:266
  64.5 20.1 %collective-permute-start.6 = (bf16[2,256,256]{2,1,0:T(8,128)(2,1)S(1)}, bf16[2,256,256]{2,1,0:T(8,128)(2,1)S(1)}, u32[]{:S(2)}, u32[]{:S(2)}) collective-permute-start(bf16[2,256,256]{2,1,0:T(8,128)(2,1)S(1)} %get-tuple-element.38), channel_id=1, source_target_pairs={{0,64},{1,65},{2,66},{3,67},{4,68},{5,69},{6,70},{7,71},{8,72},{9,... | collective-permute-start | bytes 786440 | tf_op jit(solution)/shard_map/ppermute | solution.py:266
  67.7 21.2 %copy-start.4 = (f32[2,128]{1,0:T(2,128)S(1)}, f32[2,128]{1,0:T(2,128)}, u32[]{:S(2)}) copy-start(f32[2,128]{1,0:T(2,128)} %gain_ref.5) | copy-start | bytes 3076
  67.7 21.1 %collective-permute-start.7 = (bf16[2,256,256]{2,1,0:T(8,128)(2,1)S(1)}, bf16[2,256,256]{2,1,0:T(8,128)(2,1)S(1)}, u32[]{:S(2)}, u32[]{:S(2)}) collective-permute-start(bf16[2,256,256]{2,1,0:T(8,128)(2,1)S(1)} %get-tuple-element.39), channel_id=1, source_target_pairs={{0,32},{1,33},{2,34},{3,35},{4,36},{5,37},{6,38},{7,39},{8,40},{9,... | collective-permute-start | bytes 786440 | tf_op jit(solution)/shard_map/ppermute | solution.py:266

commit v3 on v2

--- a/solution.py
+++ b/solution.py
@@ -10,9 +10,7 @@
 
 HEADS = 2
 BLOCK = 128
-BAND = 2
 LEVELS = 4
-BANDS = 2 * BAND + 1
 AXES = ("grp", "ctx")
 EPS = 1e-05
 F32 = jnp.float32
@@ -71,47 +69,49 @@
 
 
 def local_kernel(
-    dev_ref, reach_ref, part_ref, q_ref, gain_ref, cot_ref, own, left, right,
+    dev_ref, reach_ref, part_ref, q_ref, gain_ref, cot_ref, own, mate, beside,
     qn_ref, e_ref, d_ref, o_ref, l_ref, *, last_block,
 ):
     scale = 128 ** (-0.5)
-    near = (left, own, right)
+    near = (own, mate, beside)
     both = range(HEADS)
+    step = 1 - 2 * (dev_ref[0] & 1)
+    shifts = (0, 2 * step, -2 * step)
     qn = [norm(q_ref[:, cols(h)], gain_ref[h : h + 1, :])[2].astype(BF16) for h in both]
     ct = [cot_ref[:, cols(h)] for h in both]
     for h in both:
         qn_ref[:, cols(h)] = qn[h]
     s_near = [[dot(qn[h], r[0, :, cols(h)], NT) for r in near] for h in both]
     for h in both:
-        d_near = [dot(ct[h], r[1, :, cols(h)], NT) for r in near]
-        for i in range(2):
-            for slot in range(BANDS):
-                c = i + slot
-                d_ref[h, slot, rows(i), :] = d_near[c // 2][rows(i), rows(c % 2)].astype(BF16)
+        for n, r in enumerate(near):
+            d_ref[h, n] = dot(ct[h], r[1, :, cols(h)], NT).astype(BF16)
+    keep = {}
+    for i in range(2):
+        block = dev_ref[0] * 2 + i
+        for n in range(3):
+            for g in range(2):
+                off = shifts[n] + (g - i)
+                goal = block + off
+                ok = (jnp.abs(off) <= reach_ref[i]) & (goal >= 0) & (goal <= last_block)
+                keep[i, n, g] = jnp.where(ok, 1.0, 0.0).astype(F32)
     for h in both:
         for i in range(2):
-            block = dev_ref[0] * 2 + i
             total = None
-            e_list = []
-            for slot in range(BANDS):
-                c = i + slot
-                e = jnp.exp(s_near[h][c // 2][rows(i), rows(c % 2)] * scale)
-                if slot != BAND:
-                    off = slot - BAND
-                    goal = block + off
-                    ok = (abs(off) <= reach_ref[i]) & (goal >= 0) & (goal <= last_block)
-                    e = e * jnp.where(ok, 1.0, 0.0).astype(F32)
-                total = e if total is None else total + e
-                low = e.astype(BF16)
-                e_list.append(low)
-                e_ref[h, slot, rows(i), :] = low
+            for n in range(3):
+                for g in range(2):
+                    e = jnp.exp(s_near[h][n][rows(i), rows(g)] * scale)
+                    if n or g != i:
+                        e = e * keep[i, n, g]
+                    total = e if total is None else total + e
+                    e_ref[h, n, rows(i), rows(g)] = e.astype(BF16)
             l_ref[h, rows(i), :] = jnp.broadcast_to(
                 jnp.sum(total, axis=-1, keepdims=True), (BLOCK, 128)
             )
-            v_list = [near[(i + s) // 2][1, rows((i + s) % 2), cols(h)] for s in range(BANDS)]
-            o_ref[rows(i), cols(h)] = dot(
-                jnp.concatenate(e_list, axis=1), jnp.concatenate(v_list, axis=0), NN
-            )
+        o_ref[:, cols(h)] = dot(
+            jnp.concatenate([e_ref[h, n] for n in range(3)], axis=1),
+            jnp.concatenate([r[1, :, cols(h)] for r in near], axis=0),
+            NN,
+        )
 
 
 def spread(terms, picks, g):
@@ -172,50 +172,52 @@
 
 
 def near_kernel(
-    part_ref, q_ref, gain_ref, qn_ref, cot_ref, own, left, right, x2, x1, e_ref, d_ref,
+    part_ref, q_ref, gain_ref, qn_ref, cot_ref, own, mate, beside, x2, x1, e_ref, d_ref,
     ex_ref, dx_ref, rl_ref, delta_ref, dqy_ref,
-    gx2_ref, gx1_ref, gl_ref, gr_ref, gown_ref, gq_ref,
+    gx2_ref, gx1_ref, gm_ref, gb_ref, gown_ref, gq_ref,
 ):
     scale = 128 ** (-0.5)
-    near = (left, own, right)
+    near = (own, mate, beside)
+    pick = [[part_ref[i, n] & 1 for n in range(2)] for i in range(2)]
     for h in range(HEADS):
         qn = qn_ref[:, cols(h)]
         ct = cot_ref[:, cols(h)]
-        weights, grads = [], []
-        tiles = [(e_ref[h, s], d_ref[h, s]) for s in range(BANDS)]
-        tiles += [(ex_ref[h, s], dx_ref[h, s]) for s in range(2)]
-        for e, d in tiles:
-            p = e.astype(F32) * rl_ref[h]
-            weights.append(p.astype(BF16))
-            grads.append((p * (d.astype(F32) - delta_ref[h])).astype(BF16))
-        for n, (src, ref) in enumerate(((x2, gx2_ref), (x1, gx1_ref))):
-            slot = BANDS + n
-            picks = [part_ref[i, n] & 1 for i in range(2)]
-            k_terms = [dot(grads[slot][rows(i)], qn[rows(i)], TN) * scale for i in range(2)]
-            v_terms = [dot(weights[slot][rows(i)], ct[rows(i)], TN) for i in range(2)]
+        rl = rl_ref[h]
+        delta = delta_ref[h]
+        x_grads = []
+        for n, ref in enumerate((gx2_ref, gx1_ref)):
+            p = ex_ref[h, n].astype(F32) * rl
+            w = p.astype(BF16)
+            ds = (p * (dx_ref[h, n].astype(F32) - delta)).astype(BF16)
+            x_grads.append(ds)
+            picks = [pick[i][n] for i in range(2)]
+            k_terms = [dot(ds[rows(i)], qn[rows(i)], TN) * scale for i in range(2)]
+            v_terms = [dot(w[rows(i)], ct[rows(i)], TN) for i in range(2)]
             for g in range(2):
                 ref[0, rows(g), cols(h)] = spread(k_terms, picks, g)
                 ref[1, rows(g), cols(h)] = spread(v_terms, picks, g)
-        for c in range(6):
-            picked_rows = [i for i in range(2) if 0 <= c - i < 5]
-            span = slice(picked_rows[0] * BLOCK, (picked_rows[-1] + 1) * BLOCK)
-            ds = jnp.concatenate([grads[c - i][rows(i)] for i in picked_rows], axis=0)
-            w = jnp.concatenate([weights[c - i][rows(i)] for i in picked_rows], axis=0)
-            dk = dot(ds, qn[span], TN) * scale
-            dv = dot(w, ct[span], TN)
-            ref = (gl_ref, gown_ref, gr_ref)[c // 2]
-            ref[0, rows(c % 2), cols(h)] = dk.astype(ref.dtype)
-            ref[1, rows(c % 2), cols(h)] = dv.astype(ref.dtype)
+        rl2 = jnp.concatenate((rl, rl), axis=1)
+        delta2 = jnp.concatenate((delta, delta), axis=1)
+        grads = []
+        for n, ref in enumerate((gown_ref, gm_ref, gb_ref)):
+            p = e_ref[h, n].astype(F32) * rl2
+            ds = (p * (d_ref[h, n].astype(F32) - delta2)).astype(BF16)
+            grads.append(ds)
+            ref[0, :, cols(h)] = (dot(ds, qn, TN) * scale).astype(ref.dtype)
+            ref[1, :, cols(h)] = dot(p.astype(BF16), ct, TN).astype(ref.dtype)
         normed, inverse, _ = norm(q_ref[:, cols(h)], gain_ref[h : h + 1, :])
+        band = dot(
+            jnp.concatenate(grads, axis=1),
+            jnp.concatenate([r[0, :, cols(h)] for r in near], axis=0),
+            NN,
+        )
         for i in range(2):
-            k_list = [near[(i + s) // 2][0, rows((i + s) % 2), cols(h)] for s in range(5)]
-            k_list += [picked(r, 0, part_ref[i, n] & 1, h) for n, r in enumerate((x2, x1))]
             dq = dot(
-                jnp.concatenate([g[rows(i)] for g in grads], axis=1),
-                jnp.concatenate(k_list, axis=0),
+                jnp.concatenate([g[rows(i)] for g in x_grads], axis=1),
+                jnp.concatenate([picked(r, 0, p, h) for r, p in zip((x2, x1), pick[i])], axis=0),
                 NN,
             )
-            dq = (dq + dqy_ref[rows(i), cols(h)]) * scale
+            dq = (dq + band[rows(i)] + dqy_ref[rows(i), cols(h)]) * scale
             gq_ref[rows(i), cols(h)] = norm_back(
                 dq, normed[rows(i)], inverse[rows(i)], gain_ref[h : h + 1, :]
             ).astype(BF16)
@@ -257,8 +259,8 @@
 def body(query_raw, key_raw, values, band_reach, partners, gain_query, gain_key, cotangent):
     count = lax.axis_size(AXES)
     device = lax.axis_index(AXES).astype(jnp.int32).reshape(1)
-    ups = [(i, i + 1) for i in range(count - 1)]
-    downs = [(b, a) for a, b in ups]
+    mates = [(i, i ^ 1) for i in range(count)]
+    besides = [(i, j) for a in range(1, count - 1, 2) for i, j in ((a, a + 1), (a + 1, a))]
     masks = [count >> (level + 1) for level in range(LEVELS)]
     across = [[(i, i ^ m) for i in range(count)] for m in masks]
 
@@ -279,10 +281,10 @@
     y1 = send(pack, across[3])
     x2 = send(pack, across[0])
     x1 = send(pack, across[1])
-    left = send(pack, ups)
-    right = send(pack, downs)
-
-    tiles = ((HEADS, BANDS, 256, 128), BF16)
+    mate = send(pack, mates)
+    beside = send(pack, besides)
+
+    tiles = ((HEADS, 3, 256, 256), BF16)
     x_tiles = ((HEADS, 2, 256, 128), BF16)
     rowstat = ((HEADS, 256, 128), F32)
     full = ((256, 256), F32)
@@ -291,7 +293,7 @@
         [S, S, S] + [V] * 6,
         [((256, 256), BF16), tiles, tiles, full, rowstat],
         20 * 3 * 2 * 128**3,
-        device, band_reach, partners, query_raw, gain_query, cotangent, pack, left, right,
+        device, band_reach, partners, query_raw, gain_query, cotangent, pack, mate, beside,
     )
     gy2, gy1, out, rl, delta, dqy, ex, dx = call(
         far_kernel,
@@ -302,24 +304,24 @@
     )
     ry2 = send(gy2, across[2])
     ry1 = send(gy1, across[3])
-    gx2, gx1, gl, gr, gown, grad_query = call(
+    gx2, gx1, gm, gb, gown, grad_query = call(
         near_kernel,
         [S] + [V] * 16,
         [pack_t, pack_t, pack_t, pack_t, ((2, 256, 256), F32), ((256, 256), BF16)],
         28 * 3 * 2 * 128**3,
-        partners, query_raw, gain_query, qn, cotangent, pack, left, right, x2, x1, e, d,
+        partners, query_raw, gain_query, qn, cotangent, pack, mate, beside, x2, x1, e, d,
         ex, dx, rl, delta, dqy,
     )
     rx2 = send(gx2, across[0])
     rx1 = send(gx1, across[1])
-    rl_ = send(gr, ups)
-    rr_ = send(gl, downs)
+    rm = send(gm, mates)
+    rb = send(gb, besides)
     grad_key, grad_value = call(
         final_kernel,
         [V] * 9,
         [((256, 256), BF16), ((256, 256), BF16)],
         10**6,
-        key_raw, gain_key, gown, ry2, ry1, rx2, rx1, rl_, rr_,
+        key_raw, gain_key, gown, ry2, ry1, rx2, rx1, rm, rb,
     )
     return (out, grad_query, grad_key, grad_value)
 

time: 90.5 us -> 93.7 us (1.035)
  the two profiles are of different devices: /device:TPU:2 before, /device:TPU:1 now
where the time goes in v3:
time: 93.7 us; the launch traced here: 93.3 us
  starting transfers between devices  53.1 us (57%)
  waiting for transfers between devices  29.6 us (32%)
  Pallas kernels  9.03 us (10%)
    ppermute x12, starting transfers between devices, send(): return lax.ppermute(value, AXES, perm)  53.1 us
    ppermute x12, waiting for transfers between devices, send(): return lax.ppermute(value, AXES, perm)  29.6 us
    pallas_call x5, Pallas kernels, call(): pl.pallas_call(kernel, out_shape=shapes, in_specs=specs, out_specs=[V] *...  9.03 us
  transfers between devices with their start and end apart: 12, of which 3 were waited for; matrix products, arithmetic and copies ran while one was open for 0% of the time, Pallas kernels for 2%

profile of v3, /device:TPU:1, one launch (start us, length us, event | category | flops | bytes accessed | tf_op | source)
XLA Modules:
  0.0 93.3 jit_solution(16705638133410479842)
XLA Ops:
  0.7 1.2 %shard_map.111.own = bf16[2,256,256]{2,1,0:T(8,128)(2,1)S(1)} custom-call(bf16[256,256]{1,0:T(8,128)(2,1)} %k_ref.1, bf16[256,256]{1,0:T(8,128)(2,1)} %v_hbm.1, f32[2,128]{1,0:T(2,128)} %gain_ref.5), custom_call_target="tpu_custom_call" | custom-call | flops 1000000 | bytes 525312 | tf_op jit(solution)/shard_map/pallas_call | solution.py:248
  1.9 5.4 %collective-permute-start.1 = (bf16[2,256,256]{2,1,0:T(8,128)(2,1)S(1)}, bf16[2,256,256]{2,1,0:T(8,128)(2,1)S(1)}, u32[]{:S(2)}, u32[]{:S(2)}) collective-permute-start(bf16[2,256,256]{2,1,0:T(8,128)(2,1)S(1)} %shard_map.111.own), channel_id=1, source_target_pairs={{1,2},{2,1},{3,4},{4,3},{5,6},{6,5},{7,8},{8,7},{9,10},{10,9},{11,... | collective-permute-start | bytes 786440 | tf_op jit(solution)/shard_map/ppermute | solution.py:268
  7.3 4.0 %collective-permute-start = (bf16[2,256,256]{2,1,0:T(8,128)(2,1)S(1)}, bf16[2,256,256]{2,1,0:T(8,128)(2,1)S(1)}, u32[]{:S(2)}, u32[]{:S(2)}) collective-permute-start(bf16[2,256,256]{2,1,0:T(8,128)(2,1)S(1)} %shard_map.111.own), channel_id=1, source_target_pairs={{0,1},{1,0},{2,3},{3,2},{4,5},{5,4},{6,7},{7,6},{8,9},{9,8},{10,11... | collective-permute-start | bytes 786440 | tf_op jit(solution)/shard_map/ppermute | solution.py:268
  11.3 8.5 %collective-permute-start.5 = (bf16[2,256,256]{2,1,0:T(8,128)(2,1)S(1)}, bf16[2,256,256]{2,1,0:T(8,128)(2,1)S(1)}, u32[]{:S(2)}, u32[]{:S(2)}) collective-permute-start(bf16[2,256,256]{2,1,0:T(8,128)(2,1)S(1)} %shard_map.111.own), channel_id=1, source_target_pairs={{0,32},{1,33},{2,34},{3,35},{4,36},{5,37},{6,38},{7,39},{8,40},{9,... | collective-permute-start | bytes 786440 | tf_op jit(solution)/shard_map/ppermute | solution.py:268
  19.8 6.6 %collective-permute-start.4 = (bf16[2,256,256]{2,1,0:T(8,128)(2,1)S(1)}, bf16[2,256,256]{2,1,0:T(8,128)(2,1)S(1)}, u32[]{:S(2)}, u32[]{:S(2)}) collective-permute-start(bf16[2,256,256]{2,1,0:T(8,128)(2,1)S(1)} %shard_map.111.own), channel_id=1, source_target_pairs={{0,64},{1,65},{2,66},{3,67},{4,68},{5,69},{6,70},{7,71},{8,72},{9,... | collective-permute-start | bytes 786440 | tf_op jit(solution)/shard_map/ppermute | solution.py:268
  26.3 3.1 %collective-permute-start.3 = (bf16[2,256,256]{2,1,0:T(8,128)(2,1)S(1)}, bf16[2,256,256]{2,1,0:T(8,128)(2,1)S(1)}, u32[]{:S(2)}, u32[]{:S(2)}) collective-permute-start(bf16[2,256,256]{2,1,0:T(8,128)(2,1)S(1)} %shard_map.111.own), channel_id=1, source_target_pairs={{0,128},{1,129},{2,130},{3,131},{4,132},{5,133},{6,134},{7,135},{8... | collective-permute-start | bytes 786440 | tf_op jit(solution)/shard_map/ppermute | solution.py:268
  29.5 4.4 %collective-permute-start.2 = (bf16[2,256,256]{2,1,0:T(8,128)(2,1)S(1)}, bf16[2,256,256]{2,1,0:T(8,128)(2,1)S(1)}, u32[]{:S(2)}, u32[]{:S(2)}) collective-permute-start(bf16[2,256,256]{2,1,0:T(8,128)(2,1)S(1)} %shard_map.111.own), channel_id=1, source_target_pairs={{0,256},{1,257},{2,258},{3,259},{4,260},{5,261},{6,262},{7,263},{8... | collective-permute-start | bytes 786440 | tf_op jit(solution)/shard_map/ppermute | solution.py:268
  33.9 0.0 copy-start.3
  33.9 0.6 copy-done.5
  34.5 0.0 copy-done.3
  34.6 1.6 %shard_map.112 = (bf16[256,256]{1,0:T(8,128)(2,1)S(1)}, bf16[2,3,256,256]{3,2,1,0:T(8,128)(2,1)S(1)}, bf16[2,3,256,256]{3,2,1,0:T(8,128)(2,1)S(1)}, f32[256,256]{1,0:T(8,128)S(1)}, f32[2,256,128]{2,1,0:T(8,128)S(1)}) custom-call(s32[1]{0:T(128)} %bitcast.dev_ref, s32[2]{0:T(128)S(1)} %copy-done.6, s32[2,4]{1,0:T(2,128)S(1)} %copy-done.3, ...), custom_call_target="tpu_custom_call" | custom-call | flops 251658240 | bytes 3277868 | tf_op jit(solution)/shard_map/pallas_call | solution.py:248
  36.2 7.1 %collective-permute-done.5.y1 = bf16[2,256,256]{2,1,0:T(8,128)(2,1)S(1)} collective-permute-done((bf16[2,256,256]{2,1,0:T(8,128)(2,1)S(1)}, bf16[2,256,256]{2,1,0:T(8,128)(2,1)S(1)}, u32[]{:S(2)}, u32[]{:S(2)}) %collective-permute-start.5) | collective-permute-done | bytes 262176 | tf_op jit(solution)/shard_map/ppermute | solution.py:268
  43.3 0.0 collective-permute-done.2.x2
  43.3 2.3 %shard_map.113 = (bf16[2,256,256]{2,1,0:T(8,128)(2,1)S(1)}, bf16[2,256,256]{2,1,0:T(8,128)(2,1)S(1)}, bf16[256,256]{1,0:T(8,128)(2,1)}, f32[2,256,128]{2,1,0:T(8...) custom-call(s32[2,4]{1,0:T(2,128)S(1)} %copy-done.3, ...), custom_call_target="tpu_custom_call" | custom-call | flops 301989888 | bytes 3801120 | tf_op jit(solution)/shard_map/pallas_call | solution.py:248
  45.6 2.7 %shard_map.114 = (bf16[2,256,256]{2,1,0:T(8,128)(2,1)S(1)}, bf16[2,256,256]{2,1,0:T(8,128)(2,1)S(1)}, bf16[2,256,256]{2,1,0:T(8,128)(2,1)S(1)}, bf16[2,256,256]{...) custom-call(s32[2,4]{1,0:T(2,128)S(1)} %copy-done.3, bf16[256,256]{1,0:T(8,128)(2,1)S(1)} %copy-done.1, ...), custom_call_target="tpu_custom_call" | custom-call | flops 352321536 | bytes 6292512 | tf_op jit(solution)/shard_map/pallas_call | solution.py:248
  48.3 5.8 %collective-permute-start.8 = (bf16[2,256,256]{2,1,0:T(8,128)(2,1)S(1)}, bf16[2,256,256]{2,1,0:T(8,128)(2,1)S(1)}, u32[]{:S(2)}, u32[]{:S(2)}) collective-permute-start(bf16[2,256,256]{2,1,0:T(8,128)(2,1)S(1)} %get-tuple-element.40), channel_id=1, source_target_pairs={{0,256},{1,257},{2,258},{3,259},{4,260},{5,261},{6,262},{7,263},{8... | collective-permute-start | bytes 786440 | tf_op jit(solution)/shard_map/ppermute | solution.py:268
  54.1 2.2 %collective-permute-start.9 = (bf16[2,256,256]{2,1,0:T(8,128)(2,1)S(1)}, bf16[2,256,256]{2,1,0:T(8,128)(2,1)S(1)}, u32[]{:S(2)}, u32[]{:S(2)}) collective-permute-start(bf16[2,256,256]{2,1,0:T(8,128)(2,1)S(1)} %get-tuple-element.41), channel_id=1, source_target_pairs={{0,128},{1,129},{2,130},{3,131},{4,132},{5,133},{6,134},{7,135},{8... | collective-permute-start | bytes 786440 | tf_op jit(solution)/shard_map/ppermute | solution.py:268
  56.3 2.9 %collective-permute-start.10 = (bf16[2,256,256]{2,1,0:T(8,128)(2,1)S(1)}, bf16[2,256,256]{2,1,0:T(8,128)(2,1)S(1)}, u32[]{:S(2)}, u32[]{:S(2)}) collective-permute-start(bf16[2,256,256]{2,1,0:T(8,128)(2,1)S(1)} %get-tuple-element.42), channel_id=1, source_target_pairs={{0,1},{1,0},{2,3},{3,2},{4,5},{5,4},{6,7},{7,6},{8,9},{9,8},{10,11... | collective-permute-start | bytes 786440 | tf_op jit(solution)/shard_map/ppermute | solution.py:268
  59.3 1.9 %collective-permute-start.11 = (bf16[2,256,256]{2,1,0:T(8,128)(2,1)S(1)}, bf16[2,256,256]{2,1,0:T(8,128)(2,1)S(1)}, u32[]{:S(2)}, u32[]{:S(2)}) collective-permute-start(bf16[2,256,256]{2,1,0:T(8,128)(2,1)S(1)} %get-tuple-element.43), channel_id=1, source_target_pairs={{1,2},{2,1},{3,4},{4,3},{5,6},{6,5},{7,8},{8,7},{9,10},{10,9},{11,... | collective-permute-start | bytes 786440 | tf_op jit(solution)/shard_map/ppermute | solution.py:268
  61.2 6.4 %collective-permute-start.6 = (bf16[2,256,256]{2,1,0:T(8,128)(2,1)S(1)}, bf16[2,256,256]{2,1,0:T(8,128)(2,1)S(1)}, u32[]{:S(2)}, u32[]{:S(2)}) collective-permute-start(bf16[2,256,256]{2,1,0:T(8,128)(2,1)S(1)} %get-tuple-element.38), channel_id=1, source_target_pairs={{0,64},{1,65},{2,66},{3,67},{4,68},{5,69},{6,70},{7,71},{8,72},{9,... | collective-permute-start | bytes 786440 | tf_op jit(solution)/shard_map/ppermute | solution.py:268
  67.7 1.9 %collective-permute-start.7 = (bf16[2,256,256]{2,1,0:T(8,128)(2,1)S(1)}, bf16[2,256,256]{2,1,0:T(8,128)(2,1)S(1)}, u32[]{:S(2)}, u32[]{:S(2)}) collective-permute-start(bf16[2,256,256]{2,1,0:T(8,128)(2,1)S(1)} %get-tuple-element.39), channel_id=1, source_target_pairs={{0,32},{1,33},{2,34},{3,35},{4,36},{5,37},{6,38},{7,39},{8,40},{9,... | collective-permute-start | bytes 786440 | tf_op jit(solution)/shard_map/ppermute | solution.py:268
  69.6 11.2 %collective-permute-done.6.a = bf16[2,256,256]{2,1,0:T(8,128)(2,1)S(1)} collective-permute-done((bf16[2,256,256]{2,1,0:T(8,128)(2,1)S(1)}, bf16[2,256,256]{2,1,0:T(8,128)(2,1)S(1)}, u32[]{:S(2)}, u32[]{:S(2)}) %collective-permute-start.6) | collective-permute-done | bytes 262176 | tf_op jit(solution)/shard_map/ppermute | solution.py:268
  80.8 11.2 %collective-permute-done.7.b = bf16[2,256,256]{2,1,0:T(8,128)(2,1)S(1)} collective-permute-done((bf16[2,256,256]{2,1,0:T(8,128)(2,1)S(1)}, bf16[2,256,256]{2,1,0:T(8,128)(2,1)S(1)}, u32[]{:S(2)}, u32[]{:S(2)}) %collective-permute-start.7) | collective-permute-done | bytes 262176 | tf_op jit(solution)/shard_map/ppermute | solution.py:268
  92.1 1.2 %shard_map.115 = (bf16[256,256]{1,0:T(8,128)(2,1)}, bf16[256,256]{1,0:T(8,128)(2,1)}) custom-call(bf16[256,256]{1,0:T(8,128)(2,1)S(1)} %copy-done.2, f32[2,128]{1,0:T(2,128)S(1)} %copy-done.4, f32[2,256,256]{2,1,0:T(8,128)S(1)} %get-tuple-element.37.own, bf16[2,256,256]{2,1,0:T(8,128)(2,1)S(1)} %collective-permute-done.6.a, ...), custom_call_target="tpu_custom_call" | custom-call | flops 1000000 | bytes 2491392 | tf_op jit(solution)/shard_map/pallas_call | solution.py:248
  (19 shorter events, 0.0 us)
Async XLA Ops:
  0.6 33.3 %copy-start = (bf16[256,256]{1,0:T(8,128)(2,1)S(1)}, bf16[256,256]{1,0:T(8,128)(2,1)}, u32[]{:S(2)}) copy-start(bf16[256,256]{1,0:T(8,128)(2,1)} %cot_ref.5) | copy-start | bytes 393220
  0.6 33.3 %copy-start.1 = (bf16[256,256]{1,0:T(8,128)(2,1)S(1)}, bf16[256,256]{1,0:T(8,128)(2,1)}, u32[]{:S(2)}) copy-start(bf16[256,256]{1,0:T(8,128)(2,1)} %q_ref.3) | copy-start | bytes 393220
  1.9 27.6 %collective-permute-start.1 = (bf16[2,256,256]{2,1,0:T(8,128)(2,1)S(1)}, bf16[2,256,256]{2,1,0:T(8,128)(2,1)S(1)}, u32[]{:S(2)}, u32[]{:S(2)}) collective-permute-start(bf16[2,256,256]{2,1,0:T(8,128)(2,1)S(1)} %shard_map.111.own), channel_id=1, source_target_pairs={{1,2},{2,1},{3,4},{4,3},{5,6},{6,5},{7,8},{8,7},{9,10},{10,9},{11,... | collective-permute-start | bytes 786440 | tf_op jit(solution)/shard_map/ppermute | solution.py:268
  7.3 26.6 %collective-permute-start = (bf16[2,256,256]{2,1,0:T(8,128)(2,1)S(1)}, bf16[2,256,256]{2,1,0:T(8,128)(2,1)S(1)}, u32[]{:S(2)}, u32[]{:S(2)}) collective-permute-start(bf16[2,256,256]{2,1,0:T(8,128)(2,1)S(1)} %shard_map.111.own), channel_id=1, source_target_pairs={{0,1},{1,0},{2,3},{3,2},{4,5},{5,4},{6,7},{7,6},{8,9},{9,8},{10,11... | collective-permute-start | bytes 786440 | tf_op jit(solution)/shard_map/ppermute | solution.py:268
  11.3 32.0 %collective-permute-start.5 = (bf16[2,256,256]{2,1,0:T(8,128)(2,1)S(1)}, bf16[2,256,256]{2,1,0:T(8,128)(2,1)S(1)}, u32[]{:S(2)}, u32[]{:S(2)}) collective-permute-start(bf16[2,256,256]{2,1,0:T(8,128)(2,1)S(1)} %shard_map.111.own), channel_id=1, source_target_pairs={{0,32},{1,33},{2,34},{3,35},{4,36},{5,37},{6,38},{7,39},{8,40},{9,... | collective-permute-start | bytes 786440 | tf_op jit(solution)/shard_map/ppermute | solution.py:268
  19.8 23.5 %collective-permute-start.4 = (bf16[2,256,256]{2,1,0:T(8,128)(2,1)S(1)}, bf16[2,256,256]{2,1,0:T(8,128)(2,1)S(1)}, u32[]{:S(2)}, u32[]{:S(2)}) collective-permute-start(bf16[2,256,256]{2,1,0:T(8,128)(2,1)S(1)} %shard_map.111.own), channel_id=1, source_target_pairs={{0,64},{1,65},{2,66},{3,67},{4,68},{5,69},{6,70},{7,71},{8,72},{9,... | collective-permute-start | bytes 786440 | tf_op jit(solution)/shard_map/ppermute | solution.py:268
  26.3 16.9 %collective-permute-start.3 = (bf16[2,256,256]{2,1,0:T(8,128)(2,1)S(1)}, bf16[2,256,256]{2,1,0:T(8,128)(2,1)S(1)}, u32[]{:S(2)}, u32[]{:S(2)}) collective-permute-start(bf16[2,256,256]{2,1,0:T(8,128)(2,1)S(1)} %shard_map.111.own), channel_id=1, source_target_pairs={{0,128},{1,129},{2,130},{3,131},{4,132},{5,133},{6,134},{7,135},{8... | collective-permute-start | bytes 786440 | tf_op jit(solution)/shard_map/ppermute | solution.py:268
  29.5 13.9 %collective-permute-start.2 = (bf16[2,256,256]{2,1,0:T(8,128)(2,1)S(1)}, bf16[2,256,256]{2,1,0:T(8,128)(2,1)S(1)}, u32[]{:S(2)}, u32[]{:S(2)}) collective-permute-start(bf16[2,256,256]{2,1,0:T(8,128)(2,1)S(1)} %shard_map.111.own), channel_id=1, source_target_pairs={{0,256},{1,257},{2,258},{3,259},{4,260},{5,261},{6,262},{7,263},{8... | collective-permute-start | bytes 786440 | tf_op jit(solution)/shard_map/ppermute | solution.py:268
  33.9 0.7 copy-start.5
  33.9 0.7 copy-start.3
  33.9 0.7 copy-start.6
  45.6 46.4 %copy-start.2 = (bf16[256,256]{1,0:T(8,128)(2,1)S(1)}, bf16[256,256]{1,0:T(8,128)(2,1)}, u32[]{:S(2)}) copy-start(bf16[256,256]{1,0:T(8,128)(2,1)} %k_ref.1) | copy-start | bytes 393220
  48.3 19.3 %collective-permute-start.8 = (bf16[2,256,256]{2,1,0:T(8,128)(2,1)S(1)}, bf16[2,256,256]{2,1,0:T(8,128)(2,1)S(1)}, u32[]{:S(2)}, u32[]{:S(2)}) collective-permute-start(bf16[2,256,256]{2,1,0:T(8,128)(2,1)S(1)} %get-tuple-element.40), channel_id=1, source_target_pairs={{0,256},{1,257},{2,258},{3,259},{4,260},{5,261},{6,262},{7,263},{8... | collective-permute-start | bytes 786440 | tf_op jit(solution)/shard_map/ppermute | solution.py:268
  54.1 15.5 %collective-permute-start.9 = (bf16[2,256,256]{2,1,0:T(8,128)(2,1)S(1)}, bf16[2,256,256]{2,1,0:T(8,128)(2,1)S(1)}, u32[]{:S(2)}, u32[]{:S(2)}) collective-permute-start(bf16[2,256,256]{2,1,0:T(8,128)(2,1)S(1)} %get-tuple-element.41), channel_id=1, source_target_pairs={{0,128},{1,129},{2,130},{3,131},{4,132},{5,133},{6,134},{7,135},{8... | collective-permute-start | bytes 786440 | tf_op jit(solution)/shard_map/ppermute | solution.py:268
  56.3 13.3 %collective-permute-start.10 = (bf16[2,256,256]{2,1,0:T(8,128)(2,1)S(1)}, bf16[2,256,256]{2,1,0:T(8,128)(2,1)S(1)}, u32[]{:S(2)}, u32[]{:S(2)}) collective-permute-start(bf16[2,256,256]{2,1,0:T(8,128)(2,1)S(1)} %get-tuple-element.42), channel_id=1, source_target_pairs={{0,1},{1,0},{2,3},{3,2},{4,5},{5,4},{6,7},{7,6},{8,9},{9,8},{10,11... | collective-permute-start | bytes 786440 | tf_op jit(solution)/shard_map/ppermute | solution.py:268
  59.3 10.4 %collective-permute-start.11 = (bf16[2,256,256]{2,1,0:T(8,128)(2,1)S(1)}, bf16[2,256,256]{2,1,0:T(8,128)(2,1)S(1)}, u32[]{:S(2)}, u32[]{:S(2)}) collective-permute-start(bf16[2,256,256]{2,1,0:T(8,128)(2,1)S(1)} %get-tuple-element.43), channel_id=1, source_target_pairs={{1,2},{2,1},{3,4},{4,3},{5,6},{6,5},{7,8},{8,7},{9,10},{10,9},{11,... | collective-permute-start | bytes 786440 | tf_op jit(solution)/shard_map/ppermute | solution.py:268
  61.2 19.6 %collective-permute-start.6 = (bf16[2,256,256]{2,1,0:T(8,128)(2,1)S(1)}, bf16[2,256,256]{2,1,0:T(8,128)(2,1)S(1)}, u32[]{:S(2)}, u32[]{:S(2)}) collective-permute-start(bf16[2,256,256]{2,1,0:T(8,128)(2,1)S(1)} %get-tuple-element.38), channel_id=1, source_target_pairs={{0,64},{1,65},{2,66},{3,67},{4,68},{5,69},{6,70},{7,71},{8,72},{9,... | collective-permute-start | bytes 786440 | tf_op jit(solution)/shard_map/ppermute | solution.py:268
  67.6 24.4 %copy-start.4 = (f32[2,128]{1,0:T(2,128)S(1)}, f32[2,128]{1,0:T(2,128)}, u32[]{:S(2)}) copy-start(f32[2,128]{1,0:T(2,128)} %gain_ref.5) | copy-start | bytes 3076
  67.7 24.4 %collective-permute-start.7 = (bf16[2,256,256]{2,1,0:T(8,128)(2,1)S(1)}, bf16[2,256,256]{2,1,0:T(8,128)(2,1)S(1)}, u32[]{:S(2)}, u32[]{:S(2)}) collective-permute-start(bf16[2,256,256]{2,1,0:T(8,128)(2,1)S(1)} %get-tuple-element.39), channel_id=1, source_target_pairs={{0,32},{1,33},{2,34},{3,35},{4,36},{5,37},{6,38},{7,39},{8,40},{9,... | collective-permute-start | bytes 786440 | tf_op jit(solution)/shard_map/ppermute | solution.py:268

commit v4 on v3

--- a/solution.py
+++ b/solution.py
@@ -68,23 +68,28 @@
     copies[2].wait()
 
 
+def near_part(own, mate, zpair, zup, zdown, kind, h):
+    beside = zpair[kind, :, cols(h)] + zup[kind, :, cols(h)] + zdown[kind, :, cols(h)]
+    return [own[kind, :, cols(h)], mate[kind, :, cols(h)], beside]
+
+
 def local_kernel(
-    dev_ref, reach_ref, part_ref, q_ref, gain_ref, cot_ref, own, mate, beside,
+    dev_ref, reach_ref, part_ref, q_ref, gain_ref, cot_ref, own, mate, zpair, zup, zdown,
     qn_ref, e_ref, d_ref, o_ref, l_ref, *, last_block,
 ):
     scale = 128 ** (-0.5)
-    near = (own, mate, beside)
     both = range(HEADS)
+    ks, vs = ([near_part(own, mate, zpair, zup, zdown, kind, h) for h in both] for kind in (0, 1))
     step = 1 - 2 * (dev_ref[0] & 1)
     shifts = (0, 2 * step, -2 * step)
     qn = [norm(q_ref[:, cols(h)], gain_ref[h : h + 1, :])[2].astype(BF16) for h in both]
     ct = [cot_ref[:, cols(h)] for h in both]
     for h in both:
         qn_ref[:, cols(h)] = qn[h]
-    s_near = [[dot(qn[h], r[0, :, cols(h)], NT) for r in near] for h in both]
+    s_near = [[dot(qn[h], k, NT) for k in ks[h]] for h in both]
     for h in both:
-        for n, r in enumerate(near):
-            d_ref[h, n] = dot(ct[h], r[1, :, cols(h)], NT).astype(BF16)
+        for n, v in enumerate(vs[h]):
+            d_ref[h, n] = dot(ct[h], v, NT).astype(BF16)
     keep = {}
     for i in range(2):
         block = dev_ref[0] * 2 + i
@@ -109,7 +114,7 @@
             )
         o_ref[:, cols(h)] = dot(
             jnp.concatenate([e_ref[h, n] for n in range(3)], axis=1),
-            jnp.concatenate([r[1, :, cols(h)] for r in near], axis=0),
+            jnp.concatenate(vs[h], axis=0),
             NN,
         )
 
@@ -172,12 +177,11 @@
 
 
 def near_kernel(
-    part_ref, q_ref, gain_ref, qn_ref, cot_ref, own, mate, beside, x2, x1, e_ref, d_ref,
+    part_ref, q_ref, gain_ref, qn_ref, cot_ref, own, mate, zpair, zup, zdown, x2, x1, e_ref, d_ref,
     ex_ref, dx_ref, rl_ref, delta_ref, dqy_ref,
     gx2_ref, gx1_ref, gm_ref, gb_ref, gown_ref, gq_ref,
 ):
     scale = 128 ** (-0.5)
-    near = (own, mate, beside)
     pick = [[part_ref[i, n] & 1 for n in range(2)] for i in range(2)]
     for h in range(HEADS):
         qn = qn_ref[:, cols(h)]
@@ -208,7 +212,7 @@
         normed, inverse, _ = norm(q_ref[:, cols(h)], gain_ref[h : h + 1, :])
         band = dot(
             jnp.concatenate(grads, axis=1),
-            jnp.concatenate([r[0, :, cols(h)] for r in near], axis=0),
+            jnp.concatenate(near_part(own, mate, zpair, zup, zdown, 0, h), axis=0),
             NN,
         )
         for i in range(2):
@@ -223,17 +227,17 @@
             ).astype(BF16)
 
 
-def final_kernel(k_ref, gain_ref, own, a, b, c, d, e, f, gk_ref, gv_ref):
-    terms = (a, b, c, d, e, f)
-    for h in range(HEADS):
-        dk = own[0, :, cols(h)]
-        dv = own[1, :, cols(h)]
+def final_kernel(k_ref, gain_ref, own, a, b, c, d, e, f, g, h, gk_ref, gv_ref):
+    terms = (a, b, c, d, e, f, g, h)
+    for n in range(HEADS):
+        dk = own[0, :, cols(n)]
+        dv = own[1, :, cols(n)]
         for t in terms:
-            dk = dk + t[0, :, cols(h)].astype(F32)
-            dv = dv + t[1, :, cols(h)].astype(F32)
-        normed, inverse, _ = norm(k_ref[:, cols(h)], gain_ref[h : h + 1, :])
-        gk_ref[:, cols(h)] = norm_back(dk, normed, inverse, gain_ref[h : h + 1, :]).astype(BF16)
-        gv_ref[:, cols(h)] = dv.astype(BF16)
+            dk = dk + t[0, :, cols(n)].astype(F32)
+            dv = dv + t[1, :, cols(n)].astype(F32)
+        normed, inverse, _ = norm(k_ref[:, cols(n)], gain_ref[n : n + 1, :])
+        gk_ref[:, cols(n)] = norm_back(dk, normed, inverse, gain_ref[n : n + 1, :]).astype(BF16)
+        gv_ref[:, cols(n)] = dv.astype(BF16)
 
 
 V = pl.BlockSpec(memory_space=pltpu.VMEM)
@@ -260,7 +264,12 @@
     count = lax.axis_size(AXES)
     device = lax.axis_index(AXES).astype(jnp.int32).reshape(1)
     mates = [(i, i ^ 1) for i in range(count)]
-    besides = [(i, j) for a in range(1, count - 1, 2) for i, j in ((a, a + 1), (a + 1, a))]
+    run = lax.axis_size("ctx") // 2
+    joints = [(a, a + 1) for a in range(1, count - 1, 2)]
+    cross_up = [(a, b) for a, b in joints if a // run != b // run]
+    cross_down = [(b, a) for a, b in cross_up]
+    inner = [(a, b) for a, b in joints if a // run == b // run]
+    inner = [p for a, b in inner for p in ((a, b), (b, a))]
     masks = [count >> (level + 1) for level in range(LEVELS)]
     across = [[(i, i ^ m) for i in range(count)] for m in masks]
 
@@ -282,7 +291,9 @@
     x2 = send(pack, across[0])
     x1 = send(pack, across[1])
     mate = send(pack, mates)
-    beside = send(pack, besides)
+    zpair = send(pack, inner)
+    zup = send(pack, cross_up)
+    zdown = send(pack, cross_down)
 
     tiles = ((HEADS, 3, 256, 256), BF16)
     x_tiles = ((HEADS, 2, 256, 128), BF16)
@@ -290,10 +301,10 @@
     full = ((256, 256), F32)
     qn, e, d, o_part, l_part = call(
         functools.partial(local_kernel, last_block=2 * count - 1),
-        [S, S, S] + [V] * 6,
+        [S, S, S] + [V] * 8,
         [((256, 256), BF16), tiles, tiles, full, rowstat],
         20 * 3 * 2 * 128**3,
-        device, band_reach, partners, query_raw, gain_query, cotangent, pack, mate, beside,
+        device, band_reach, partners, query_raw, gain_query, cotangent, pack, mate, zpair, zup, zdown,
     )
     gy2, gy1, out, rl, delta, dqy, ex, dx = call(
         far_kernel,
@@ -306,22 +317,24 @@
     ry1 = send(gy1, across[3])
     gx2, gx1, gm, gb, gown, grad_query = call(
         near_kernel,
-        [S] + [V] * 16,
+        [S] + [V] * 18,
         [pack_t, pack_t, pack_t, pack_t, ((2, 256, 256), F32), ((256, 256), BF16)],
         28 * 3 * 2 * 128**3,
-        partners, query_raw, gain_query, qn, cotangent, pack, mate, beside, x2, x1, e, d,
+        partners, query_raw, gain_query, qn, cotangent, pack, mate, zpair, zup, zdown, x2, x1, e, d,
         ex, dx, rl, delta, dqy,
     )
     rx2 = send(gx2, across[0])
     rx1 = send(gx1, across[1])
     rm = send(gm, mates)
-    rb = send(gb, besides)
+    rb = send(gb, inner)
+    ru = send(gb, cross_up)
+    rd = send(gb, cross_down)
     grad_key, grad_value = call(
         final_kernel,
-        [V] * 9,
+        [V] * 11,
         [((256, 256), BF16), ((256, 256), BF16)],
         10**6,
-        key_raw, gain_key, gown, ry2, ry1, rx2, rx1, rm, rb,
+        key_raw, gain_key, gown, ry2, ry1, rx2, rx1, rm, rb, ru, rd,
     )
     return (out, grad_query, grad_key, grad_value)
 

time: 93.7 us -> 99.8 us (1.065)
  waiting for transfers between devices: 29.6 us -> 33 us
  starting transfers between devices: 53.1 us -> 55.6 us
    ppermute x12 -> x16, waiting for transfers between devices: 29.6 us -> 33 us  [send(): return lax.ppermute(value, AXES, perm)]
    ppermute x12 -> x16, starting transfers between devices: 53.1 us -> 55.6 us  [send(): return lax.ppermute(value, AXES, perm)]
  transfers between devices with their start and end apart: 12 -> 16, of which waited for: 3 -> 5; matrix products, arithmetic and copies ran while one was open for 0% -> 0% of each run, Pallas kernels for 2% -> 2%
where the time goes in v4:
time: 99.8 us; the launch traced here: 99.3 us
  starting transfers between devices  55.6 us (56%)
  waiting for transfers between devices  33 us (33%)
  Pallas kernels  9.15 us (9%)
    ppermute x16, starting transfers between devices, send(): return lax.ppermute(value, AXES, perm)  55.6 us
    ppermute x16, waiting for transfers between devices, send(): return lax.ppermute(value, AXES, perm)  33 us
    pallas_call x5, Pallas kernels, call(): pl.pallas_call(kernel, out_shape=shapes, in_specs=specs, out_specs=[V] *...  9.15 us
  transfers between devices with their start and end apart: 16, of which 5 were waited for; matrix products, arithmetic and copies ran while one was open for 0% of the time, Pallas kernels for 2%

profile of v4, /device:TPU:1, one launch (start us, length us, event | category | flops | bytes accessed | tf_op | source)
XLA Modules:
  0.0 99.3 jit_solution(12172811620286395857)
XLA Ops:
  0.7 1.2 %shard_map.111.own = bf16[2,256,256]{2,1,0:T(8,128)(2,1)S(1)} custom-call(bf16[256,256]{1,0:T(8,128)(2,1)} %k_ref.1, bf16[256,256]{1,0:T(8,128)(2,1)} %v_hbm.1, f32[2,128]{1,0:T(2,128)} %gain_ref.5), custom_call_target="tpu_custom_call" | custom-call | flops 1000000 | bytes 525312 | tf_op jit(solution)/shard_map/pallas_call | solution.py:252
  1.9 0.7 collective-permute-start.3
  2.6 0.7 collective-permute-start.2
  3.2 5.4 %collective-permute-start.1 = (bf16[2,256,256]{2,1,0:T(8,128)(2,1)S(1)}, bf16[2,256,256]{2,1,0:T(8,128)(2,1)S(1)}, u32[]{:S(2)}, u32[]{:S(2)}) collective-permute-start(bf16[2,256,256]{2,1,0:T(8,128)(2,1)S(1)} %shard_map.111.own), channel_id=1, source_target_pairs={{1,2},{2,1},{3,4},{4,3},{5,6},{6,5},{7,8},{8,7},{9,10},{10,9},{11,... | collective-permute-start | bytes 786440 | tf_op jit(solution)/shard_map/ppermute | solution.py:277
  8.6 4.0 %collective-permute-start = (bf16[2,256,256]{2,1,0:T(8,128)(2,1)S(1)}, bf16[2,256,256]{2,1,0:T(8,128)(2,1)S(1)}, u32[]{:S(2)}, u32[]{:S(2)}) collective-permute-start(bf16[2,256,256]{2,1,0:T(8,128)(2,1)S(1)} %shard_map.111.own), channel_id=1, source_target_pairs={{0,1},{1,0},{2,3},{3,2},{4,5},{5,4},{6,7},{7,6},{8,9},{9,8},{10,11... | collective-permute-start | bytes 786440 | tf_op jit(solution)/shard_map/ppermute | solution.py:277
  12.7 9.1 %collective-permute-start.7 = (bf16[2,256,256]{2,1,0:T(8,128)(2,1)S(1)}, bf16[2,256,256]{2,1,0:T(8,128)(2,1)S(1)}, u32[]{:S(2)}, u32[]{:S(2)}) collective-permute-start(bf16[2,256,256]{2,1,0:T(8,128)(2,1)S(1)} %shard_map.111.own), channel_id=1, source_target_pairs={{0,32},{1,33},{2,34},{3,35},{4,36},{5,37},{6,38},{7,39},{8,40},{9,... | collective-permute-start | bytes 786440 | tf_op jit(solution)/shard_map/ppermute | solution.py:277
  21.8 6.6 %collective-permute-start.6 = (bf16[2,256,256]{2,1,0:T(8,128)(2,1)S(1)}, bf16[2,256,256]{2,1,0:T(8,128)(2,1)S(1)}, u32[]{:S(2)}, u32[]{:S(2)}) collective-permute-start(bf16[2,256,256]{2,1,0:T(8,128)(2,1)S(1)} %shard_map.111.own), channel_id=1, source_target_pairs={{0,64},{1,65},{2,66},{3,67},{4,68},{5,69},{6,70},{7,71},{8,72},{9,... | collective-permute-start | bytes 786440 | tf_op jit(solution)/shard_map/ppermute | solution.py:277
  28.4 3.1 %collective-permute-start.5 = (bf16[2,256,256]{2,1,0:T(8,128)(2,1)S(1)}, bf16[2,256,256]{2,1,0:T(8,128)(2,1)S(1)}, u32[]{:S(2)}, u32[]{:S(2)}) collective-permute-start(bf16[2,256,256]{2,1,0:T(8,128)(2,1)S(1)} %shard_map.111.own), channel_id=1, source_target_pairs={{0,128},{1,129},{2,130},{3,131},{4,132},{5,133},{6,134},{7,135},{8... | collective-permute-start | bytes 786440 | tf_op jit(solution)/shard_map/ppermute | solution.py:277
  31.5 4.4 %collective-permute-start.4 = (bf16[2,256,256]{2,1,0:T(8,128)(2,1)S(1)}, bf16[2,256,256]{2,1,0:T(8,128)(2,1)S(1)}, u32[]{:S(2)}, u32[]{:S(2)}) collective-permute-start(bf16[2,256,256]{2,1,0:T(8,128)(2,1)S(1)} %shard_map.111.own), channel_id=1, source_target_pairs={{0,256},{1,257},{2,258},{3,259},{4,260},{5,261},{6,262},{7,263},{8... | collective-permute-start | bytes 786440 | tf_op jit(solution)/shard_map/ppermute | solution.py:277
  36.6 1.7 %shard_map.112 = (bf16[256,256]{1,0:T(8,128)(2,1)S(1)}, bf16[2,3,256,256]{3,2,1,0:T(8,128)(2,1)S(1)}, bf16[2,3,256,256]{3,2,1,0:T(8,128)(2,1)S(1)}, f32[256,256]{1,0:T(8,128)S(1)}, f32[2,256,128]{2,1,0:T(8,128)S(1)}) custom-call(s32[1]{0:T(128)} %bitcast.dev_ref, s32[2]{0:T(128)S(1)} %copy-done.6, s32[2,4]{1,0:T(2,128)S(1)} %copy-done.3, ...), custom_call_target="tpu_custom_call" | custom-call | flops 251658240 | bytes 3802156 | tf_op jit(solution)/shard_map/pallas_call | solution.py:252
  38.3 7.0 %collective-permute-done.7.y1 = bf16[2,256,256]{2,1,0:T(8,128)(2,1)S(1)} collective-permute-done((bf16[2,256,256]{2,1,0:T(8,128)(2,1)S(1)}, bf16[2,256,256]{2,1,0:T(8,128)(2,1)S(1)}, u32[]{:S(2)}, u32[]{:S(2)}) %collective-permute-start.7) | collective-permute-done | bytes 262176 | tf_op jit(solution)/shard_map/ppermute | solution.py:277
  45.4 2.3 %shard_map.113 = (bf16[2,256,256]{2,1,0:T(8,128)(2,1)S(1)}, bf16[2,256,256]{2,1,0:T(8,128)(2,1)S(1)}, bf16[256,256]{1,0:T(8,128)(2,1)}, f32[2,256,128]{2,1,0:T(8...) custom-call(s32[2,4]{1,0:T(2,128)S(1)} %copy-done.3, ...), custom_call_target="tpu_custom_call" | custom-call | flops 301989888 | bytes 3801120 | tf_op jit(solution)/shard_map/pallas_call | solution.py:252
  47.6 2.7 %shard_map.114 = (bf16[2,256,256]{2,1,0:T(8,128)(2,1)S(1)}, bf16[2,256,256]{2,1,0:T(8,128)(2,1)S(1)}, bf16[2,256,256]{2,1,0:T(8,128)(2,1)S(1)}, bf16[2,256,256]{...) custom-call(s32[2,4]{1,0:T(2,128)S(1)} %copy-done.3, bf16[256,256]{1,0:T(8,128)(2,1)S(1)} %copy-done.2, ...), custom_call_target="tpu_custom_call" | custom-call | flops 352321536 | bytes 6816800 | tf_op jit(solution)/shard_map/pallas_call | solution.py:252
  50.3 5.8 %collective-permute-start.10 = (bf16[2,256,256]{2,1,0:T(8,128)(2,1)S(1)}, bf16[2,256,256]{2,1,0:T(8,128)(2,1)S(1)}, u32[]{:S(2)}, u32[]{:S(2)}) collective-permute-start(bf16[2,256,256]{2,1,0:T(8,128)(2,1)S(1)} %get-tuple-element.40), channel_id=1, source_target_pairs={{0,256},{1,257},{2,258},{3,259},{4,260},{5,261},{6,262},{7,263},{8... | collective-permute-start | bytes 786440 | tf_op jit(solution)/shard_map/ppermute | solution.py:277
  56.1 2.2 %collective-permute-start.11 = (bf16[2,256,256]{2,1,0:T(8,128)(2,1)S(1)}, bf16[2,256,256]{2,1,0:T(8,128)(2,1)S(1)}, u32[]{:S(2)}, u32[]{:S(2)}) collective-permute-start(bf16[2,256,256]{2,1,0:T(8,128)(2,1)S(1)} %get-tuple-element.41), channel_id=1, source_target_pairs={{0,128},{1,129},{2,130},{3,131},{4,132},{5,133},{6,134},{7,135},{8... | collective-permute-start | bytes 786440 | tf_op jit(solution)/shard_map/ppermute | solution.py:277
  58.4 2.9 %collective-permute-start.12 = (bf16[2,256,256]{2,1,0:T(8,128)(2,1)S(1)}, bf16[2,256,256]{2,1,0:T(8,128)(2,1)S(1)}, u32[]{:S(2)}, u32[]{:S(2)}) collective-permute-start(bf16[2,256,256]{2,1,0:T(8,128)(2,1)S(1)} %get-tuple-element.42), channel_id=1, source_target_pairs={{0,1},{1,0},{2,3},{3,2},{4,5},{5,4},{6,7},{7,6},{8,9},{9,8},{10,11... | collective-permute-start | bytes 786440 | tf_op jit(solution)/shard_map/ppermute | solution.py:277
  61.3 0.7 collective-permute-start.15
  62.7 1.9 %collective-permute-start.13 = (bf16[2,256,256]{2,1,0:T(8,128)(2,1)S(1)}, bf16[2,256,256]{2,1,0:T(8,128)(2,1)S(1)}, u32[]{:S(2)}, u32[]{:S(2)}) collective-permute-start(bf16[2,256,256]{2,1,0:T(8,128)(2,1)S(1)} %get-tuple-element.43), channel_id=1, source_target_pairs={{1,2},{2,1},{3,4},{4,3},{5,6},{6,5},{7,8},{8,7},{9,10},{10,9},{11,... | collective-permute-start | bytes 786440 | tf_op jit(solution)/shard_map/ppermute | solution.py:277
  64.6 3.4 %collective-permute-done.11.d = bf16[2,256,256]{2,1,0:T(8,128)(2,1)S(1)} collective-permute-done((bf16[2,256,256]{2,1,0:T(8,128)(2,1)S(1)}, bf16[2,256,256]{2,1,0:T(8,128)(2,1)S(1)}, u32[]{:S(2)}, u32[]{:S(2)}) %collective-permute-start.11) | collective-permute-done | bytes 262176 | tf_op jit(solution)/shard_map/ppermute | solution.py:277
  68.0 5.6 %collective-permute-start.8 = (bf16[2,256,256]{2,1,0:T(8,128)(2,1)S(1)}, bf16[2,256,256]{2,1,0:T(8,128)(2,1)S(1)}, u32[]{:S(2)}, u32[]{:S(2)}) collective-permute-start(bf16[2,256,256]{2,1,0:T(8,128)(2,1)S(1)} %get-tuple-element.38), channel_id=1, source_target_pairs={{0,64},{1,65},{2,66},{3,67},{4,68},{5,69},{6,70},{7,71},{8,72},{9,... | collective-permute-start | bytes 786440 | tf_op jit(solution)/shard_map/ppermute | solution.py:277
  73.6 1.9 %collective-permute-start.9 = (bf16[2,256,256]{2,1,0:T(8,128)(2,1)S(1)}, bf16[2,256,256]{2,1,0:T(8,128)(2,1)S(1)}, u32[]{:S(2)}, u32[]{:S(2)}) collective-permute-start(bf16[2,256,256]{2,1,0:T(8,128)(2,1)S(1)} %get-tuple-element.39), channel_id=1, source_target_pairs={{0,32},{1,33},{2,34},{3,35},{4,36},{5,37},{6,38},{7,39},{8,40},{9,... | collective-permute-start | bytes 786440 | tf_op jit(solution)/shard_map/ppermute | solution.py:277
  75.6 11.5 %collective-permute-done.8.a = bf16[2,256,256]{2,1,0:T(8,128)(2,1)S(1)} collective-permute-done((bf16[2,256,256]{2,1,0:T(8,128)(2,1)S(1)}, bf16[2,256,256]{2,1,0:T(8,128)(2,1)S(1)}, u32[]{:S(2)}, u32[]{:S(2)}) %collective-permute-start.8) | collective-permute-done | bytes 262176 | tf_op jit(solution)/shard_map/ppermute | solution.py:277
  87.1 10.9 %collective-permute-done.9.b = bf16[2,256,256]{2,1,0:T(8,128)(2,1)S(1)} collective-permute-done((bf16[2,256,256]{2,1,0:T(8,128)(2,1)S(1)}, bf16[2,256,256]{2,1,0:T(8,128)(2,1)S(1)}, u32[]{:S(2)}, u32[]{:S(2)}) %collective-permute-start.9) | collective-permute-done | bytes 262176 | tf_op jit(solution)/shard_map/ppermute | solution.py:277
  98.0 1.3 %shard_map.115 = (bf16[256,256]{1,0:T(8,128)(2,1)}, bf16[256,256]{1,0:T(8,128)(2,1)}) custom-call(bf16[256,256]{1,0:T(8,128)(2,1)S(1)} %copy-done.1, f32[2,128]{1,0:T(2,128)S(1)} %copy-done.4, f32[2,256,256]{2,1,0:T(8,128)S(1)} %get-tuple-element.37.own, bf16[2,256,256]{2,1,0:T(8,128)(2,1)S(1)} %collective-permute-done.8.a, ...), custom_call_target="tpu_custom_call" | custom-call | flops 1000000 | bytes 3015680 | tf_op jit(solution)/shard_map/pallas_call | solution.py:252
  (27 shorter events, 1.4 us)
Async XLA Ops:
  0.6 35.3 %copy-start = (bf16[256,256]{1,0:T(8,128)(2,1)S(1)}, bf16[256,256]{1,0:T(8,128)(2,1)}, u32[]{:S(2)}) copy-start(bf16[256,256]{1,0:T(8,128)(2,1)} %cot_ref.5) | copy-start | bytes 393220
  0.6 35.3 %copy-start.2 = (bf16[256,256]{1,0:T(8,128)(2,1)S(1)}, bf16[256,256]{1,0:T(8,128)(2,1)}, u32[]{:S(2)}) copy-start(bf16[256,256]{1,0:T(8,128)(2,1)} %q_ref.3) | copy-start | bytes 393220
  1.9 19.9 %collective-permute-start.3 = (bf16[2,256,256]{2,1,0:T(8,128)(2,1)S(1)}, bf16[2,256,256]{2,1,0:T(8,128)(2,1)S(1)}, u32[]{:S(2)}, u32[]{:S(2)}) collective-permute-start(bf16[2,256,256]{2,1,0:T(8,128)(2,1)S(1)} %shard_map.111.own), channel_id=1, source_target_pairs={{16,15},{32,31},{48,47},{64,63},{80,79},{96,95},{112,111},{128,127... | collective-permute-start | bytes 786440 | tf_op jit(solution)/shard_map/ppermute | solution.py:277
  2.6 25.8 %collective-permute-start.2 = (bf16[2,256,256]{2,1,0:T(8,128)(2,1)S(1)}, bf16[2,256,256]{2,1,0:T(8,128)(2,1)S(1)}, u32[]{:S(2)}, u32[]{:S(2)}) collective-permute-start(bf16[2,256,256]{2,1,0:T(8,128)(2,1)S(1)} %shard_map.111.own), channel_id=1, source_target_pairs={{15,16},{31,32},{47,48},{63,64},{79,80},{95,96},{111,112},{127,128... | collective-permute-start | bytes 786440 | tf_op jit(solution)/shard_map/ppermute | solution.py:277
  3.2 28.3 %collective-permute-start.1 = (bf16[2,256,256]{2,1,0:T(8,128)(2,1)S(1)}, bf16[2,256,256]{2,1,0:T(8,128)(2,1)S(1)}, u32[]{:S(2)}, u32[]{:S(2)}) collective-permute-start(bf16[2,256,256]{2,1,0:T(8,128)(2,1)S(1)} %shard_map.111.own), channel_id=1, source_target_pairs={{1,2},{2,1},{3,4},{4,3},{5,6},{6,5},{7,8},{8,7},{9,10},{10,9},{11,... | collective-permute-start | bytes 786440 | tf_op jit(solution)/shard_map/ppermute | solution.py:277
  8.6 27.3 %collective-permute-start = (bf16[2,256,256]{2,1,0:T(8,128)(2,1)S(1)}, bf16[2,256,256]{2,1,0:T(8,128)(2,1)S(1)}, u32[]{:S(2)}, u32[]{:S(2)}) collective-permute-start(bf16[2,256,256]{2,1,0:T(8,128)(2,1)S(1)} %shard_map.111.own), channel_id=1, source_target_pairs={{0,1},{1,0},{2,3},{3,2},{4,5},{5,4},{6,7},{7,6},{8,9},{9,8},{10,11... | collective-permute-start | bytes 786440 | tf_op jit(solution)/shard_map/ppermute | solution.py:277
  12.7 32.6 %collective-permute-start.7 = (bf16[2,256,256]{2,1,0:T(8,128)(2,1)S(1)}, bf16[2,256,256]{2,1,0:T(8,128)(2,1)S(1)}, u32[]{:S(2)}, u32[]{:S(2)}) collective-permute-start(bf16[2,256,256]{2,1,0:T(8,128)(2,1)S(1)} %shard_map.111.own), channel_id=1, source_target_pairs={{0,32},{1,33},{2,34},{3,35},{4,36},{5,37},{6,38},{7,39},{8,40},{9,... | collective-permute-start | bytes 786440 | tf_op jit(solution)/shard_map/ppermute | solution.py:277
  21.8 23.5 %collective-permute-start.6 = (bf16[2,256,256]{2,1,0:T(8,128)(2,1)S(1)}, bf16[2,256,256]{2,1,0:T(8,128)(2,1)S(1)}, u32[]{:S(2)}, u32[]{:S(2)}) collective-permute-start(bf16[2,256,256]{2,1,0:T(8,128)(2,1)S(1)} %shard_map.111.own), channel_id=1, source_target_pairs={{0,64},{1,65},{2,66},{3,67},{4,68},{5,69},{6,70},{7,71},{8,72},{9,... | collective-permute-start | bytes 786440 | tf_op jit(solution)/shard_map/ppermute | solution.py:277
  28.4 16.9 %collective-permute-start.5 = (bf16[2,256,256]{2,1,0:T(8,128)(2,1)S(1)}, bf16[2,256,256]{2,1,0:T(8,128)(2,1)S(1)}, u32[]{:S(2)}, u32[]{:S(2)}) collective-permute-start(bf16[2,256,256]{2,1,0:T(8,128)(2,1)S(1)} %shard_map.111.own), channel_id=1, source_target_pairs={{0,128},{1,129},{2,130},{3,131},{4,132},{5,133},{6,134},{7,135},{8... | collective-permute-start | bytes 786440 | tf_op jit(solution)/shard_map/ppermute | solution.py:277
  31.5 13.9 %collective-permute-start.4 = (bf16[2,256,256]{2,1,0:T(8,128)(2,1)S(1)}, bf16[2,256,256]{2,1,0:T(8,128)(2,1)S(1)}, u32[]{:S(2)}, u32[]{:S(2)}) collective-permute-start(bf16[2,256,256]{2,1,0:T(8,128)(2,1)S(1)} %shard_map.111.own), channel_id=1, source_target_pairs={{0,256},{1,257},{2,258},{3,259},{4,260},{5,261},{6,262},{7,263},{8... | collective-permute-start | bytes 786440 | tf_op jit(solution)/shard_map/ppermute | solution.py:277
  35.9 0.7 copy-start.5
  35.9 0.7 copy-start.3
  35.9 0.7 copy-start.6
  47.6 50.4 %copy-start.1 = (bf16[256,256]{1,0:T(8,128)(2,1)S(1)}, bf16[256,256]{1,0:T(8,128)(2,1)}, u32[]{:S(2)}) copy-start(bf16[256,256]{1,0:T(8,128)(2,1)} %k_ref.1) | copy-start | bytes 393220
  50.3 12.3 %collective-permute-start.10 = (bf16[2,256,256]{2,1,0:T(8,128)(2,1)S(1)}, bf16[2,256,256]{2,1,0:T(8,128)(2,1)S(1)}, u32[]{:S(2)}, u32[]{:S(2)}) collective-permute-start(bf16[2,256,256]{2,1,0:T(8,128)(2,1)S(1)} %get-tuple-element.40), channel_id=1, source_target_pairs={{0,256},{1,257},{2,258},{3,259},{4,260},{5,261},{6,262},{7,263},{8... | collective-permute-start | bytes 786440 | tf_op jit(solution)/shard_map/ppermute | solution.py:277
  56.1 11.9 %collective-permute-start.11 = (bf16[2,256,256]{2,1,0:T(8,128)(2,1)S(1)}, bf16[2,256,256]{2,1,0:T(8,128)(2,1)S(1)}, u32[]{:S(2)}, u32[]{:S(2)}) collective-permute-start(bf16[2,256,256]{2,1,0:T(8,128)(2,1)S(1)} %get-tuple-element.41), channel_id=1, source_target_pairs={{0,128},{1,129},{2,130},{3,131},{4,132},{5,133},{6,134},{7,135},{8... | collective-permute-start | bytes 786440 | tf_op jit(solution)/shard_map/ppermute | solution.py:277
  58.4 15.2 %collective-permute-start.12 = (bf16[2,256,256]{2,1,0:T(8,128)(2,1)S(1)}, bf16[2,256,256]{2,1,0:T(8,128)(2,1)S(1)}, u32[]{:S(2)}, u32[]{:S(2)}) collective-permute-start(bf16[2,256,256]{2,1,0:T(8,128)(2,1)S(1)} %get-tuple-element.42), channel_id=1, source_target_pairs={{0,1},{1,0},{2,3},{3,2},{4,5},{5,4},{6,7},{7,6},{8,9},{9,8},{10,11... | collective-permute-start | bytes 786440 | tf_op jit(solution)/shard_map/ppermute | solution.py:277
  61.3 14.3 %collective-permute-start.15 = (bf16[2,256,256]{2,1,0:T(8,128)(2,1)S(1)}, bf16[2,256,256]{2,1,0:T(8,128)(2,1)S(1)}, u32[]{:S(2)}, u32[]{:S(2)}) collective-permute-start(bf16[2,256,256]{2,1,0:T(8,128)(2,1)S(1)} %get-tuple-element.43), channel_id=1, source_target_pairs={{16,15},{32,31},{48,47},{64,63},{80,79},{96,95},{112,111},{128,127... | collective-permute-start | bytes 786440 | tf_op jit(solution)/shard_map/ppermute | solution.py:277
  62.0 13.6 %collective-permute-start.14 = (bf16[2,256,256]{2,1,0:T(8,128)(2,1)S(1)}, bf16[2,256,256]{2,1,0:T(8,128)(2,1)S(1)}, u32[]{:S(2)}, u32[]{:S(2)}) collective-permute-start(bf16[2,256,256]{2,1,0:T(8,128)(2,1)S(1)} %get-tuple-element.43), channel_id=1, source_target_pairs={{15,16},{31,32},{47,48},{63,64},{79,80},{95,96},{111,112},{127,128... | collective-permute-start | bytes 786440 | tf_op jit(solution)/shard_map/ppermute | solution.py:277
  62.7 12.9 %collective-permute-start.13 = (bf16[2,256,256]{2,1,0:T(8,128)(2,1)S(1)}, bf16[2,256,256]{2,1,0:T(8,128)(2,1)S(1)}, u32[]{:S(2)}, u32[]{:S(2)}) collective-permute-start(bf16[2,256,256]{2,1,0:T(8,128)(2,1)S(1)} %get-tuple-element.43), channel_id=1, source_target_pairs={{1,2},{2,1},{3,4},{4,3},{5,6},{6,5},{7,8},{8,7},{9,10},{10,9},{11,... | collective-permute-start | bytes 786440 | tf_op jit(solution)/shard_map/ppermute | solution.py:277
  68.0 19.1 %collective-permute-start.8 = (bf16[2,256,256]{2,1,0:T(8,128)(2,1)S(1)}, bf16[2,256,256]{2,1,0:T(8,128)(2,1)S(1)}, u32[]{:S(2)}, u32[]{:S(2)}) collective-permute-start(bf16[2,256,256]{2,1,0:T(8,128)(2,1)S(1)} %get-tuple-element.38), channel_id=1, source_target_pairs={{0,64},{1,65},{2,66},{3,67},{4,68},{5,69},{6,70},{7,71},{8,72},{9,... | collective-permute-start | bytes 786440 | tf_op jit(solution)/shard_map/ppermute | solution.py:277
  73.6 24.4 %copy-start.4 = (f32[2,128]{1,0:T(2,128)S(1)}, f32[2,128]{1,0:T(2,128)}, u32[]{:S(2)}) copy-start(f32[2,128]{1,0:T(2,128)} %gain_ref.5) | copy-start | bytes 3076
  73.6 24.4 %collective-permute-start.9 = (bf16[2,256,256]{2,1,0:T(8,128)(2,1)S(1)}, bf16[2,256,256]{2,1,0:T(8,128)(2,1)S(1)}, u32[]{:S(2)}, u32[]{:S(2)}) collective-permute-start(bf16[2,256,256]{2,1,0:T(8,128)(2,1)S(1)} %get-tuple-element.39), channel_id=1, source_target_pairs={{0,32},{1,33},{2,34},{3,35},{4,36},{5,37},{6,38},{7,39},{8,40},{9,... | collective-permute-start | bytes 786440 | tf_op jit(solution)/shard_map/ppermute | solution.py:277

commit v5 on v4

--- a/solution.py
+++ b/solution.py
@@ -125,8 +125,8 @@
 
 
 def far_kernel(
-    part_ref, qn_ref, cot_ref, x2, x1, y2, y1, o_ref, l_ref,
-    g2_ref, g1_ref, out_ref, rl_ref, delta_ref, dq_ref, e_ref, d_ref,
+    part_ref, qn_ref, cot_ref, x2, x1, y2, y1, o_ref, l_ref, eb_ref, db_ref,
+    g2_ref, g1_ref, gb_ref, out_ref, rl_ref, delta_ref, dq_ref, e_ref, d_ref,
 ):
     scale = 128 ** (-0.5)
     levels = (x2, x1, y2, y1)
@@ -146,7 +146,7 @@
     dp = {t: dot(ct[t], vs[t], NT) for t in each}
     low = {t: e[t].astype(BF16) for t in each}
     far_o = {t: dot(low[t], vs[t], NN) for t in each}
-    p, ds, rl = {}, {}, {}
+    p, ds, rl, delta = {}, {}, {}, {}
     for t in each:
         h, i = t
         total = e[t][:, :128] + e[t][:, 128:256] + e[t][:, 256:384] + e[t][:, 384:]
@@ -154,12 +154,12 @@
         rl[t] = 1.0 / total
         o = ((o_ref[rows(i), cols(h)] + far_o[t]) * rl[t]).astype(BF16)
         out_ref[rows(i), cols(h)] = o
-        delta = jnp.sum(ct[t].astype(F32) * o.astype(F32), axis=-1, keepdims=True)
+        delta[t] = jnp.sum(ct[t].astype(F32) * o.astype(F32), axis=-1, keepdims=True)
         rl_ref[h, rows(i), :] = jnp.broadcast_to(rl[t], (BLOCK, 128))
-        delta_ref[h, rows(i), :] = jnp.broadcast_to(delta, (BLOCK, 128))
+        delta_ref[h, rows(i), :] = jnp.broadcast_to(delta[t], (BLOCK, 128))
         y = slice(256, 512)
         p[t] = e[t][:, y] * rl[t]
-        ds[t] = (p[t] * (dp[t][:, y] - delta)).astype(BF16)
+        ds[t] = (p[t] * (dp[t][:, y] - delta[t])).astype(BF16)
     dk = {t: dot(ds[t], q[t], TN) * scale for t in each}
     dv = {t: dot(p[t].astype(BF16), ct[t], TN) for t in each}
     for h in range(HEADS):
@@ -168,6 +168,12 @@
             for g in range(2):
                 ref[0, rows(g), cols(h)] = spread([dk[h, i][rows(n)] for i in range(2)], picks, g)
                 ref[1, rows(g), cols(h)] = spread([dv[h, i][rows(n)] for i in range(2)], picks, g)
+    for h in range(HEADS):
+        full = [jnp.concatenate((v[h, 0], v[h, 1]), axis=0) for v in (rl, delta, q, ct)]
+        pb = eb_ref[h, 2].astype(F32) * full[0]
+        dsb = (pb * (db_ref[h, 2].astype(F32) - full[1])).astype(BF16)
+        gb_ref[0, :, cols(h)] = (dot(dsb, full[2], TN) * scale).astype(BF16)
+        gb_ref[1, :, cols(h)] = dot(pb.astype(BF16), full[3], TN).astype(BF16)
     for t in each:
         h, i = t
         dq_ref[rows(i), cols(h)] = dot(ds[t], ks[t][256:], NN)
@@ -179,7 +185,7 @@
 def near_kernel(
     part_ref, q_ref, gain_ref, qn_ref, cot_ref, own, mate, zpair, zup, zdown, x2, x1, e_ref, d_ref,
     ex_ref, dx_ref, rl_ref, delta_ref, dqy_ref,
-    gx2_ref, gx1_ref, gm_ref, gb_ref, gown_ref, gq_ref,
+    gx2_ref, gx1_ref, gm_ref, gown_ref, gq_ref,
 ):
     scale = 128 ** (-0.5)
     pick = [[part_ref[i, n] & 1 for n in range(2)] for i in range(2)]
@@ -203,10 +209,12 @@
         rl2 = jnp.concatenate((rl, rl), axis=1)
         delta2 = jnp.concatenate((delta, delta), axis=1)
         grads = []
-        for n, ref in enumerate((gown_ref, gm_ref, gb_ref)):
+        for n, ref in enumerate((gown_ref, gm_ref, None)):
             p = e_ref[h, n].astype(F32) * rl2
             ds = (p * (d_ref[h, n].astype(F32) - delta2)).astype(BF16)
             grads.append(ds)
+            if ref is None:
+                continue
             ref[0, :, cols(h)] = (dot(ds, qn, TN) * scale).astype(ref.dtype)
             ref[1, :, cols(h)] = dot(p.astype(BF16), ct, TN).astype(ref.dtype)
         normed, inverse, _ = norm(q_ref[:, cols(h)], gain_ref[h : h + 1, :])
@@ -306,19 +314,19 @@
         20 * 3 * 2 * 128**3,
         device, band_reach, partners, query_raw, gain_query, cotangent, pack, mate, zpair, zup, zdown,
     )
-    gy2, gy1, out, rl, delta, dqy, ex, dx = call(
+    gy2, gy1, gb, out, rl, delta, dqy, ex, dx = call(
         far_kernel,
-        [S] + [V] * 8,
-        [pack_t, pack_t, ((256, 256), BF16), rowstat, rowstat, full, x_tiles, x_tiles],
+        [S] + [V] * 10,
+        [pack_t, pack_t, pack_t, ((256, 256), BF16), rowstat, rowstat, full, x_tiles, x_tiles],
         8 * 9 * 2 * 128**3,
-        partners, qn, cotangent, x2, x1, y2, y1, o_part, l_part,
+        partners, qn, cotangent, x2, x1, y2, y1, o_part, l_part, e, d,
     )
     ry2 = send(gy2, across[2])
     ry1 = send(gy1, across[3])
-    gx2, gx1, gm, gb, gown, grad_query = call(
+    gx2, gx1, gm, gown, grad_query = call(
         near_kernel,
         [S] + [V] * 18,
-        [pack_t, pack_t, pack_t, pack_t, ((2, 256, 256), F32), ((256, 256), BF16)],
+        [pack_t, pack_t, pack_t, ((2, 256, 256), F32), ((256, 256), BF16)],
         28 * 3 * 2 * 128**3,
         partners, query_raw, gain_query, qn, cotangent, pack, mate, zpair, zup, zdown, x2, x1, e, d,
         ex, dx, rl, delta, dqy,

time: 99.8 us -> 96.4 us (0.966)
  the two profiles are of different devices: /device:TPU:1 before, /device:TPU:20 now
where the time goes in v5:
time: 96.4 us; the launch traced here: 96 us
  starting transfers between devices  58.4 us (61%)
  waiting for transfers between devices  26.5 us (27%)
  Pallas kernels  9.5 us (10%)
    ppermute x16, starting transfers between devices, send(): return lax.ppermute(value, AXES, perm)  58.4 us
    ppermute x16, waiting for transfers between devices, send(): return lax.ppermute(value, AXES, perm)  26.5 us
    pallas_call x5, Pallas kernels, call(): pl.pallas_call(kernel, out_shape=shapes, in_specs=specs, out_specs=[V] *...  9.5 us
  transfers between devices with their start and end apart: 16, of which 4 were waited for; matrix products, arithmetic and copies ran while one was open for 0% of the time, Pallas kernels for 2%

profile of v5, /device:TPU:20, one launch (start us, length us, event | category | flops | bytes accessed | tf_op | source)
XLA Modules:
  0.0 96.0 jit_solution(5020095863458697198)
XLA Ops:
  0.7 1.2 %shard_map.111.own = bf16[2,256,256]{2,1,0:T(8,128)(2,1)S(1)} custom-call(bf16[256,256]{1,0:T(8,128)(2,1)} %k_ref.1, bf16[256,256]{1,0:T(8,128)(2,1)} %v_hbm.1, f32[2,128]{1,0:T(2,128)} %gain_ref.5), custom_call_target="tpu_custom_call" | custom-call | flops 1000000 | bytes 525312 | tf_op jit(solution)/shard_map/pallas_call | solution.py:260
  1.9 10.3 %collective-permute-start.3 = (bf16[2,256,256]{2,1,0:T(8,128)(2,1)S(1)}, bf16[2,256,256]{2,1,0:T(8,128)(2,1)S(1)}, u32[]{:S(2)}, u32[]{:S(2)}) collective-permute-start(bf16[2,256,256]{2,1,0:T(8,128)(2,1)S(1)} %shard_map.111.own), channel_id=1, source_target_pairs={{16,15},{32,31},{48,47},{64,63},{80,79},{96,95},{112,111},{128,127... | collective-permute-start | bytes 786440 | tf_op jit(solution)/shard_map/ppermute | solution.py:285
  12.2 1.3 %collective-permute-start.2 = (bf16[2,256,256]{2,1,0:T(8,128)(2,1)S(1)}, bf16[2,256,256]{2,1,0:T(8,128)(2,1)S(1)}, u32[]{:S(2)}, u32[]{:S(2)}) collective-permute-start(bf16[2,256,256]{2,1,0:T(8,128)(2,1)S(1)} %shard_map.111.own), channel_id=1, source_target_pairs={{15,16},{31,32},{47,48},{63,64},{79,80},{95,96},{111,112},{127,128... | collective-permute-start | bytes 786440 | tf_op jit(solution)/shard_map/ppermute | solution.py:285
  13.5 0.7 collective-permute-start.1
  14.1 1.9 %collective-permute-start = (bf16[2,256,256]{2,1,0:T(8,128)(2,1)S(1)}, bf16[2,256,256]{2,1,0:T(8,128)(2,1)S(1)}, u32[]{:S(2)}, u32[]{:S(2)}) collective-permute-start(bf16[2,256,256]{2,1,0:T(8,128)(2,1)S(1)} %shard_map.111.own), channel_id=1, source_target_pairs={{0,1},{1,0},{2,3},{3,2},{4,5},{5,4},{6,7},{7,6},{8,9},{9,8},{10,11... | collective-permute-start | bytes 786440 | tf_op jit(solution)/shard_map/ppermute | solution.py:285
  16.1 5.2 %collective-permute-start.7 = (bf16[2,256,256]{2,1,0:T(8,128)(2,1)S(1)}, bf16[2,256,256]{2,1,0:T(8,128)(2,1)S(1)}, u32[]{:S(2)}, u32[]{:S(2)}) collective-permute-start(bf16[2,256,256]{2,1,0:T(8,128)(2,1)S(1)} %shard_map.111.own), channel_id=1, source_target_pairs={{0,32},{1,33},{2,34},{3,35},{4,36},{5,37},{6,38},{7,39},{8,40},{9,... | collective-permute-start | bytes 786440 | tf_op jit(solution)/shard_map/ppermute | solution.py:285
  21.3 4.7 %collective-permute-start.6 = (bf16[2,256,256]{2,1,0:T(8,128)(2,1)S(1)}, bf16[2,256,256]{2,1,0:T(8,128)(2,1)S(1)}, u32[]{:S(2)}, u32[]{:S(2)}) collective-permute-start(bf16[2,256,256]{2,1,0:T(8,128)(2,1)S(1)} %shard_map.111.own), channel_id=1, source_target_pairs={{0,64},{1,65},{2,66},{3,67},{4,68},{5,69},{6,70},{7,71},{8,72},{9,... | collective-permute-start | bytes 786440 | tf_op jit(solution)/shard_map/ppermute | solution.py:285
  26.1 3.1 %collective-permute-start.5 = (bf16[2,256,256]{2,1,0:T(8,128)(2,1)S(1)}, bf16[2,256,256]{2,1,0:T(8,128)(2,1)S(1)}, u32[]{:S(2)}, u32[]{:S(2)}) collective-permute-start(bf16[2,256,256]{2,1,0:T(8,128)(2,1)S(1)} %shard_map.111.own), channel_id=1, source_target_pairs={{0,128},{1,129},{2,130},{3,131},{4,132},{5,133},{6,134},{7,135},{8... | collective-permute-start | bytes 786440 | tf_op jit(solution)/shard_map/ppermute | solution.py:285
  29.2 2.7 %collective-permute-start.4 = (bf16[2,256,256]{2,1,0:T(8,128)(2,1)S(1)}, bf16[2,256,256]{2,1,0:T(8,128)(2,1)S(1)}, u32[]{:S(2)}, u32[]{:S(2)}) collective-permute-start(bf16[2,256,256]{2,1,0:T(8,128)(2,1)S(1)} %shard_map.111.own), channel_id=1, source_target_pairs={{0,256},{1,257},{2,258},{3,259},{4,260},{5,261},{6,262},{7,263},{8... | collective-permute-start | bytes 786440 | tf_op jit(solution)/shard_map/ppermute | solution.py:285
  32.6 1.7 %shard_map.112 = (bf16[256,256]{1,0:T(8,128)(2,1)S(1)}, bf16[2,3,256,256]{3,2,1,0:T(8,128)(2,1)S(1)}, bf16[2,3,256,256]{3,2,1,0:T(8,128)(2,1)S(1)}, f32[256,256]{1,0:T(8,128)S(1)}, f32[2,256,128]{2,1,0:T(8,128)S(1)}) custom-call(s32[1]{0:T(128)} %bitcast.dev_ref, s32[2]{0:T(128)S(1)} %copy-done.6, s32[2,4]{1,0:T(2,128)S(1)} %copy-done.3, ...), custom_call_target="tpu_custom_call" | custom-call | flops 251658240 | bytes 3802156 | tf_op jit(solution)/shard_map/pallas_call | solution.py:260
  34.3 8.1 %collective-permute-done.7.y1 = bf16[2,256,256]{2,1,0:T(8,128)(2,1)S(1)} collective-permute-done((bf16[2,256,256]{2,1,0:T(8,128)(2,1)S(1)}, bf16[2,256,256]{2,1,0:T(8,128)(2,1)S(1)}, u32[]{:S(2)}, u32[]{:S(2)}) %collective-permute-start.7) | collective-permute-done | bytes 262176 | tf_op jit(solution)/shard_map/ppermute | solution.py:285
  42.4 2.8 %shard_map.113 = (bf16[2,256,256]{2,1,0:T(8,128)(2,1)S(1)}, bf16[2,256,256]{2,1,0:T(8,128)(2,1)S(1)}, bf16[2,256,256]{2,1,0:T(8,128)(2,1)S(1)}, bf16[256,256]{1,...) custom-call(s32[2,4]{1,0:T(2,128)S(1)} %copy-done.3, ...), custom_call_target="tpu_custom_call" | custom-call | flops 301989888 | bytes 5636128 | tf_op jit(solution)/shard_map/pallas_call | solution.py:260
  45.2 2.6 %shard_map.114 = (bf16[2,256,256]{2,1,0:T(8,128)(2,1)S(1)}, bf16[2,256,256]{2,1,0:T(8,128)(2,1)S(1)}, bf16[2,256,256]{2,1,0:T(8,128)(2,1)S(1)}, f32[2,256,256]{2,1,0:T(8,128)S(1)}, bf16[256,256]{1,0:T(8,128)(2,1)}) custom-call(s32[2,4]{1,0:T(2,128)S(1)} %copy-done.3, bf16[256,256]{1,0:T(8,128)(2,1)S(1)} %copy-done.2, f32[2,128]{1,0:T(2,128)S(1)} %copy-done.5, ...), custom_call_target="tpu_custom_call" | custom-call | flops 352321536 | bytes 6554656 | tf_op jit(solution)/shard_map/pallas_call | solution.py:260
  47.8 3.9 %collective-permute-start.10 = (bf16[2,256,256]{2,1,0:T(8,128)(2,1)S(1)}, bf16[2,256,256]{2,1,0:T(8,128)(2,1)S(1)}, u32[]{:S(2)}, u32[]{:S(2)}) collective-permute-start(bf16[2,256,256]{2,1,0:T(8,128)(2,1)S(1)} %get-tuple-element.40), channel_id=1, source_target_pairs={{0,256},{1,257},{2,258},{3,259},{4,260},{5,261},{6,262},{7,263},{8... | collective-permute-start | bytes 786440 | tf_op jit(solution)/shard_map/ppermute | solution.py:285
  51.7 2.7 %collective-permute-start.11 = (bf16[2,256,256]{2,1,0:T(8,128)(2,1)S(1)}, bf16[2,256,256]{2,1,0:T(8,128)(2,1)S(1)}, u32[]{:S(2)}, u32[]{:S(2)}) collective-permute-start(bf16[2,256,256]{2,1,0:T(8,128)(2,1)S(1)} %get-tuple-element.41), channel_id=1, source_target_pairs={{0,128},{1,129},{2,130},{3,131},{4,132},{5,133},{6,134},{7,135},{8... | collective-permute-start | bytes 786440 | tf_op jit(solution)/shard_map/ppermute | solution.py:285
  54.4 1.9 %collective-permute-start.12 = (bf16[2,256,256]{2,1,0:T(8,128)(2,1)S(1)}, bf16[2,256,256]{2,1,0:T(8,128)(2,1)S(1)}, u32[]{:S(2)}, u32[]{:S(2)}) collective-permute-start(bf16[2,256,256]{2,1,0:T(8,128)(2,1)S(1)} %get-tuple-element.42), channel_id=1, source_target_pairs={{0,1},{1,0},{2,3},{3,2},{4,5},{5,4},{6,7},{7,6},{8,9},{9,8},{10,11... | collective-permute-start | bytes 786440 | tf_op jit(solution)/shard_map/ppermute | solution.py:285
  56.3 6.5 %collective-permute-start.8 = (bf16[2,256,256]{2,1,0:T(8,128)(2,1)S(1)}, bf16[2,256,256]{2,1,0:T(8,128)(2,1)S(1)}, u32[]{:S(2)}, u32[]{:S(2)}) collective-permute-start(bf16[2,256,256]{2,1,0:T(8,128)(2,1)S(1)} %get-tuple-element.38), channel_id=1, source_target_pairs={{0,64},{1,65},{2,66},{3,67},{4,68},{5,69},{6,70},{7,71},{8,72},{9,... | collective-permute-start | bytes 786440 | tf_op jit(solution)/shard_map/ppermute | solution.py:285
  62.8 5.3 %collective-permute-start.9 = (bf16[2,256,256]{2,1,0:T(8,128)(2,1)S(1)}, bf16[2,256,256]{2,1,0:T(8,128)(2,1)S(1)}, u32[]{:S(2)}, u32[]{:S(2)}) collective-permute-start(bf16[2,256,256]{2,1,0:T(8,128)(2,1)S(1)} %get-tuple-element.39), channel_id=1, source_target_pairs={{0,32},{1,33},{2,34},{3,35},{4,36},{5,37},{6,38},{7,39},{8,40},{9,... | collective-permute-start | bytes 786440 | tf_op jit(solution)/shard_map/ppermute | solution.py:285
  68.1 6.2 %collective-permute-start.15 = (bf16[2,256,256]{2,1,0:T(8,128)(2,1)S(1)}, bf16[2,256,256]{2,1,0:T(8,128)(2,1)S(1)}, u32[]{:S(2)}, u32[]{:S(2)}) collective-permute-start(bf16[2,256,256]{2,1,0:T(8,128)(2,1)S(1)} %get-tuple-element.43), channel_id=1, source_target_pairs={{16,15},{32,31},{48,47},{64,63},{80,79},{96,95},{112,111},{128,127... | collective-permute-start | bytes 786440 | tf_op jit(solution)/shard_map/ppermute | solution.py:285
  74.3 1.3 %collective-permute-start.14 = (bf16[2,256,256]{2,1,0:T(8,128)(2,1)S(1)}, bf16[2,256,256]{2,1,0:T(8,128)(2,1)S(1)}, u32[]{:S(2)}, u32[]{:S(2)}) collective-permute-start(bf16[2,256,256]{2,1,0:T(8,128)(2,1)S(1)} %get-tuple-element.43), channel_id=1, source_target_pairs={{15,16},{31,32},{47,48},{63,64},{79,80},{95,96},{111,112},{127,128... | collective-permute-start | bytes 786440 | tf_op jit(solution)/shard_map/ppermute | solution.py:285
  76.3 10.4 %collective-permute-done.9.b = bf16[2,256,256]{2,1,0:T(8,128)(2,1)S(1)} collective-permute-done((bf16[2,256,256]{2,1,0:T(8,128)(2,1)S(1)}, bf16[2,256,256]{2,1,0:T(8,128)(2,1)S(1)}, u32[]{:S(2)}, u32[]{:S(2)}) %collective-permute-start.9) | collective-permute-done | bytes 262176 | tf_op jit(solution)/shard_map/ppermute | solution.py:285
  86.7 2.8 %collective-permute-done.15.h = bf16[2,256,256]{2,1,0:T(8,128)(2,1)S(1)} collective-permute-done((bf16[2,256,256]{2,1,0:T(8,128)(2,1)S(1)}, bf16[2,256,256]{2,1,0:T(8,128)(2,1)S(1)}, u32[]{:S(2)}, u32[]{:S(2)}) %collective-permute-start.15) | collective-permute-done | bytes 262176 | tf_op jit(solution)/shard_map/ppermute | solution.py:285
  89.5 5.2 %collective-permute-done.14.g = bf16[2,256,256]{2,1,0:T(8,128)(2,1)S(1)} collective-permute-done((bf16[2,256,256]{2,1,0:T(8,128)(2,1)S(1)}, bf16[2,256,256]{2,1,0:T(8,128)(2,1)S(1)}, u32[]{:S(2)}, u32[]{:S(2)}) %collective-permute-start.14) | collective-permute-done | bytes 262176 | tf_op jit(solution)/shard_map/ppermute | solution.py:285
  94.7 1.3 %shard_map.115 = (bf16[256,256]{1,0:T(8,128)(2,1)}, bf16[256,256]{1,0:T(8,128)(2,1)}) custom-call(bf16[256,256]{1,0:T(8,128)(2,1)S(1)} %copy-done.1, f32[2,128]{1,0:T(2,128)S(1)} %copy-done.4, f32[2,256,256]{2,1,0:T(8,128)S(1)} %get-tuple-element.37.own, bf16[2,256,256]{2,1,0:T(8,128)(2,1)S(1)} %collective-permute-done.8.a, ...), custom_call_target="tpu_custom_call" | custom-call | flops 1000000 | bytes 3015680 | tf_op jit(solution)/shard_map/pallas_call | solution.py:260
  (27 shorter events, 1.4 us)
Async XLA Ops:
  0.6 31.4 %copy-start = (bf16[256,256]{1,0:T(8,128)(2,1)S(1)}, bf16[256,256]{1,0:T(8,128)(2,1)}, u32[]{:S(2)}) copy-start(bf16[256,256]{1,0:T(8,128)(2,1)} %cot_ref.5) | copy-start | bytes 393220
  0.6 31.4 %copy-start.2 = (bf16[256,256]{1,0:T(8,128)(2,1)S(1)}, bf16[256,256]{1,0:T(8,128)(2,1)}, u32[]{:S(2)}) copy-start(bf16[256,256]{1,0:T(8,128)(2,1)} %q_ref.3) | copy-start | bytes 393220
  1.9 19.5 %collective-permute-start.3 = (bf16[2,256,256]{2,1,0:T(8,128)(2,1)S(1)}, bf16[2,256,256]{2,1,0:T(8,128)(2,1)S(1)}, u32[]{:S(2)}, u32[]{:S(2)}) collective-permute-start(bf16[2,256,256]{2,1,0:T(8,128)(2,1)S(1)} %shard_map.111.own), channel_id=1, source_target_pairs={{16,15},{32,31},{48,47},{64,63},{80,79},{96,95},{112,111},{128,127... | collective-permute-start | bytes 786440 | tf_op jit(solution)/shard_map/ppermute | solution.py:285
  12.2 13.9 %collective-permute-start.2 = (bf16[2,256,256]{2,1,0:T(8,128)(2,1)S(1)}, bf16[2,256,256]{2,1,0:T(8,128)(2,1)S(1)}, u32[]{:S(2)}, u32[]{:S(2)}) collective-permute-start(bf16[2,256,256]{2,1,0:T(8,128)(2,1)S(1)} %shard_map.111.own), channel_id=1, source_target_pairs={{15,16},{31,32},{47,48},{63,64},{79,80},{95,96},{111,112},{127,128... | collective-permute-start | bytes 786440 | tf_op jit(solution)/shard_map/ppermute | solution.py:285
  13.5 15.7 %collective-permute-start.1 = (bf16[2,256,256]{2,1,0:T(8,128)(2,1)S(1)}, bf16[2,256,256]{2,1,0:T(8,128)(2,1)S(1)}, u32[]{:S(2)}, u32[]{:S(2)}) collective-permute-start(bf16[2,256,256]{2,1,0:T(8,128)(2,1)S(1)} %shard_map.111.own), channel_id=1, source_target_pairs={{1,2},{2,1},{3,4},{4,3},{5,6},{6,5},{7,8},{8,7},{9,10},{10,9},{11,... | collective-permute-start | bytes 786440 | tf_op jit(solution)/shard_map/ppermute | solution.py:285
  14.1 17.8 %collective-permute-start = (bf16[2,256,256]{2,1,0:T(8,128)(2,1)S(1)}, bf16[2,256,256]{2,1,0:T(8,128)(2,1)S(1)}, u32[]{:S(2)}, u32[]{:S(2)}) collective-permute-start(bf16[2,256,256]{2,1,0:T(8,128)(2,1)S(1)} %shard_map.111.own), channel_id=1, source_target_pairs={{0,1},{1,0},{2,3},{3,2},{4,5},{5,4},{6,7},{7,6},{8,9},{9,8},{10,11... | collective-permute-start | bytes 786440 | tf_op jit(solution)/shard_map/ppermute | solution.py:285
  16.1 26.3 %collective-permute-start.7 = (bf16[2,256,256]{2,1,0:T(8,128)(2,1)S(1)}, bf16[2,256,256]{2,1,0:T(8,128)(2,1)S(1)}, u32[]{:S(2)}, u32[]{:S(2)}) collective-permute-start(bf16[2,256,256]{2,1,0:T(8,128)(2,1)S(1)} %shard_map.111.own), channel_id=1, source_target_pairs={{0,32},{1,33},{2,34},{3,35},{4,36},{5,37},{6,38},{7,39},{8,40},{9,... | collective-permute-start | bytes 786440 | tf_op jit(solution)/shard_map/ppermute | solution.py:285
  21.3 21.1 %collective-permute-start.6 = (bf16[2,256,256]{2,1,0:T(8,128)(2,1)S(1)}, bf16[2,256,256]{2,1,0:T(8,128)(2,1)S(1)}, u32[]{:S(2)}, u32[]{:S(2)}) collective-permute-start(bf16[2,256,256]{2,1,0:T(8,128)(2,1)S(1)} %shard_map.111.own), channel_id=1, source_target_pairs={{0,64},{1,65},{2,66},{3,67},{4,68},{5,69},{6,70},{7,71},{8,72},{9,... | collective-permute-start | bytes 786440 | tf_op jit(solution)/shard_map/ppermute | solution.py:285
  26.1 16.3 %collective-permute-start.5 = (bf16[2,256,256]{2,1,0:T(8,128)(2,1)S(1)}, bf16[2,256,256]{2,1,0:T(8,128)(2,1)S(1)}, u32[]{:S(2)}, u32[]{:S(2)}) collective-permute-start(bf16[2,256,256]{2,1,0:T(8,128)(2,1)S(1)} %shard_map.111.own), channel_id=1, source_target_pairs={{0,128},{1,129},{2,130},{3,131},{4,132},{5,133},{6,134},{7,135},{8... | collective-permute-start | bytes 786440 | tf_op jit(solution)/shard_map/ppermute | solution.py:285
  29.2 13.2 %collective-permute-start.4 = (bf16[2,256,256]{2,1,0:T(8,128)(2,1)S(1)}, bf16[2,256,256]{2,1,0:T(8,128)(2,1)S(1)}, u32[]{:S(2)}, u32[]{:S(2)}) collective-permute-start(bf16[2,256,256]{2,1,0:T(8,128)(2,1)S(1)} %shard_map.111.own), channel_id=1, source_target_pairs={{0,256},{1,257},{2,258},{3,259},{4,260},{5,261},{6,262},{7,263},{8... | collective-permute-start | bytes 786440 | tf_op jit(solution)/shard_map/ppermute | solution.py:285
  31.9 0.7 copy-start.5
  31.9 0.7 copy-start.3
  32.0 0.7 copy-start.6
  45.2 49.5 %copy-start.1 = (bf16[256,256]{1,0:T(8,128)(2,1)S(1)}, bf16[256,256]{1,0:T(8,128)(2,1)}, u32[]{:S(2)}) copy-start(bf16[256,256]{1,0:T(8,128)(2,1)} %k_ref.1) | copy-start | bytes 393220
  47.8 20.4 %collective-permute-start.10 = (bf16[2,256,256]{2,1,0:T(8,128)(2,1)S(1)}, bf16[2,256,256]{2,1,0:T(8,128)(2,1)S(1)}, u32[]{:S(2)}, u32[]{:S(2)}) collective-permute-start(bf16[2,256,256]{2,1,0:T(8,128)(2,1)S(1)} %get-tuple-element.40), channel_id=1, source_target_pairs={{0,256},{1,257},{2,258},{3,259},{4,260},{5,261},{6,262},{7,263},{8... | collective-permute-start | bytes 786440 | tf_op jit(solution)/shard_map/ppermute | solution.py:285
  51.7 22.7 %collective-permute-start.11 = (bf16[2,256,256]{2,1,0:T(8,128)(2,1)S(1)}, bf16[2,256,256]{2,1,0:T(8,128)(2,1)S(1)}, u32[]{:S(2)}, u32[]{:S(2)}) collective-permute-start(bf16[2,256,256]{2,1,0:T(8,128)(2,1)S(1)} %get-tuple-element.41), channel_id=1, source_target_pairs={{0,128},{1,129},{2,130},{3,131},{4,132},{5,133},{6,134},{7,135},{8... | collective-permute-start | bytes 786440 | tf_op jit(solution)/shard_map/ppermute | solution.py:285
  54.4 21.2 %collective-permute-start.12 = (bf16[2,256,256]{2,1,0:T(8,128)(2,1)S(1)}, bf16[2,256,256]{2,1,0:T(8,128)(2,1)S(1)}, u32[]{:S(2)}, u32[]{:S(2)}) collective-permute-start(bf16[2,256,256]{2,1,0:T(8,128)(2,1)S(1)} %get-tuple-element.42), channel_id=1, source_target_pairs={{0,1},{1,0},{2,3},{3,2},{4,5},{5,4},{6,7},{7,6},{8,9},{9,8},{10,11... | collective-permute-start | bytes 786440 | tf_op jit(solution)/shard_map/ppermute | solution.py:285
  56.3 20.0 %collective-permute-start.8 = (bf16[2,256,256]{2,1,0:T(8,128)(2,1)S(1)}, bf16[2,256,256]{2,1,0:T(8,128)(2,1)S(1)}, u32[]{:S(2)}, u32[]{:S(2)}) collective-permute-start(bf16[2,256,256]{2,1,0:T(8,128)(2,1)S(1)} %get-tuple-element.38), channel_id=1, source_target_pairs={{0,64},{1,65},{2,66},{3,67},{4,68},{5,69},{6,70},{7,71},{8,72},{9,... | collective-permute-start | bytes 786440 | tf_op jit(solution)/shard_map/ppermute | solution.py:285
  62.8 23.9 %collective-permute-start.9 = (bf16[2,256,256]{2,1,0:T(8,128)(2,1)S(1)}, bf16[2,256,256]{2,1,0:T(8,128)(2,1)S(1)}, u32[]{:S(2)}, u32[]{:S(2)}) collective-permute-start(bf16[2,256,256]{2,1,0:T(8,128)(2,1)S(1)} %get-tuple-element.39), channel_id=1, source_target_pairs={{0,32},{1,33},{2,34},{3,35},{4,36},{5,37},{6,38},{7,39},{8,40},{9,... | collective-permute-start | bytes 786440 | tf_op jit(solution)/shard_map/ppermute | solution.py:285
  68.1 26.6 %copy-start.4 = (f32[2,128]{1,0:T(2,128)S(1)}, f32[2,128]{1,0:T(2,128)}, u32[]{:S(2)}) copy-start(f32[2,128]{1,0:T(2,128)} %gain_ref.5) | copy-start | bytes 3076
  68.1 21.4 %collective-permute-start.15 = (bf16[2,256,256]{2,1,0:T(8,128)(2,1)S(1)}, bf16[2,256,256]{2,1,0:T(8,128)(2,1)S(1)}, u32[]{:S(2)}, u32[]{:S(2)}) collective-permute-start(bf16[2,256,256]{2,1,0:T(8,128)(2,1)S(1)} %get-tuple-element.43), channel_id=1, source_target_pairs={{16,15},{32,31},{48,47},{64,63},{80,79},{96,95},{112,111},{128,127... | collective-permute-start | bytes 786440 | tf_op jit(solution)/shard_map/ppermute | solution.py:285
  74.3 20.3 %collective-permute-start.14 = (bf16[2,256,256]{2,1,0:T(8,128)(2,1)S(1)}, bf16[2,256,256]{2,1,0:T(8,128)(2,1)S(1)}, u32[]{:S(2)}, u32[]{:S(2)}) collective-permute-start(bf16[2,256,256]{2,1,0:T(8,128)(2,1)S(1)} %get-tuple-element.43), channel_id=1, source_target_pairs={{15,16},{31,32},{47,48},{63,64},{79,80},{95,96},{111,112},{127,128... | collective-permute-start | bytes 786440 | tf_op jit(solution)/shard_map/ppermute | solution.py:285
  75.7 19.0 %collective-permute-start.13 = (bf16[2,256,256]{2,1,0:T(8,128)(2,1)S(1)}, bf16[2,256,256]{2,1,0:T(8,128)(2,1)S(1)}, u32[]{:S(2)}, u32[]{:S(2)}) collective-permute-start(bf16[2,256,256]{2,1,0:T(8,128)(2,1)S(1)} %get-tuple-element.43), channel_id=1, source_target_pairs={{1,2},{2,1},{3,4},{4,3},{5,6},{6,5},{7,8},{8,7},{9,10},{10,9},{11,... | collective-permute-start | bytes 786440 | tf_op jit(solution)/shard_map/ppermute | solution.py:285

commit v6 on v5

--- a/solution.py
+++ b/solution.py
@@ -235,8 +235,15 @@
             ).astype(BF16)
 
 
-def final_kernel(k_ref, gain_ref, own, a, b, c, d, e, f, g, h, gk_ref, gv_ref):
-    terms = (a, b, c, d, e, f, g, h)
+def gather_kernel(own, a, b, c, d, e, f, out_ref):
+    total = own[...]
+    for t in (a, b, c, d, e, f):
+        total = total + t[...].astype(F32)
+    out_ref[...] = total
+
+
+def final_kernel(k_ref, gain_ref, own, a, b, gk_ref, gv_ref):
+    terms = (a, b)
     for n in range(HEADS):
         dk = own[0, :, cols(n)]
         dv = own[1, :, cols(n)]
@@ -337,12 +344,16 @@
     rb = send(gb, inner)
     ru = send(gb, cross_up)
     rd = send(gb, cross_down)
+    (gsum,) = call(
+        gather_kernel, [V] * 7, [((2, 256, 256), F32)], 10**6,
+        gown, ry2, ry1, rx2, rx1, rb, ru,
+    )
     grad_key, grad_value = call(
         final_kernel,
-        [V] * 11,
+        [V] * 5,
         [((256, 256), BF16), ((256, 256), BF16)],
         10**6,
-        key_raw, gain_key, gown, ry2, ry1, rx2, rx1, rm, rb, ru, rd,
+        key_raw, gain_key, gsum, rm, rd,
     )
     return (out, grad_query, grad_key, grad_value)
 

time: 96.4 us -> 94.1 us (0.976)
  the two profiles are of different devices: /device:TPU:20 before, /device:TPU:16 now
where the time goes in v6:
time: 94.1 us; the launch traced here: 93.6 us
  starting transfers between devices  60.8 us (65%)
  waiting for transfers between devices  21 us (22%)
  Pallas kernels  9.59 us (10%)
  local copies, waits for them, and re-layouts  1.31 us (1%)
    ppermute x16, starting transfers between devices, send(): return lax.ppermute(value, AXES, perm)  60.8 us
    ppermute x16, waiting for transfers between devices, send(): return lax.ppermute(value, AXES, perm)  21 us
    pallas_call x6, Pallas kernels, call(): pl.pallas_call(kernel, out_shape=shapes, in_specs=specs, out_specs=[V] *...  9.59 us
  transfers between devices with their start and end apart: 16, of which 4 were waited for; matrix products, arithmetic and copies ran while one was open for 0% of the time, Pallas kernels for 2%

profile of v6, /device:TPU:16, one launch (start us, length us, event | category | flops | bytes accessed | tf_op | source)
XLA Modules:
  0.0 93.6 jit_solution(14436657717038686999)
XLA Ops:
  0.7 1.2 %shard_map.111.own = bf16[2,256,256]{2,1,0:T(8,128)(2,1)S(1)} custom-call(bf16[256,256]{1,0:T(8,128)(2,1)} %k_ref.1, bf16[256,256]{1,0:T(8,128)(2,1)} %v_hbm.1, f32[2,128]{1,0:T(2,128)} %gain_ref.5), custom_call_target="tpu_custom_call" | custom-call | flops 1000000 | bytes 525312 | tf_op jit(solution)/shard_map/pallas_call | solution.py:267
  1.9 10.3 %collective-permute-start.3 = (bf16[2,256,256]{2,1,0:T(8,128)(2,1)S(1)}, bf16[2,256,256]{2,1,0:T(8,128)(2,1)S(1)}, u32[]{:S(2)}, u32[]{:S(2)}) collective-permute-start(bf16[2,256,256]{2,1,0:T(8,128)(2,1)S(1)} %shard_map.111.own), channel_id=1, source_target_pairs={{16,15},{32,31},{48,47},{64,63},{80,79},{96,95},{112,111},{128,127... | collective-permute-start | bytes 786440 | tf_op jit(solution)/shard_map/ppermute | solution.py:292
  12.2 1.3 %collective-permute-start.2 = (bf16[2,256,256]{2,1,0:T(8,128)(2,1)S(1)}, bf16[2,256,256]{2,1,0:T(8,128)(2,1)S(1)}, u32[]{:S(2)}, u32[]{:S(2)}) collective-permute-start(bf16[2,256,256]{2,1,0:T(8,128)(2,1)S(1)} %shard_map.111.own), channel_id=1, source_target_pairs={{15,16},{31,32},{47,48},{63,64},{79,80},{95,96},{111,112},{127,128... | collective-permute-start | bytes 786440 | tf_op jit(solution)/shard_map/ppermute | solution.py:292
  13.5 0.7 collective-permute-start.1
  14.1 1.9 %collective-permute-start = (bf16[2,256,256]{2,1,0:T(8,128)(2,1)S(1)}, bf16[2,256,256]{2,1,0:T(8,128)(2,1)S(1)}, u32[]{:S(2)}, u32[]{:S(2)}) collective-permute-start(bf16[2,256,256]{2,1,0:T(8,128)(2,1)S(1)} %shard_map.111.own), channel_id=1, source_target_pairs={{0,1},{1,0},{2,3},{3,2},{4,5},{5,4},{6,7},{7,6},{8,9},{9,8},{10,11... | collective-permute-start | bytes 786440 | tf_op jit(solution)/shard_map/ppermute | solution.py:292
  16.1 1.9 %collective-permute-start.7 = (bf16[2,256,256]{2,1,0:T(8,128)(2,1)S(1)}, bf16[2,256,256]{2,1,0:T(8,128)(2,1)S(1)}, u32[]{:S(2)}, u32[]{:S(2)}) collective-permute-start(bf16[2,256,256]{2,1,0:T(8,128)(2,1)S(1)} %shard_map.111.own), channel_id=1, source_target_pairs={{0,32},{1,33},{2,34},{3,35},{4,36},{5,37},{6,38},{7,39},{8,40},{9,... | collective-permute-start | bytes 786440 | tf_op jit(solution)/shard_map/ppermute | solution.py:292
  18.0 8.1 %collective-permute-start.6 = (bf16[2,256,256]{2,1,0:T(8,128)(2,1)S(1)}, bf16[2,256,256]{2,1,0:T(8,128)(2,1)S(1)}, u32[]{:S(2)}, u32[]{:S(2)}) collective-permute-start(bf16[2,256,256]{2,1,0:T(8,128)(2,1)S(1)} %shard_map.111.own), channel_id=1, source_target_pairs={{0,64},{1,65},{2,66},{3,67},{4,68},{5,69},{6,70},{7,71},{8,72},{9,... | collective-permute-start | bytes 786440 | tf_op jit(solution)/shard_map/ppermute | solution.py:292
  26.1 3.4 %collective-permute-start.5 = (bf16[2,256,256]{2,1,0:T(8,128)(2,1)S(1)}, bf16[2,256,256]{2,1,0:T(8,128)(2,1)S(1)}, u32[]{:S(2)}, u32[]{:S(2)}) collective-permute-start(bf16[2,256,256]{2,1,0:T(8,128)(2,1)S(1)} %shard_map.111.own), channel_id=1, source_target_pairs={{0,128},{1,129},{2,130},{3,131},{4,132},{5,133},{6,134},{7,135},{8... | collective-permute-start | bytes 786440 | tf_op jit(solution)/shard_map/ppermute | solution.py:292
  29.5 4.6 %collective-permute-start.4 = (bf16[2,256,256]{2,1,0:T(8,128)(2,1)S(1)}, bf16[2,256,256]{2,1,0:T(8,128)(2,1)S(1)}, u32[]{:S(2)}, u32[]{:S(2)}) collective-permute-start(bf16[2,256,256]{2,1,0:T(8,128)(2,1)S(1)} %shard_map.111.own), channel_id=1, source_target_pairs={{0,256},{1,257},{2,258},{3,259},{4,260},{5,261},{6,262},{7,263},{8... | collective-permute-start | bytes 786440 | tf_op jit(solution)/shard_map/ppermute | solution.py:292
  34.9 1.7 %shard_map.112 = (bf16[256,256]{1,0:T(8,128)(2,1)S(1)}, bf16[2,3,256,256]{3,2,1,0:T(8,128)(2,1)S(1)}, bf16[2,3,256,256]{3,2,1,0:T(8,128)(2,1)S(1)}, f32[256,256]{1,0:T(8,128)S(1)}, f32[2,256,128]{2,1,0:T(8,128)S(1)}) custom-call(s32[1]{0:T(128)} %bitcast.dev_ref, s32[2]{0:T(128)S(1)} %copy-done.6, s32[2,4]{1,0:T(2,128)S(1)} %copy-done.3, ...), custom_call_target="tpu_custom_call" | custom-call | flops 251658240 | bytes 3802156 | tf_op jit(solution)/shard_map/pallas_call | solution.py:267
  36.6 4.8 %collective-permute-done.7.y1 = bf16[2,256,256]{2,1,0:T(8,128)(2,1)S(1)} collective-permute-done((bf16[2,256,256]{2,1,0:T(8,128)(2,1)S(1)}, bf16[2,256,256]{2,1,0:T(8,128)(2,1)S(1)}, u32[]{:S(2)}, u32[]{:S(2)}) %collective-permute-start.7) | collective-permute-done | bytes 262176 | tf_op jit(solution)/shard_map/ppermute | solution.py:292
  41.3 2.6 %collective-permute-done.4.x2 = bf16[2,256,256]{2,1,0:T(8,128)(2,1)S(1)} collective-permute-done((bf16[2,256,256]{2,1,0:T(8,128)(2,1)S(1)}, bf16[2,256,256]{2,1,0:T(8,128)(2,1)S(1)}, u32[]{:S(2)}, u32[]{:S(2)}) %collective-permute-start.4) | collective-permute-done | bytes 262176 | tf_op jit(solution)/shard_map/ppermute | solution.py:292
  43.9 2.7 %shard_map.113 = (bf16[2,256,256]{2,1,0:T(8,128)(2,1)S(1)}, bf16[2,256,256]{2,1,0:T(8,128)(2,1)S(1)}, bf16[2,256,256]{2,1,0:T(8,128)(2,1)S(1)}, bf16[256,256]{1,...) custom-call(s32[2,4]{1,0:T(2,128)S(1)} %copy-done.3, ...), custom_call_target="tpu_custom_call" | custom-call | flops 301989888 | bytes 5636128 | tf_op jit(solution)/shard_map/pallas_call | solution.py:267
  46.7 2.6 %shard_map.114 = (bf16[2,256,256]{2,1,0:T(8,128)(2,1)S(1)}, bf16[2,256,256]{2,1,0:T(8,128)(2,1)S(1)}, bf16[2,256,256]{2,1,0:T(8,128)(2,1)S(1)}, f32[2,256,256]{2,1,0:T(8,128)S(1)}, bf16[256,256]{1,0:T(8,128)(2,1)}) custom-call(s32[2,4]{1,0:T(2,128)S(1)} %copy-done.3, bf16[256,256]{1,0:T(8,128)(2,1)S(1)} %copy-done.1, f32[2,128]{1,0:T(2,128)S(1)} %copy-done.4, ...), custom_call_target="tpu_custom_call" | custom-call | flops 352321536 | bytes 6554656 | tf_op jit(solution)/shard_map/pallas_call | solution.py:267
  49.2 3.4 %collective-permute-start.10 = (bf16[2,256,256]{2,1,0:T(8,128)(2,1)S(1)}, bf16[2,256,256]{2,1,0:T(8,128)(2,1)S(1)}, u32[]{:S(2)}, u32[]{:S(2)}) collective-permute-start(bf16[2,256,256]{2,1,0:T(8,128)(2,1)S(1)} %get-tuple-element.40), channel_id=1, source_target_pairs={{0,256},{1,257},{2,258},{3,259},{4,260},{5,261},{6,262},{7,263},{8... | collective-permute-start | bytes 786440 | tf_op jit(solution)/shard_map/ppermute | solution.py:292
  52.7 2.5 %collective-permute-start.11 = (bf16[2,256,256]{2,1,0:T(8,128)(2,1)S(1)}, bf16[2,256,256]{2,1,0:T(8,128)(2,1)S(1)}, u32[]{:S(2)}, u32[]{:S(2)}) collective-permute-start(bf16[2,256,256]{2,1,0:T(8,128)(2,1)S(1)} %get-tuple-element.41), channel_id=1, source_target_pairs={{0,128},{1,129},{2,130},{3,131},{4,132},{5,133},{6,134},{7,135},{8... | collective-permute-start | bytes 786440 | tf_op jit(solution)/shard_map/ppermute | solution.py:292
  55.2 6.7 %collective-permute-start.8 = (bf16[2,256,256]{2,1,0:T(8,128)(2,1)S(1)}, bf16[2,256,256]{2,1,0:T(8,128)(2,1)S(1)}, u32[]{:S(2)}, u32[]{:S(2)}) collective-permute-start(bf16[2,256,256]{2,1,0:T(8,128)(2,1)S(1)} %get-tuple-element.38), channel_id=1, source_target_pairs={{0,64},{1,65},{2,66},{3,67},{4,68},{5,69},{6,70},{7,71},{8,72},{9,... | collective-permute-start | bytes 786440 | tf_op jit(solution)/shard_map/ppermute | solution.py:292
  61.9 5.3 %collective-permute-start.9 = (bf16[2,256,256]{2,1,0:T(8,128)(2,1)S(1)}, bf16[2,256,256]{2,1,0:T(8,128)(2,1)S(1)}, u32[]{:S(2)}, u32[]{:S(2)}) collective-permute-start(bf16[2,256,256]{2,1,0:T(8,128)(2,1)S(1)} %get-tuple-element.39), channel_id=1, source_target_pairs={{0,32},{1,33},{2,34},{3,35},{4,36},{5,37},{6,38},{7,39},{8,40},{9,... | collective-permute-start | bytes 786440 | tf_op jit(solution)/shard_map/ppermute | solution.py:292
  67.2 1.3 %collective-permute-start.13 = (bf16[2,256,256]{2,1,0:T(8,128)(2,1)S(1)}, bf16[2,256,256]{2,1,0:T(8,128)(2,1)S(1)}, u32[]{:S(2)}, u32[]{:S(2)}) collective-permute-start(bf16[2,256,256]{2,1,0:T(8,128)(2,1)S(1)} %get-tuple-element.42), channel_id=1, source_target_pairs={{15,16},{31,32},{47,48},{63,64},{79,80},{95,96},{111,112},{127,128... | collective-permute-start | bytes 786440 | tf_op jit(solution)/shard_map/ppermute | solution.py:292
  69.2 1.9 %collective-permute-start.14 = (bf16[2,256,256]{2,1,0:T(8,128)(2,1)S(1)}, bf16[2,256,256]{2,1,0:T(8,128)(2,1)S(1)}, u32[]{:S(2)}, u32[]{:S(2)}) collective-permute-start(bf16[2,256,256]{2,1,0:T(8,128)(2,1)S(1)} %get-tuple-element.43), channel_id=1, source_target_pairs={{0,1},{1,0},{2,3},{3,2},{4,5},{5,4},{6,7},{7,6},{8,9},{9,8},{10,11... | collective-permute-start | bytes 786440 | tf_op jit(solution)/shard_map/ppermute | solution.py:292
  71.2 6.8 %collective-permute-start.15 = (bf16[2,256,256]{2,1,0:T(8,128)(2,1)S(1)}, bf16[2,256,256]{2,1,0:T(8,128)(2,1)S(1)}, u32[]{:S(2)}, u32[]{:S(2)}) collective-permute-start(bf16[2,256,256]{2,1,0:T(8,128)(2,1)S(1)} %get-tuple-element.42), channel_id=1, source_target_pairs={{16,15},{32,31},{48,47},{64,63},{80,79},{96,95},{112,111},{128,127... | collective-permute-start | bytes 786440 | tf_op jit(solution)/shard_map/ppermute | solution.py:292
  77.9 6.5 %collective-permute-done.9.b = bf16[2,256,256]{2,1,0:T(8,128)(2,1)S(1)} collective-permute-done((bf16[2,256,256]{2,1,0:T(8,128)(2,1)S(1)}, bf16[2,256,256]{2,1,0:T(8,128)(2,1)S(1)}, u32[]{:S(2)}, u32[]{:S(2)}) %collective-permute-start.9) | collective-permute-done | bytes 262176 | tf_op jit(solution)/shard_map/ppermute | solution.py:292
  84.4 7.1 %collective-permute-done.13.f = bf16[2,256,256]{2,1,0:T(8,128)(2,1)S(1)} collective-permute-done((bf16[2,256,256]{2,1,0:T(8,128)(2,1)S(1)}, bf16[2,256,256]{2,1,0:T(8,128)(2,1)S(1)}, u32[]{:S(2)}, u32[]{:S(2)}) %collective-permute-start.13) | collective-permute-done | bytes 262176 | tf_op jit(solution)/shard_map/ppermute | solution.py:292
  92.4 1.2 %shard_map.116 = (bf16[256,256]{1,0:T(8,128)(2,1)}, bf16[256,256]{1,0:T(8,128)(2,1)}) custom-call(bf16[256,256]{1,0:T(8,128)(2,1)S(1)} %copy-done.2, f32[2,128]{1,0:T(2,128)S(1)} %copy-done.5, f32[2,256,256]{2,1,0:T(8,128)S(1)} %shard_map.115.own, bf16[2,256,256]{2,1,0:T(8,128)(2,1)S(1)} %collective-permute-done.14.a, ...), custom_call_target="tpu_custom_call" | custom-call | flops 1000000 | bytes 1442816 | tf_op jit(solution)/shard_map/pallas_call | solution.py:267
  (28 shorter events, 2.2 us)
Async XLA Ops:
  0.6 33.6 %copy-start = (bf16[256,256]{1,0:T(8,128)(2,1)S(1)}, bf16[256,256]{1,0:T(8,128)(2,1)}, u32[]{:S(2)}) copy-start(bf16[256,256]{1,0:T(8,128)(2,1)} %cot_ref.5) | copy-start | bytes 393220
  0.6 33.6 %copy-start.1 = (bf16[256,256]{1,0:T(8,128)(2,1)S(1)}, bf16[256,256]{1,0:T(8,128)(2,1)}, u32[]{:S(2)}) copy-start(bf16[256,256]{1,0:T(8,128)(2,1)} %q_ref.3) | copy-start | bytes 393220
  1.9 16.1 %collective-permute-start.3 = (bf16[2,256,256]{2,1,0:T(8,128)(2,1)S(1)}, bf16[2,256,256]{2,1,0:T(8,128)(2,1)S(1)}, u32[]{:S(2)}, u32[]{:S(2)}) collective-permute-start(bf16[2,256,256]{2,1,0:T(8,128)(2,1)S(1)} %shard_map.111.own), channel_id=1, source_target_pairs={{16,15},{32,31},{48,47},{64,63},{80,79},{96,95},{112,111},{128,127... | collective-permute-start | bytes 786440 | tf_op jit(solution)/shard_map/ppermute | solution.py:292
  12.2 13.9 %collective-permute-start.2 = (bf16[2,256,256]{2,1,0:T(8,128)(2,1)S(1)}, bf16[2,256,256]{2,1,0:T(8,128)(2,1)S(1)}, u32[]{:S(2)}, u32[]{:S(2)}) collective-permute-start(bf16[2,256,256]{2,1,0:T(8,128)(2,1)S(1)} %shard_map.111.own), channel_id=1, source_target_pairs={{15,16},{31,32},{47,48},{63,64},{79,80},{95,96},{111,112},{127,128... | collective-permute-start | bytes 786440 | tf_op jit(solution)/shard_map/ppermute | solution.py:292
  13.5 16.0 %collective-permute-start.1 = (bf16[2,256,256]{2,1,0:T(8,128)(2,1)S(1)}, bf16[2,256,256]{2,1,0:T(8,128)(2,1)S(1)}, u32[]{:S(2)}, u32[]{:S(2)}) collective-permute-start(bf16[2,256,256]{2,1,0:T(8,128)(2,1)S(1)} %shard_map.111.own), channel_id=1, source_target_pairs={{1,2},{2,1},{3,4},{4,3},{5,6},{6,5},{7,8},{8,7},{9,10},{10,9},{11,... | collective-permute-start | bytes 786440 | tf_op jit(solution)/shard_map/ppermute | solution.py:292
  14.1 20.1 %collective-permute-start = (bf16[2,256,256]{2,1,0:T(8,128)(2,1)S(1)}, bf16[2,256,256]{2,1,0:T(8,128)(2,1)S(1)}, u32[]{:S(2)}, u32[]{:S(2)}) collective-permute-start(bf16[2,256,256]{2,1,0:T(8,128)(2,1)S(1)} %shard_map.111.own), channel_id=1, source_target_pairs={{0,1},{1,0},{2,3},{3,2},{4,5},{5,4},{6,7},{7,6},{8,9},{9,8},{10,11... | collective-permute-start | bytes 786440 | tf_op jit(solution)/shard_map/ppermute | solution.py:292
  16.1 25.3 %collective-permute-start.7 = (bf16[2,256,256]{2,1,0:T(8,128)(2,1)S(1)}, bf16[2,256,256]{2,1,0:T(8,128)(2,1)S(1)}, u32[]{:S(2)}, u32[]{:S(2)}) collective-permute-start(bf16[2,256,256]{2,1,0:T(8,128)(2,1)S(1)} %shard_map.111.own), channel_id=1, source_target_pairs={{0,32},{1,33},{2,34},{3,35},{4,36},{5,37},{6,38},{7,39},{8,40},{9,... | collective-permute-start | bytes 786440 | tf_op jit(solution)/shard_map/ppermute | solution.py:292
  18.0 23.3 %collective-permute-start.6 = (bf16[2,256,256]{2,1,0:T(8,128)(2,1)S(1)}, bf16[2,256,256]{2,1,0:T(8,128)(2,1)S(1)}, u32[]{:S(2)}, u32[]{:S(2)}) collective-permute-start(bf16[2,256,256]{2,1,0:T(8,128)(2,1)S(1)} %shard_map.111.own), channel_id=1, source_target_pairs={{0,64},{1,65},{2,66},{3,67},{4,68},{5,69},{6,70},{7,71},{8,72},{9,... | collective-permute-start | bytes 786440 | tf_op jit(solution)/shard_map/ppermute | solution.py:292
  26.1 15.3 %collective-permute-start.5 = (bf16[2,256,256]{2,1,0:T(8,128)(2,1)S(1)}, bf16[2,256,256]{2,1,0:T(8,128)(2,1)S(1)}, u32[]{:S(2)}, u32[]{:S(2)}) collective-permute-start(bf16[2,256,256]{2,1,0:T(8,128)(2,1)S(1)} %shard_map.111.own), channel_id=1, source_target_pairs={{0,128},{1,129},{2,130},{3,131},{4,132},{5,133},{6,134},{7,135},{8... | collective-permute-start | bytes 786440 | tf_op jit(solution)/shard_map/ppermute | solution.py:292
  29.5 14.4 %collective-permute-start.4 = (bf16[2,256,256]{2,1,0:T(8,128)(2,1)S(1)}, bf16[2,256,256]{2,1,0:T(8,128)(2,1)S(1)}, u32[]{:S(2)}, u32[]{:S(2)}) collective-permute-start(bf16[2,256,256]{2,1,0:T(8,128)(2,1)S(1)} %shard_map.111.own), channel_id=1, source_target_pairs={{0,256},{1,257},{2,258},{3,259},{4,260},{5,261},{6,262},{7,263},{8... | collective-permute-start | bytes 786440 | tf_op jit(solution)/shard_map/ppermute | solution.py:292
  34.2 0.7 copy-start.4
  34.2 0.7 copy-start.3
  34.2 0.7 copy-start.6
  49.2 19.3 %collective-permute-start.10 = (bf16[2,256,256]{2,1,0:T(8,128)(2,1)S(1)}, bf16[2,256,256]{2,1,0:T(8,128)(2,1)S(1)}, u32[]{:S(2)}, u32[]{:S(2)}) collective-permute-start(bf16[2,256,256]{2,1,0:T(8,128)(2,1)S(1)} %get-tuple-element.40), channel_id=1, source_target_pairs={{0,256},{1,257},{2,258},{3,259},{4,260},{5,261},{6,262},{7,263},{8... | collective-permute-start | bytes 786440 | tf_op jit(solution)/shard_map/ppermute | solution.py:292
  52.7 16.5 %collective-permute-start.11 = (bf16[2,256,256]{2,1,0:T(8,128)(2,1)S(1)}, bf16[2,256,256]{2,1,0:T(8,128)(2,1)S(1)}, u32[]{:S(2)}, u32[]{:S(2)}) collective-permute-start(bf16[2,256,256]{2,1,0:T(8,128)(2,1)S(1)} %get-tuple-element.41), channel_id=1, source_target_pairs={{0,128},{1,129},{2,130},{3,131},{4,132},{5,133},{6,134},{7,135},{8... | collective-permute-start | bytes 786440 | tf_op jit(solution)/shard_map/ppermute | solution.py:292
  55.2 15.9 %collective-permute-start.8 = (bf16[2,256,256]{2,1,0:T(8,128)(2,1)S(1)}, bf16[2,256,256]{2,1,0:T(8,128)(2,1)S(1)}, u32[]{:S(2)}, u32[]{:S(2)}) collective-permute-start(bf16[2,256,256]{2,1,0:T(8,128)(2,1)S(1)} %get-tuple-element.38), channel_id=1, source_target_pairs={{0,64},{1,65},{2,66},{3,67},{4,68},{5,69},{6,70},{7,71},{8,72},{9,... | collective-permute-start | bytes 786440 | tf_op jit(solution)/shard_map/ppermute | solution.py:292
  61.9 22.5 %collective-permute-start.9 = (bf16[2,256,256]{2,1,0:T(8,128)(2,1)S(1)}, bf16[2,256,256]{2,1,0:T(8,128)(2,1)S(1)}, u32[]{:S(2)}, u32[]{:S(2)}) collective-permute-start(bf16[2,256,256]{2,1,0:T(8,128)(2,1)S(1)} %get-tuple-element.39), channel_id=1, source_target_pairs={{0,32},{1,33},{2,34},{3,35},{4,36},{5,37},{6,38},{7,39},{8,40},{9,... | collective-permute-start | bytes 786440 | tf_op jit(solution)/shard_map/ppermute | solution.py:292
  67.2 24.3 %collective-permute-start.13 = (bf16[2,256,256]{2,1,0:T(8,128)(2,1)S(1)}, bf16[2,256,256]{2,1,0:T(8,128)(2,1)S(1)}, u32[]{:S(2)}, u32[]{:S(2)}) collective-permute-start(bf16[2,256,256]{2,1,0:T(8,128)(2,1)S(1)} %get-tuple-element.42), channel_id=1, source_target_pairs={{15,16},{31,32},{47,48},{63,64},{79,80},{95,96},{111,112},{127,128... | collective-permute-start | bytes 786440 | tf_op jit(solution)/shard_map/ppermute | solution.py:292
  68.5 23.0 %collective-permute-start.12 = (bf16[2,256,256]{2,1,0:T(8,128)(2,1)S(1)}, bf16[2,256,256]{2,1,0:T(8,128)(2,1)S(1)}, u32[]{:S(2)}, u32[]{:S(2)}) collective-permute-start(bf16[2,256,256]{2,1,0:T(8,128)(2,1)S(1)} %get-tuple-element.42), channel_id=1, source_target_pairs={{1,2},{2,1},{3,4},{4,3},{5,6},{6,5},{7,8},{8,7},{9,10},{10,9},{11,... | collective-permute-start | bytes 786440 | tf_op jit(solution)/shard_map/ppermute | solution.py:292
  69.2 22.5 %collective-permute-start.14 = (bf16[2,256,256]{2,1,0:T(8,128)(2,1)S(1)}, bf16[2,256,256]{2,1,0:T(8,128)(2,1)S(1)}, u32[]{:S(2)}, u32[]{:S(2)}) collective-permute-start(bf16[2,256,256]{2,1,0:T(8,128)(2,1)S(1)} %get-tuple-element.43), channel_id=1, source_target_pairs={{0,1},{1,0},{2,3},{3,2},{4,5},{5,4},{6,7},{7,6},{8,9},{9,8},{10,11... | collective-permute-start | bytes 786440 | tf_op jit(solution)/shard_map/ppermute | solution.py:292
  71.2 20.6 %collective-permute-start.15 = (bf16[2,256,256]{2,1,0:T(8,128)(2,1)S(1)}, bf16[2,256,256]{2,1,0:T(8,128)(2,1)S(1)}, u32[]{:S(2)}, u32[]{:S(2)}) collective-permute-start(bf16[2,256,256]{2,1,0:T(8,128)(2,1)S(1)} %get-tuple-element.42), channel_id=1, source_target_pairs={{16,15},{32,31},{48,47},{64,63},{80,79},{96,95},{112,111},{128,127... | collective-permute-start | bytes 786440 | tf_op jit(solution)/shard_map/ppermute | solution.py:292
  91.5 0.9 copy-start.2
  91.5 0.9 copy-start.5
